TPU v7x, 256 devices: a whole 4x4x8 slice. The times are simulated.
256 devices in a mesh: ctx: 32 (over x, z_hi, core), tp: 8 (over z_lo, y).
Axes of the slice: x: 4, y: 4, z: 8 (z_hi: 4, z_lo: 2; z = z_hi * 2 + z_lo), core: 2. Of those that a mesh axis runs over, the one named last changes fastest.
Arguments:
- tokens: bfloat16 [32768, 5120], P(('ctx', 'tp')), may hold values from -6 to 6
- queries: bfloat16 [32768, 3072], P('ctx', 'tp'), may hold values from -500 to 500
- w_key: bfloat16 [5120, 3072], P('ctx', 'tp'), may hold values from -0.078125 to 0.078125
- w_value: bfloat16 [5120, 3072], P('ctx', 'tp'), may hold values from -0.078125 to 0.078125
- tile_slot: int32 [128], replicated, may hold values from 0 to 127, as said below
- neighbour_tile: int32 [128, 6], replicated, may hold values from 0 to 127, as said below
- slab_start: int32 [128, 6], replicated, may hold values from 0 to 192
- slab_length: int32 [128, 6], replicated, may hold values from 0 to 64, as said below
- window_low: int32 [128, 6], replicated, may hold values from 0 to 127, as said below
- window_high: int32 [128, 6], replicated, may hold values from 129 to 256
Outputs:
- attended: bfloat16 [32768, 3072], P('ctx', 'tp')
Inputs may be any that keep to these rules, and one draw needn't show every extreme that they name: `tile_slot`: the slots form a permutation, and tile t has a slot in the block of 4 slots starting at (t // 4) * 4. `neighbour_tile`: call b = t // 4 the block of tile t; blocks b and b + 1 modulo 128 // 4 are adjacent. The first clip is the tiles of blocks 128 // 16 to 23, the second clip the other tiles. Each entry names a tile of the same clip whose block is the own one or adjacent to it; at most 2 entries of a tile name tiles of the previous block, and at most 2 of the next; entries naming the own block name other tiles than the own one. `slab_length`: zero leaves the entry unused. window_low is below window_high of the same entry.
All inputs are finite; a program needn't handle non-finite values.
Results may differ from a plain program's by a relative error of at most 0.0065.
The roundings to bfloat16 on the way count: a program that leaves them out, or rounds other values in their place, can miss the bound.
Values may be sent and summed in bfloat16 or wider, within the bound.
No kernel may reach another device: no remote copies, remote signals or barrier semaphores. Data moves between devices by JAX's collectives and lax.ppermute only.
A program may use at most 64 MiB of HBM per device.

v0:
```python
import math

import jax
import jax.numpy as jnp
from jax import lax
from jax.experimental import pallas as pl
from jax.experimental.pallas import tpu as pltpu
from jax.sharding import PartitionSpec as P


HD = 128
TILE = 256
NB = 6
SLAB = 64
TPD = 4
HALO = TPD * 2 * SLAB
WIN = 80
NX, NZH, NC, NZL, NY = 4, 4, 2, 2, 4
AXES = ("ctx", "tp")
BF16 = jnp.bfloat16
F32 = jnp.float32


def _index(x, zh, c, zl, y):
    return (((x % NX) * NZH + zh % NZH) * NC + c % NC) * (NZL * NY) + zl % NZL * NY + y % NY


def _moves(dx=0, dzh=0, dc=0, dzl=0, dy=0, sx=0, sz=0):
    pairs = []
    for x in range(NX):
        for zh in range(NZH):
            for c in range(NC):
                for zl in range(NZL):
                    for y in range(NY):
                        pairs.append(
                            (
                                _index(x, zh, c, zl, y),
                                _index(
                                    x + dx + sx * (1 - 2 * c),
                                    zh + dzh + sz * (1 - 2 * c),
                                    c + dc,
                                    zl + dzl,
                                    y + dy,
                                ),
                            )
                        )
    return pairs


def _far_moves():
    blocks = NX * NZH * NC
    tps = NZL * NY
    return [
        (b * tps + t, (b - 1 + 2 * (b % 2)) % blocks * tps + t)
        for b in range(blocks)
        for t in range(tps)
    ]


def send(a, **step):
    return lax.ppermute(a, AXES, _moves(**step))


PAIR = ((0, False, 0), (0, False, 1))
NEAR = ((1, True, 0), (1, True, 1), (2, False, 0))
BOTH = NEAR + ((-1, True, 1), (-1, True, 0), (2, False, 1))


ANY = pl.BlockSpec(memory_space=pl.ANY)
SM = pl.BlockSpec(memory_space=pltpu.SMEM)
VM = pl.BlockSpec(memory_space=pltpu.VMEM)
MIB = 1024 * 1024


def join(*parts):
    rows = [p.shape[0] for p in parts]

    def body(*refs):
        out, sems = refs[-2:]
        copies = []
        for i, ref in enumerate(refs[:-2]):
            copies.append(
                pltpu.make_async_copy(ref, out.at[pl.ds(sum(rows[:i]), rows[i]), :], sems.at[i])
            )
        for cp in copies:
            cp.start()
        for cp in copies:
            cp.wait()

    return pl.pallas_call(
        body,
        out_shape=jax.ShapeDtypeStruct((sum(rows), parts[0].shape[1]), parts[0].dtype),
        in_specs=[ANY] * len(parts),
        out_specs=ANY,
        scratch_shapes=[pltpu.SemaphoreType.DMA((len(parts),))],
        compiler_params=pltpu.CompilerParams(vmem_limit_bytes=MIB),
    )(*parts)


def project(pos, toks, tok_at, rows, pieces, fs):
    nt, np_ = len(toks), len(pieces)
    features = fs * NX * NZH * NC
    quarter = features // NX

    def body(*refs):
        pos_ref = refs[0]
        tok_refs = refs[1 : 1 + nt]
        piece_refs = refs[1 + nt : 1 + nt + np_]
        out, w_out, t_buf, w_buf, acc, t_sem, w_sem, o_sem = refs[1 + nt + np_ :]
        x, zh, c = pos_ref[0], pos_ref[1], pos_ref[2]
        waits = []
        for ref, (_, xrel, signed, flip, plan) in zip(piece_refs, pieces):
            core = (c + flip) % NC
            sign = 2 * core - 1
            xs = (x + (sign * xrel if signed else xrel) + NX) % NX
            for i, (zrel, zsigned, other) in enumerate(plan):
                zs = (zh + (sign * zrel if zsigned else zrel) + NZH) % NZH
                place = pl.multiple_of(((xs * NZH + zs) * NC + (core + other) % NC) * fs, 32)
                for kv in range(2):
                    cp = pltpu.make_async_copy(
                        ref.at[pl.ds((2 * i + kv) * fs, fs), :],
                        w_buf.at[pl.ds(place, fs), pl.ds(kv * 384, 384)],
                        w_sem.at[len(waits)],
                    )
                    cp.start()
                    waits.append(cp)
        for i, (ref, (r0, c0)) in enumerate(zip(tok_refs, tok_at)):
            cp = pltpu.make_async_copy(
                ref,
                t_buf.at[pl.ds(r0, ref.shape[0]), pl.ds(c0, ref.shape[1])],
                t_sem.at[i],
            )
            cp.start()
            waits.append(cp)
        for cp in waits:
            cp.wait()
        back = pltpu.make_async_copy(w_buf, w_out, o_sem)
        back.start()
        for q in range(NX):
            part = jnp.dot(
                t_buf[:, q * quarter : (q + 1) * quarter],
                w_buf[q * quarter : (q + 1) * quarter, :],
                preferred_element_type=F32,
            )
            if q == 0:
                acc[...] = part
            elif q < NX - 1:
                acc[...] += part
            else:
                out[...] = (acc[...] + part).astype(BF16)
        back.wait()

    n_copies = 2 * sum(len(p[4]) for p in pieces)
    return pl.pallas_call(
        body,
        out_shape=[
            jax.ShapeDtypeStruct((rows, 768), BF16),
            jax.ShapeDtypeStruct((features, 768), BF16),
        ],
        in_specs=[SM] + [ANY] * (nt + np_),
        out_specs=[VM, ANY],
        scratch_shapes=[
            pltpu.VMEM((rows, features), BF16),
            pltpu.VMEM((features, 768), BF16),
            pltpu.VMEM((rows, 768), F32),
            pltpu.SemaphoreType.DMA((nt,)),
            pltpu.SemaphoreType.DMA((n_copies,)),
            pltpu.SemaphoreType.DMA,
        ],
        compiler_params=pltpu.CompilerParams(vmem_limit_bytes=30 * MIB),
    )(pos, *toks, *[p[0] for p in pieces])


def _half_product(toks, w, row0, t_buf, w_buf, t_sem, w_sem):
    n = toks[0].shape[0]
    half = toks[0].shape[1]
    step = half // 2
    waits = []
    for i, ref in enumerate(toks):
        waits.append(pltpu.make_async_copy(ref, t_buf.at[pl.ds(i * n, n), :], t_sem.at[i]))
    loads = [
        pltpu.make_async_copy(
            w.at[pl.ds(row0 + i * step, step), :], w_buf.at[pl.ds(i * step, step), :], w_sem.at[i]
        )
        for i in range(2)
    ]
    for cp in loads[:1] + waits + loads[1:]:
        cp.start()

    def product(acc):
        for cp in waits:
            cp.wait()
        for i in range(2):
            loads[i].wait()
            acc[...] += jnp.dot(
                t_buf[:, i * step : (i + 1) * step],
                w_buf[i * step : (i + 1) * step, :],
                preferred_element_type=F32,
            )

    return product


def _half_scratch(rows, half):
    return [
        pltpu.VMEM((rows, half), BF16),
        pltpu.VMEM((half, 768), BF16),
        pltpu.SemaphoreType.DMA((3,)),
        pltpu.SemaphoreType.DMA((2,)),
    ]


def project_half(toks, w):
    rows = sum(t.shape[0] for t in toks)
    half = toks[0].shape[1]

    def body(t0, t1, t2, w_ref, acc, t_buf, w_buf, t_sem, w_sem):
        product = _half_product((t0, t1, t2), w_ref, 0, t_buf, w_buf, t_sem, w_sem)
        acc[...] = jnp.zeros_like(acc)
        product(acc)

    return pl.pallas_call(
        body,
        out_shape=jax.ShapeDtypeStruct((rows, 768), F32),
        in_specs=[ANY] * 4,
        out_specs=VM,
        scratch_shapes=_half_scratch(rows, half),
        compiler_params=pltpu.CompilerParams(vmem_limit_bytes=16 * MIB),
    )(*toks, w)


def _tile_at(slot_ref, block, p):
    tile = block * TPD
    for i in range(1, TPD):
        tile = jnp.where(slot_ref[0, block * TPD + i] == block * TPD + p, block * TPD + i, tile)
    return tile


def _aligned(start):
    return jnp.minimum(start // 16 * 16, TILE - WIN)


def project_last(pos, toks, w, acc_in, done, done_places, places, tables):
    rows = sum(t.shape[0] for t in toks)
    half = toks[0].shape[1]
    n = toks[0].shape[0]

    def body(pos_ref, t0, t1, t2, w_ref, acc_ref, done_ref, slot, neighbour, first,
             full, to_near, to_far, t_buf, w_buf, t_sem, w_sem, acc, wide):
        block, zl, y, blocks = pos_ref[3], pos_ref[4], pos_ref[5], pos_ref[6]
        product = _half_product((t0, t1, t2), w_ref, half, t_buf, w_buf, t_sem, w_sem)

        def row_of(place):
            dzl, dy = place
            return pl.multiple_of(((zl + dzl) % NZL * NY + (y + dy + NY) % NY) * n, n)

        for i, place in enumerate(done_places):
            part = done_ref[i * n : (i + 1) * n, :]
            full[pl.ds(row_of(place), n), :] = part
            wide[pl.ds(row_of(place), n), :] = part.astype(F32)
        acc[...] = acc_ref[...]
        product(acc)
        for i, place in enumerate(places):
            part = acc[i * n : (i + 1) * n, :].astype(BF16)
            full[pl.ds(row_of(place), n), :] = part
            wide[pl.ds(row_of(place), n), :] = part.astype(F32)
        up = 1 - 2 * pos_ref[2]
        for out, step in ((to_near, up), (to_far, -up)):
            target = (block + step + blocks) % blocks

            def pick(p, carry, out=out, target=target):
                tile = _tile_at(slot, target, p)
                seen = jnp.int32(0)
                starts = [jnp.int32(0), jnp.int32(0)]
                for j in range(NB):
                    other = neighbour[j, tile]
                    hit = other // TPD == block
                    row = slot[0, other] % TPD * TILE + first[j, tile]
                    for o in range(2):
                        take = jnp.logical_and(hit, seen == o)
                        starts[o] = jnp.where(take, row, starts[o])
                    seen = seen + hit.astype(jnp.int32)
                for o in range(2):
                    al = pl.multiple_of(starts[o] // 8 * 8, 8)
                    rem = starts[o] - al
                    window = pltpu.roll(
                        wide[pl.ds(al, SLAB + 8), :], (SLAB + 8 - rem) % (SLAB + 8), 0
                    )
                    at = pl.multiple_of((p * 2 + o) * SLAB, SLAB)
                    out[pl.ds(at, SLAB), :] = window[:SLAB].astype(BF16)
                return carry

            lax.fori_loop(0, TPD, pick, 0)

    return pl.pallas_call(
        body,
        out_shape=[
            jax.ShapeDtypeStruct((TPD * TILE, 768), BF16),
            jax.ShapeDtypeStruct((HALO, 768), BF16),
            jax.ShapeDtypeStruct((HALO, 768), BF16),
        ],
        in_specs=[SM] + [ANY] * 4 + [VM, VM] + [SM] * 3,
        out_specs=[VM, VM, VM],
        scratch_shapes=_half_scratch(rows, half)
        + [pltpu.VMEM((rows, 768), F32), pltpu.VMEM((TPD * TILE + 8, 768), F32)],
        compiler_params=pltpu.CompilerParams(vmem_limit_bytes=24 * MIB),
    )(pos, *toks, w, acc_in, done, *tables)


CAND = 768


def attend(pos, queries, full, from_near, from_far, tables):
    scale = 1.0 / math.sqrt(HD)

    def body(pos_ref, q_ref, full_ref, near_ref, far_ref, slot, neighbour, first, length,
             low, high, out, cand):
        p = pl.program_id(0)
        block, blocks = pos_ref[3], pos_ref[6]

        @pl.when(p == 0)
        def _():
            cand[pl.ds(TILE + NB * WIN, CAND - TILE - NB * WIN), :] = jnp.zeros(
                (CAND - TILE - NB * WIN, 768), BF16
            )
            for j in range(NB):
                cand[pl.ds(TILE + j * WIN + SLAB, WIN - SLAB), :] = jnp.zeros(
                    (WIN - SLAB, 768), BF16
                )

        tile = _tile_at(slot, block, p)
        own = pl.multiple_of(p * TILE, TILE)
        cand[pl.ds(0, TILE), :] = full_ref[pl.ds(own, TILE), :]
        col = lax.broadcasted_iota(jnp.int32, (8, CAND), 1)
        lows = jnp.where(col < TILE, 0, TILE)
        highs = jnp.where(col < TILE, TILE, 0)
        up = 1 - 2 * pos_ref[2]
        near_block = (block + up + blocks) % blocks
        far_block = (block - up + blocks) % blocks
        seen_near = jnp.int32(0)
        seen_far = jnp.int32(0)
        for j in range(NB):
            other = neighbour[j, tile]
            at = other // TPD
            is_near = at == near_block
            is_far = at == far_block
            s = first[j, tile]
            al = _aligned(s)
            c0 = TILE + j * WIN
            begin = slot[0, other] % TPD * TILE + al

            @pl.when(is_near)
            def _(c0=c0, seen_near=seen_near):
                at = pl.multiple_of((p * 2 + seen_near) * SLAB, SLAB)
                cand[pl.ds(c0, SLAB), :] = near_ref[pl.ds(at, SLAB), :]

            @pl.when(is_far)
            def _(c0=c0, seen_far=seen_far):
                at = pl.multiple_of((p * 2 + seen_far) * SLAB, SLAB)
                cand[pl.ds(c0, SLAB), :] = far_ref[pl.ds(at, SLAB), :]

            away = jnp.logical_or(is_near, is_far)

            @pl.when(jnp.logical_not(away))
            def _(c0=c0, begin=begin):
                cand[pl.ds(c0, WIN), :] = full_ref[pl.ds(pl.multiple_of(begin, 16), WIN), :]

            rem = jnp.where(away, 0, s - al)
            seen_near = seen_near + is_near.astype(jnp.int32)
            seen_far = seen_far + is_far.astype(jnp.int32)
            valid = jnp.logical_and(col >= c0 + rem, col < c0 + rem + length[j, tile])
            lows = jnp.where(valid, low[j, tile], lows)
            highs = jnp.where(valid, high[j, tile], highs)
        row = lax.broadcasted_iota(jnp.int32, (TILE, CAND), 0)
        allowed = jnp.logical_and(row >= lows[0:1, :], row < highs[0:1, :])
        for h in range(3):
            q = q_ref[:, h * HD : (h + 1) * HD]
            k = cand[:, h * HD : (h + 1) * HD]
            v = cand[:, 384 + h * HD : 384 + (h + 1) * HD]
            scores = lax.dot_general(
                q, k, (((1,), (1,)), ((), ())), preferred_element_type=F32
            ) * scale
            scores = jnp.where(allowed, scores, -jnp.inf)
            top = jnp.max(scores, axis=-1, keepdims=True)
            weights = jnp.exp(scores - top)
            total = jnp.sum(weights, axis=-1, keepdims=True)
            mixed = jnp.dot(weights.astype(BF16), v, preferred_element_type=F32)
            out[:, h * HD : (h + 1) * HD] = (mixed / total).astype(BF16)

    return pl.pallas_call(
        body,
        grid=(TPD,),
        out_shape=jax.ShapeDtypeStruct(queries.shape, BF16),
        in_specs=[SM, pl.BlockSpec((TILE, 384), lambda p: (p, 0)), VM, VM, VM] + [SM] * 6,
        out_specs=pl.BlockSpec((TILE, 384), lambda p: (p, 0)),
        scratch_shapes=[pltpu.VMEM((CAND, 768), BF16)],
        compiler_params=pltpu.CompilerParams(vmem_limit_bytes=24 * MIB),
    )(pos, queries, full, from_near, from_far, *tables)


def per_device(
    tokens,
    queries,
    w_key,
    w_value,
    tile_slot,
    neighbour_tile,
    slab_start,
    slab_length,
    window_low,
    window_high,
):
    fs = w_key.shape[0]
    ctx = lax.axis_index("ctx")
    tp = lax.axis_index("tp")
    pos = jnp.stack(
        [ctx >> 3, (ctx >> 1) & 3, ctx & 1, ctx, tp >> 2, tp & 3, jnp.int32(lax.axis_size("ctx"))]
    ).astype(jnp.int32)
    tables = (
        tile_slot.reshape(1, -1),
        neighbour_tile.T,
        slab_start.T,
        slab_length.T,
        window_low.T,
        window_high.T,
    )

    h = tokens.shape[1] // 2
    w = join(w_key, w_value)
    pair = join(w, send(w, dc=1))
    ya = send(tokens, dy=1)
    z1 = send(pair, sz=1)
    yb = send(tokens, dy=-1)
    xa1 = send(pair, sx=1)
    tl, tr = tokens[:, :h], tokens[:, h:]
    xa2 = send(xa1[: 2 * fs], sx=1)
    z2 = send(z1[: 2 * fs], sz=1)
    z_l = send(tl, dzl=1)
    z_r = send(tr, dzl=1)
    near = join(z1, z2)
    both = join(near, send(near, dc=1))
    xb1 = send(both, sx=1)
    yo_l = send(ya[:, :h], dy=1)
    yo_r = send(yb[:, h:], dy=-1)
    ua_l = send(z_l, dy=1)
    ub_l = send(z_l, dy=-1)
    xb2 = send(xb1[: 6 * fs], sx=1)
    uo_l = send(yo_l, dzl=1)
    uo_r = send(yo_r, dzl=1)
    ua_r = send(z_r, dy=1)
    ub_r = send(z_r, dy=-1)
    pieces = [(pair, 0, False, 0, PAIR), (both, 0, False, 0, BOTH)]
    for p, xrel, signed, plan in (
        (xa1, 1, True, PAIR), (xa2, 2, False, PAIR[:1]), (xb1, 1, True, BOTH), (xb2, 2, False, NEAR)
    ):
        pieces += [(p, xrel, signed, 0, plan), (send(p, dc=1), xrel, signed, 1, plan)]

    n = tokens.shape[0]
    toks = (tokens, ya, yb, yo_l, yo_r, z_l, z_r)
    at = ((0, 0), (n, 0), (2 * n, 0), (3 * n, 0), (3 * n, h), (4 * n, 0), (4 * n, h))
    kv1, w_all = project(pos, toks, at, 5 * n, pieces, fs)
    part = project_half((ua_l, ub_l, uo_l), w_all)
    full, to_near, to_far = project_last(
        pos,
        (ua_r, ub_r, uo_r),
        w_all,
        part,
        kv1,
        ((0, 0), (0, -1), (0, 1), (0, 2), (1, 0)),
        ((1, -1), (1, 1), (1, 2)),
        tables[:3],
    )
    from_far = lax.ppermute(to_far, AXES, _far_moves())
    from_near = lax.ppermute(to_near, AXES, _moves(dc=1))
    return attend(pos, queries, full, from_near, from_far, tables)


def solution(mesh):
    in_specs = (
        P(("ctx", "tp"), None),
        P("ctx", "tp"),
        P("ctx", "tp"),
        P("ctx", "tp"),
        P(),
        P(),
        P(),
        P(),
        P(),
        P(),
    )
    out_specs = P("ctx", "tp")
    return jax.shard_map(
        per_device, mesh=mesh, in_specs=in_specs, out_specs=out_specs, check_vma=False
    )
```

profile of v0, /device:TPU:32, one launch (start us, length us, event | category | flops | bytes accessed | tf_op | source)
XLA Modules:
  0.0 185.7 jit_solution(2790224933762005499)
XLA Ops:
  4.3 3.3 %collective-permute-start.10 = (bf16[640,384]{1,0:T(8,128)(2,1)S(1)}, bf16[640,384]{1,0:T(8,128)(2,1)S(1)}, u32[]{:S(2)}, u32[]{:S(2)}) collective-permute-start(bf16[640,384]{1,0:T(8,128)(2,1)S(1)} %shard_map.101.refs_8_), channel_id=1, source_target_pairs={{0,16},{1,17},{2,18},{3,19},{4,20},{5,21},{6,22},{7,23},{8,56},{9,... | collective-permute-start | bytes 1474568 | tf_op jit(solution)/shard_map/ppermute | solution.py:61
  7.7 14.2 %collective-permute-done.10.refs_0_ = bf16[640,384]{1,0:T(8,128)(2,1)S(1)} collective-permute-done((bf16[640,384]{1,0:T(8,128)(2,1)S(1)}, bf16[640,384]{1,0:T(8,128)(2,1)S(1)}, u32[]{:S(2)}, u32[]{:S(2)}) %collective-permute-start.10) | collective-permute-done | bytes 491552 | tf_op jit(solution)/shard_map/ppermute | solution.py:61
  22.4 9.8 %collective-permute-done.11.refs_1_ = bf16[320,384]{1,0:T(8,128)(2,1)S(1)} collective-permute-done((bf16[320,384]{1,0:T(8,128)(2,1)S(1)}, bf16[320,384]{1,0:T(8,128)(2,1)S(1)}, u32[]{:S(2)}, u32[]{:S(2)}) %collective-permute-start.11) | collective-permute-done | bytes 245792 | tf_op jit(solution)/shard_map/ppermute | solution.py:61
  33.0 2.2 %collective-permute-done.12.refs_1_ = bf16[960,384]{1,0:T(8,128)(2,1)S(1)} collective-permute-done((bf16[960,384]{1,0:T(8,128)(2,1)S(1)}, bf16[960,384]{1,0:T(8,128)(2,1)S(1)}, u32[]{:S(2)}, u32[]{:S(2)}) %collective-permute-start.12) | collective-permute-done | bytes 737312 | tf_op jit(solution)/shard_map/ppermute | solution.py:61
  35.8 1.6 collective-permute-start.17
  37.4 3.0 %collective-permute-start.3 = (bf16[128,5120]{1,0:T(8,128)(2,1)S(1)}, bf16[128,5120]{1,0:T(8,128)(2,1)S(1)}, u32[]{:S(2)}, u32[]{:S(2)}) collective-permute-start(bf16[128,5120]{1,0:T(8,128)(2,1)S(1)} %copy-done), channel_id=1, source_target_pairs={{0,3},{1,0},{2,1},{3,2},{4,7},{5,4},{6,5},{7,6},{8,11},{9,8},{10,9... | collective-permute-start | bytes 3932168 | tf_op jit(solution)/shard_map/ppermute | solution.py:61
  40.6 1.6 collective-permute-start.13
  42.2 19.6 %collective-permute-done.13.refs_10_ = bf16[640,384]{1,0:T(8,128)(2,1)S(1)} collective-permute-done((bf16[640,384]{1,0:T(8,128)(2,1)S(1)}, bf16[640,384]{1,0:T(8,128)(2,1)S(1)}, u32[]{:S(2)}, u32[]{:S(2)}) %collective-permute-start.13) | collective-permute-done | bytes 491552 | tf_op jit(solution)/shard_map/ppermute | solution.py:61
  63.9 5.4 %collective-permute-done.15.refs_12_ = bf16[320,384]{1,0:T(8,128)(2,1)S(1)} collective-permute-done((bf16[320,384]{1,0:T(8,128)(2,1)S(1)}, bf16[320,384]{1,0:T(8,128)(2,1)S(1)}, u32[]{:S(2)}, u32[]{:S(2)}) %collective-permute-start.15) | collective-permute-done | bytes 245792 | tf_op jit(solution)/shard_map/ppermute | solution.py:61
  69.8 3.4 %collective-permute-done.6.refs_2_ = bf16[128,5120]{1,0:T(8,128)(2,1)S(1)} collective-permute-done((bf16[128,5120]{1,0:T(8,128)(2,1)S(1)}, bf16[128,5120]{1,0:T(8,128)(2,1)S(1)}, u32[]{:S(2)}, u32[]{:S(2)}) %collective-permute-start.6) | collective-permute-done | bytes 1310752 | tf_op jit(solution)/shard_map/ppermute | solution.py:61
  73.2 4.0 %collective-permute-done.19.refs_16_ = bf16[960,384]{1,0:T(8,128)(2,1)S(1)} collective-permute-done((bf16[960,384]{1,0:T(8,128)(2,1)S(1)}, bf16[960,384]{1,0:T(8,128)(2,1)S(1)}, u32[]{:S(2)}, u32[]{:S(2)}) %collective-permute-start.19) | collective-permute-done | bytes 737312 | tf_op jit(solution)/shard_map/ppermute | solution.py:61
  78.2 5.4 %collective-permute-done.8.refs_6_ = bf16[128,2560]{1,0:T(8,128)(2,1)} collective-permute-done((bf16[128,2560]{1,0:T(8,128)(2,1)S(1)}, bf16[128,2560]{1,0:T(8,128)(2,1)}, u32[]{:S(2)}, u32[]{:S(2)}) %collective-permute-start.8) | collective-permute-done | bytes 655392 | tf_op jit(solution)/shard_map/ppermute | solution.py:61
  85.5 1.6 collective-permute-start.7
  87.9 1.7 collective-permute-start.4
  89.5 13.0 %collective-permute-done.21.t0 = bf16[128,2560]{1,0:T(8,128)(2,1)S(1)} collective-permute-done((bf16[128,2560]{1,0:T(8,128)(2,1)}, bf16[128,2560]{1,0:T(8,128)(2,1)S(1)}, u32[]{:S(2)}, u32[]{:S(2)}) %collective-permute-start.21) | collective-permute-done | bytes 655392 | tf_op jit(solution)/shard_map/ppermute | solution.py:61
  103.4 1.8 collective-permute-start.22
  105.2 7.2 %collective-permute-done.7.refs_4_ = bf16[128,2560]{1,0:T(8,128)(2,1)} collective-permute-done((bf16[128,2560]{1,0:T(8,128)(2,1)S(1)}, bf16[128,2560]{1,0:T(8,128)(2,1)}, u32[]{:S(2)}, u32[]{:S(2)}) %collective-permute-start.7) | collective-permute-done | bytes 655392 | tf_op jit(solution)/shard_map/ppermute | solution.py:61
  113.9 3.2 %collective-permute-start.2 = (bf16[128,2560]{1,0:T(8,128)(2,1)}, bf16[128,2560]{1,0:T(8,128)(2,1)}, u32[]{:S(2)}, u32[]{:S(2)}) collective-permute-start(bf16[128,2560]{1,0:T(8,128)(2,1)} %collective-permute-done.refs_7_), channel_id=1, source_target_pairs={{0,3},{1,0},{2,1},{3,2},{4,7},{5,4},{6,5},{7,6},{8,11},{9,8},{10,9... | collective-permute-start | bytes 1966088 | tf_op jit(solution)/shard_map/ppermute | solution.py:61
  130.4 10.0 %shard_map.104 = (bf16[640,768]{1,0:T(8,128)(2,1)S(1)}, bf16[5120,768]{1,0:T(8,128)(2,1)S(1)}) custom-call(s32[7]{0:T(128)S(1)} %stack.27.refs_0_.pos_ref, bf16[128,5120]{1,0:T(8,128)(2,1)S(1)} %copy-done, bf16[128,5120]{1,0:T(8,128)(2,1)S(1)} %copy-done.6, bf16[128,5120]{1,0:T(8,128)(2,1)S(1)} %copy-done.4, ...), custom_call_target="tpu_custom_call" | custom-call | tf_op jit(solution)/shard_map/pallas_call | solution.py:154
  140.5 4.1 %shard_map.105.acc_ref = f32[384,768]{1,0:T(8,128)S(1)} custom-call(bf16[128,2560]{1,0:T(8,128)(2,1)S(1)} %copy-done.17, bf16[128,2560]{1,0:T(8,128)(2,1)} %collective-permute-done.22.t1, bf16[128,2560]{1,0:T(8,128)(2,1)} %collective-permute-done.23.t2, bf16[5120,768]{1,0:T(8,128)(2,1)S(1)} %get-tuple-element.10.w_ref), custom_call_target="tpu_custom_call" | custom-call | tf_op jit(solution)/shard_map/pallas_call | solution.py:222
  144.6 6.3 %shard_map.106 = (bf16[1024,768]{1,0:T(8,128)(2,1)S(1)}, bf16[512,768]{1,0:T(8,128)(2,1)S(1)}, bf16[512,768]{1,0:T(8,128)(2,1)S(1)}) custom-call(s32[7]{0:T(128)S(1)} %stack.27.refs_0_.pos_ref, bf16[128,2560]{1,0:T(8,128)(2,1)} %collective-permute-done.1.t0, bf16[128,2560]{1,0:T(8,128)(2,1)} %collective-permute-done.2.t1, ...), custom_call_target="tpu_custom_call" | custom-call | tf_op jit(solution)/shard_map/pallas_call | solution.py:295
  151.1 8.1 %collective-permute-start.25 = (bf16[512,768]{1,0:T(8,128)(2,1)S(1)}, bf16[512,768]{1,0:T(8,128)(2,1)S(1)}, u32[]{:S(2)}, u32[]{:S(2)}) collective-permute-start(bf16[512,768]{1,0:T(8,128)(2,1)S(1)} %get-tuple-element.14), channel_id=1, source_target_pairs={{0,248},{1,249},{2,250},{3,251},{4,252},{5,253},{6,254},{7,255},{8... | collective-permute-start | bytes 2359304 | tf_op jit(solution)/shard_map/ppermute | solution.py:473
  159.2 16.9 %collective-permute-done.25.far_ref = bf16[512,768]{1,0:T(8,128)(2,1)S(1)} collective-permute-done((bf16[512,768]{1,0:T(8,128)(2,1)S(1)}, bf16[512,768]{1,0:T(8,128)(2,1)S(1)}, u32[]{:S(2)}, u32[]{:S(2)}) %collective-permute-start.25) | collective-permute-done | bytes 786464 | tf_op jit(solution)/shard_map/ppermute | solution.py:473
  176.2 9.5 %shard_map.107 = bf16[1024,384]{1,0:T(8,128)(2,1)} custom-call(s32[7]{0:T(128)S(1)} %stack.27.refs_0_.pos_ref, bf16[1024,384]{1,0:T(8,128)(2,1)S(1)} %copy-done.11, bf16[1024,768]{1,0:T(8,128)(2,1)S(1)} %get-tuple-element.12.full_ref, bf16[512,768]{1,0:T(8,128)(2,1)S(1)} %collective-permute-done.24.near_ref, ...), custom_call_target="tpu_custom_call" | custom-call | tf_op jit(solution)/shard_map/pallas_call | solution.py:390
  (103 shorter events, 28.5 us)
Async XLA Ops:
  4.3 17.6 %collective-permute-start.10 = (bf16[640,384]{1,0:T(8,128)(2,1)S(1)}, bf16[640,384]{1,0:T(8,128)(2,1)S(1)}, u32[]{:S(2)}, u32[]{:S(2)}) collective-permute-start(bf16[640,384]{1,0:T(8,128)(2,1)S(1)} %shard_map.101.refs_8_), channel_id=1, source_target_pairs={{0,16},{1,17},{2,18},{3,19},{4,20},{5,21},{6,22},{7,23},{8,56},{9,... | collective-permute-start | bytes 1474568 | tf_op jit(solution)/shard_map/ppermute | solution.py:61
  21.9 10.3 %collective-permute-start.11 = (bf16[320,384]{1,0:T(8,128)(2,1)S(1)}, bf16[320,384]{1,0:T(8,128)(2,1)S(1)}, u32[]{:S(2)}, u32[]{:S(2)}) collective-permute-start(bf16[320,384]{1,0:T(8,128)(2,1)S(1)} %slice.30), channel_id=1, source_target_pairs={{0,16},{1,17},{2,18},{3,19},{4,20},{5,21},{6,22},{7,23},{8,56},{9,... | collective-permute-start | bytes 737288 | tf_op jit(solution)/shard_map/ppermute | solution.py:61
  35.8 26.3 %collective-permute-start.17 = (bf16[1920,384]{1,0:T(8,128)(2,1)S(1)}, bf16[1920,384]{1,0:T(8,128)(2,1)S(1)}, u32[]{:S(2)}, u32[]{:S(2)}) collective-permute-start(bf16[1920,384]{1,0:T(8,128)(2,1)S(1)} %shard_map.103.refs_9_), channel_id=1, source_target_pairs={{0,64},{1,65},{2,66},{3,67},{4,68},{5,69},{6,70},{7,71},{8,200},{9... | collective-permute-start | bytes 4423688 | tf_op jit(solution)/shard_map/ppermute | solution.py:61
  37.4 32.0 %collective-permute-start.3 = (bf16[128,5120]{1,0:T(8,128)(2,1)S(1)}, bf16[128,5120]{1,0:T(8,128)(2,1)S(1)}, u32[]{:S(2)}, u32[]{:S(2)}) collective-permute-start(bf16[128,5120]{1,0:T(8,128)(2,1)S(1)} %copy-done), channel_id=1, source_target_pairs={{0,3},{1,0},{2,1},{3,2},{4,7},{5,4},{6,5},{7,6},{8,11},{9,8},{10,9... | collective-permute-start | bytes 3932168 | tf_op jit(solution)/shard_map/ppermute | solution.py:61
  40.4 32.7 %collective-permute-start.6 = (bf16[128,5120]{1,0:T(8,128)(2,1)S(1)}, bf16[128,5120]{1,0:T(8,128)(2,1)S(1)}, u32[]{:S(2)}, u32[]{:S(2)}) collective-permute-start(bf16[128,5120]{1,0:T(8,128)(2,1)S(1)} %copy-done), channel_id=1, source_target_pairs={{0,1},{1,2},{2,3},{3,0},{4,5},{5,6},{6,7},{7,4},{8,9},{9,10},{10,1... | collective-permute-start | bytes 3932168 | tf_op jit(solution)/shard_map/ppermute | solution.py:61
  40.5 23.3 %collective-permute-start = (bf16[128,2560]{1,0:T(8,128)(2,1)S(1)}, bf16[128,2560]{1,0:T(8,128)(2,1)}, u32[]{:S(2)}, u32[]{:S(2)}) collective-permute-start(bf16[128,2560]{1,0:T(8,128)(2,1)S(1)} %get-tuple-element.16), channel_id=1, source_target_pairs={{0,4},{1,5},{2,6},{3,7},{4,0},{5,1},{6,2},{7,3},{8,12},{9,13},{10,... | collective-permute-start | bytes 1966088 | tf_op jit(solution)/shard_map/ppermute | solution.py:61
  40.6 21.1 %collective-permute-start.13 = (bf16[640,384]{1,0:T(8,128)(2,1)S(1)}, bf16[640,384]{1,0:T(8,128)(2,1)S(1)}, u32[]{:S(2)}, u32[]{:S(2)}) collective-permute-start(bf16[640,384]{1,0:T(8,128)(2,1)S(1)} %shard_map.101.refs_8_), channel_id=1, source_target_pairs={{0,64},{1,65},{2,66},{3,67},{4,68},{5,69},{6,70},{7,71},{8,200},{9... | collective-permute-start | bytes 1474568 | tf_op jit(solution)/shard_map/ppermute | solution.py:61
  61.8 7.5 %collective-permute-start.15 = (bf16[320,384]{1,0:T(8,128)(2,1)S(1)}, bf16[320,384]{1,0:T(8,128)(2,1)S(1)}, u32[]{:S(2)}, u32[]{:S(2)}) collective-permute-start(bf16[320,384]{1,0:T(8,128)(2,1)S(1)} %slice.31), channel_id=1, source_target_pairs={{0,64},{1,65},{2,66},{3,67},{4,68},{5,69},{6,70},{7,71},{8,200},{9... | collective-permute-start | bytes 737288 | tf_op jit(solution)/shard_map/ppermute | solution.py:61
  62.2 14.9 %collective-permute-start.19 = (bf16[960,384]{1,0:T(8,128)(2,1)S(1)}, bf16[960,384]{1,0:T(8,128)(2,1)S(1)}, u32[]{:S(2)}, u32[]{:S(2)}) collective-permute-start(bf16[960,384]{1,0:T(8,128)(2,1)S(1)} %slice.32), channel_id=1, source_target_pairs={{0,64},{1,65},{2,66},{3,67},{4,68},{5,69},{6,70},{7,71},{8,200},{9... | collective-permute-start | bytes 2211848 | tf_op jit(solution)/shard_map/ppermute | solution.py:61
  63.8 53.3 %collective-permute-start.18 = (bf16[1920,384]{1,0:T(8,128)(2,1)S(1)}, bf16[1920,384]{1,0:T(8,128)(2,1)S(1)}, u32[]{:S(2)}, u32[]{:S(2)}) collective-permute-start(bf16[1920,384]{1,0:T(8,128)(2,1)S(1)} %collective-permute-done.17.refs_14_), channel_id=1, source_target_pairs={{0,8},{1,9},{2,10},{3,11},{4,12},{5,13},{6,14},{7,15},{8,0},{9,1},... | collective-permute-start | bytes 4423688 | tf_op jit(solution)/shard_map/ppermute | solution.py:61
  69.3 14.2 %collective-permute-start.8 = (bf16[128,2560]{1,0:T(8,128)(2,1)S(1)}, bf16[128,2560]{1,0:T(8,128)(2,1)}, u32[]{:S(2)}, u32[]{:S(2)}) collective-permute-start(bf16[128,2560]{1,0:T(8,128)(2,1)S(1)} %get-tuple-element.15), channel_id=1, source_target_pairs={{0,4},{1,5},{2,6},{3,7},{4,0},{5,1},{6,2},{7,3},{8,12},{9,13},{10,... | collective-permute-start | bytes 1966088 | tf_op jit(solution)/shard_map/ppermute | solution.py:61
  69.4 17.6 %collective-permute-start.14 = (bf16[640,384]{1,0:T(8,128)(2,1)S(1)}, bf16[640,384]{1,0:T(8,128)(2,1)S(1)}, u32[]{:S(2)}, u32[]{:S(2)}) collective-permute-start(bf16[640,384]{1,0:T(8,128)(2,1)S(1)} %collective-permute-done.13.refs_10_), channel_id=1, source_target_pairs={{0,8},{1,9},{2,10},{3,11},{4,12},{5,13},{6,14},{7,15},{8,0},{9,1},... | collective-permute-start | bytes 1474568 | tf_op jit(solution)/shard_map/ppermute | solution.py:61
  73.2 11.6 %collective-permute-start.16 = (bf16[320,384]{1,0:T(8,128)(2,1)S(1)}, bf16[320,384]{1,0:T(8,128)(2,1)S(1)}, u32[]{:S(2)}, u32[]{:S(2)}) collective-permute-start(bf16[320,384]{1,0:T(8,128)(2,1)S(1)} %collective-permute-done.15.refs_12_), channel_id=1, source_target_pairs={{0,8},{1,9},{2,10},{3,11},{4,12},{5,13},{6,14},{7,15},{8,0},{9,1},... | collective-permute-start | bytes 737288 | tf_op jit(solution)/shard_map/ppermute | solution.py:61
  77.2 35.8 %collective-permute-start.20 = (bf16[960,384]{1,0:T(8,128)(2,1)S(1)}, bf16[960,384]{1,0:T(8,128)(2,1)S(1)}, u32[]{:S(2)}, u32[]{:S(2)}) collective-permute-start(bf16[960,384]{1,0:T(8,128)(2,1)S(1)} %collective-permute-done.19.refs_16_), channel_id=1, source_target_pairs={{0,8},{1,9},{2,10},{3,11},{4,12},{5,13},{6,14},{7,15},{8,0},{9,1},... | collective-permute-start | bytes 2211848 | tf_op jit(solution)/shard_map/ppermute | solution.py:61
  83.5 19.0 %collective-permute-start.21 = (bf16[128,2560]{1,0:T(8,128)(2,1)}, bf16[128,2560]{1,0:T(8,128)(2,1)S(1)}, u32[]{:S(2)}, u32[]{:S(2)}) collective-permute-start(bf16[128,2560]{1,0:T(8,128)(2,1)} %collective-permute-done.8.refs_6_), channel_id=1, source_target_pairs={{0,1},{1,2},{2,3},{3,0},{4,5},{5,6},{6,7},{7,4},{8,9},{9,10},{10,1... | collective-permute-start | bytes 1966088 | tf_op jit(solution)/shard_map/ppermute | solution.py:61
  85.5 26.9 %collective-permute-start.7 = (bf16[128,2560]{1,0:T(8,128)(2,1)S(1)}, bf16[128,2560]{1,0:T(8,128)(2,1)}, u32[]{:S(2)}, u32[]{:S(2)}) collective-permute-start(bf16[128,2560]{1,0:T(8,128)(2,1)S(1)} %slice.29), channel_id=1, source_target_pairs={{0,1},{1,2},{2,3},{3,0},{4,5},{5,6},{6,7},{7,4},{8,9},{9,10},{10,1... | collective-permute-start | bytes 1966088 | tf_op jit(solution)/shard_map/ppermute | solution.py:61
  87.9 25.1 %collective-permute-start.4 = (bf16[128,2560]{1,0:T(8,128)(2,1)S(1)}, bf16[128,2560]{1,0:T(8,128)(2,1)}, u32[]{:S(2)}, u32[]{:S(2)}) collective-permute-start(bf16[128,2560]{1,0:T(8,128)(2,1)S(1)} %slice.28), channel_id=1, source_target_pairs={{0,3},{1,0},{2,1},{3,2},{4,7},{5,4},{6,5},{7,6},{8,11},{9,8},{10,9... | collective-permute-start | bytes 1966088 | tf_op jit(solution)/shard_map/ppermute | solution.py:61
  103.4 37.0 %collective-permute-start.22 = (bf16[128,2560]{1,0:T(8,128)(2,1)}, bf16[128,2560]{1,0:T(8,128)(2,1)}, u32[]{:S(2)}, u32[]{:S(2)}) collective-permute-start(bf16[128,2560]{1,0:T(8,128)(2,1)} %collective-permute-done.8.refs_6_), channel_id=1, source_target_pairs={{0,3},{1,0},{2,1},{3,2},{4,7},{5,4},{6,5},{7,6},{8,11},{9,8},{10,9... | collective-permute-start | bytes 1966088 | tf_op jit(solution)/shard_map/ppermute | solution.py:61
  112.4 28.0 %collective-permute-start.23 = (bf16[128,2560]{1,0:T(8,128)(2,1)}, bf16[128,2560]{1,0:T(8,128)(2,1)}, u32[]{:S(2)}, u32[]{:S(2)}) collective-permute-start(bf16[128,2560]{1,0:T(8,128)(2,1)} %collective-permute-done.7.refs_4_), channel_id=1, source_target_pairs={{0,4},{1,5},{2,6},{3,7},{4,0},{5,1},{6,2},{7,3},{8,12},{9,13},{10,... | collective-permute-start | bytes 1966088 | tf_op jit(solution)/shard_map/ppermute | solution.py:61
  113.0 31.6 %collective-permute-start.1 = (bf16[128,2560]{1,0:T(8,128)(2,1)}, bf16[128,2560]{1,0:T(8,128)(2,1)}, u32[]{:S(2)}, u32[]{:S(2)}) collective-permute-start(bf16[128,2560]{1,0:T(8,128)(2,1)} %collective-permute-done.refs_7_), channel_id=1, source_target_pairs={{0,1},{1,2},{2,3},{3,0},{4,5},{5,6},{6,7},{7,4},{8,9},{9,10},{10,1... | collective-permute-start | bytes 1966088 | tf_op jit(solution)/shard_map/ppermute | solution.py:61
  113.9 30.7 %collective-permute-start.2 = (bf16[128,2560]{1,0:T(8,128)(2,1)}, bf16[128,2560]{1,0:T(8,128)(2,1)}, u32[]{:S(2)}, u32[]{:S(2)}) collective-permute-start(bf16[128,2560]{1,0:T(8,128)(2,1)} %collective-permute-done.refs_7_), channel_id=1, source_target_pairs={{0,3},{1,0},{2,1},{3,2},{4,7},{5,4},{6,5},{7,6},{8,11},{9,8},{10,9... | collective-permute-start | bytes 1966088 | tf_op jit(solution)/shard_map/ppermute | solution.py:61
  118.3 26.3 %collective-permute-start.5 = (bf16[128,2560]{1,0:T(8,128)(2,1)}, bf16[128,2560]{1,0:T(8,128)(2,1)}, u32[]{:S(2)}, u32[]{:S(2)}) collective-permute-start(bf16[128,2560]{1,0:T(8,128)(2,1)} %collective-permute-done.4.refs_5_), channel_id=1, source_target_pairs={{0,4},{1,5},{2,6},{3,7},{4,0},{5,1},{6,2},{7,3},{8,12},{9,13},{10,... | collective-permute-start | bytes 1966088 | tf_op jit(solution)/shard_map/ppermute | solution.py:61
  151.0 8.2 %collective-permute-start.24 = (bf16[512,768]{1,0:T(8,128)(2,1)S(1)}, bf16[512,768]{1,0:T(8,128)(2,1)S(1)}, u32[]{:S(2)}, u32[]{:S(2)}) collective-permute-start(bf16[512,768]{1,0:T(8,128)(2,1)S(1)} %get-tuple-element.13), channel_id=1, source_target_pairs={{0,8},{1,9},{2,10},{3,11},{4,12},{5,13},{6,14},{7,15},{8,0},{9,1},... | collective-permute-start | bytes 2359304 | tf_op jit(solution)/shard_map/ppermute | solution.py:474
  151.1 25.1 %collective-permute-start.25 = (bf16[512,768]{1,0:T(8,128)(2,1)S(1)}, bf16[512,768]{1,0:T(8,128)(2,1)S(1)}, u32[]{:S(2)}, u32[]{:S(2)}) collective-permute-start(bf16[512,768]{1,0:T(8,128)(2,1)S(1)} %get-tuple-element.14), channel_id=1, source_target_pairs={{0,248},{1,249},{2,250},{3,251},{4,252},{5,253},{6,254},{7,255},{8... | collective-permute-start | bytes 2359304 | tf_op jit(solution)/shard_map/ppermute | solution.py:473
  (32 other events, 301.2 us)
where the time goes:
time: 188 us; the launch traced here: 186 us
  waiting for transfers between devices  103 us (55%)
  starting transfers between devices  32.5 us (17%)
  Pallas kernels  32.1 us (17%)
  local copies, waits for them, and re-layouts  18.1 us (10%)
    ppermute x24, waiting for transfers between devices, send(): return lax.ppermute(a, AXES, _moves(**step))  85.8 us
    ppermute x24, starting transfers between devices, send(): return lax.ppermute(a, AXES, _moves(**step))  24.2 us
    unnamed x60, local copies, waits for them, and re-layouts  17.7 us
    ppermute x1, waiting for transfers between devices, per_device(): from_far = lax.ppermute(to_far, AXES, _far_moves())  16.9 us
    pallas_call x1, Pallas kernels, project(): pl.pallas_call(body, out_shape=[jax.ShapeDtypeStruct((rows, 768), BF16),...  9.96 us
    pallas_call x1, Pallas kernels, attend(): pl.pallas_call(body, grid=(TPD,), out_shape=jax.ShapeDtypeStruct(queries....  9.54 us
    ppermute x1, starting transfers between devices, per_device(): from_far = lax.ppermute(to_far, AXES, _far_moves())  8.13 us
    pallas_call x1, Pallas kernels, project_last(): pl.pallas_call(body, out_shape=[jax.ShapeDtypeStruct((TPD * TILE, 768), B...  6.32 us
  transfers between devices with their start and end apart: 26, of which 13 were waited for; matrix products, arithmetic and copies ran while one was open for 0% of the time, Pallas kernels for 8%

commit v1 on v0

--- a/solution.py
+++ b/solution.py
@@ -58,21 +58,23 @@
 
 
 def send(a, **step):
-    return lax.ppermute(a, AXES, _moves(**step))
-
-
-PAIR = ((0, False, 0), (0, False, 1))
+    return lax.ppermute(a, AXES, _far_moves() if "far" in step else _moves(**step))
+
+
+SAME = ((0, False, 0),)
+OTHER = ((0, False, 1),)
 NEAR = ((1, True, 0), (1, True, 1), (2, False, 0))
-BOTH = NEAR + ((-1, True, 1), (-1, True, 0), (2, False, 1))
+FAR = ((-1, True, 1), (-1, True, 0), (2, False, 1))
 
 
 ANY = pl.BlockSpec(memory_space=pl.ANY)
+HBM = pl.BlockSpec(memory_space=pltpu.HBM)
 SM = pl.BlockSpec(memory_space=pltpu.SMEM)
 VM = pl.BlockSpec(memory_space=pltpu.VMEM)
 MIB = 1024 * 1024
 
 
-def join(*parts):
+def join(*parts, space=None):
     rows = [p.shape[0] for p in parts]
 
     def body(*refs):
@@ -90,7 +92,7 @@
     return pl.pallas_call(
         body,
         out_shape=jax.ShapeDtypeStruct((sum(rows), parts[0].shape[1]), parts[0].dtype),
-        in_specs=[ANY] * len(parts),
+        in_specs=[space or ANY] * len(parts),
         out_specs=ANY,
         scratch_shapes=[pltpu.SemaphoreType.DMA((len(parts),))],
         compiler_params=pltpu.CompilerParams(vmem_limit_bytes=MIB),
@@ -157,7 +159,7 @@
             jax.ShapeDtypeStruct((rows, 768), BF16),
             jax.ShapeDtypeStruct((features, 768), BF16),
         ],
-        in_specs=[SM] + [ANY] * (nt + np_),
+        in_specs=[SM] + [HBM] * (nt + np_),
         out_specs=[VM, ANY],
         scratch_shapes=[
             pltpu.VMEM((rows, features), BF16),
@@ -167,7 +169,7 @@
             pltpu.SemaphoreType.DMA((n_copies,)),
             pltpu.SemaphoreType.DMA,
         ],
-        compiler_params=pltpu.CompilerParams(vmem_limit_bytes=30 * MIB),
+        compiler_params=pltpu.CompilerParams(vmem_limit_bytes=60 * MIB),
     )(pos, *toks, *[p[0] for p in pieces])
 
 
@@ -225,7 +227,7 @@
         in_specs=[ANY] * 4,
         out_specs=VM,
         scratch_shapes=_half_scratch(rows, half),
-        compiler_params=pltpu.CompilerParams(vmem_limit_bytes=16 * MIB),
+        compiler_params=pltpu.CompilerParams(vmem_limit_bytes=60 * MIB),
     )(*toks, w)
 
 
@@ -246,7 +248,7 @@
     n = toks[0].shape[0]
 
     def body(pos_ref, t0, t1, t2, w_ref, acc_ref, done_ref, slot, neighbour, first,
-             full, to_near, to_far, t_buf, w_buf, t_sem, w_sem, acc, wide):
+             full, near_k, near_v, far_k, far_v, t_buf, w_buf, t_sem, w_sem, acc, wide):
         block, zl, y, blocks = pos_ref[3], pos_ref[4], pos_ref[5], pos_ref[6]
         product = _half_product((t0, t1, t2), w_ref, half, t_buf, w_buf, t_sem, w_sem)
 
@@ -265,10 +267,10 @@
             full[pl.ds(row_of(place), n), :] = part
             wide[pl.ds(row_of(place), n), :] = part.astype(F32)
         up = 1 - 2 * pos_ref[2]
-        for out, step in ((to_near, up), (to_far, -up)):
+        for keys, values, step in ((far_k, far_v, -up), (near_k, near_v, up)):
             target = (block + step + blocks) % blocks
 
-            def pick(p, carry, out=out, target=target):
+            def pick(p, carry, keys=keys, values=values, target=target):
                 tile = _tile_at(slot, target, p)
                 seen = jnp.int32(0)
                 starts = [jnp.int32(0), jnp.int32(0)]
@@ -287,20 +289,18 @@
                         wide[pl.ds(al, SLAB + 8), :], (SLAB + 8 - rem) % (SLAB + 8), 0
                     )
                     at = pl.multiple_of((p * 2 + o) * SLAB, SLAB)
-                    out[pl.ds(at, SLAB), :] = window[:SLAB].astype(BF16)
+                    keys[pl.ds(at, SLAB), :] = window[:SLAB, :384].astype(BF16)
+                    values[pl.ds(at, SLAB), :] = window[:SLAB, 384:].astype(BF16)
                 return carry
 
             lax.fori_loop(0, TPD, pick, 0)
 
     return pl.pallas_call(
         body,
-        out_shape=[
-            jax.ShapeDtypeStruct((TPD * TILE, 768), BF16),
-            jax.ShapeDtypeStruct((HALO, 768), BF16),
-            jax.ShapeDtypeStruct((HALO, 768), BF16),
-        ],
+        out_shape=[jax.ShapeDtypeStruct((TPD * TILE, 768), BF16)]
+        + [jax.ShapeDtypeStruct((HALO, 384), BF16)] * 4,
         in_specs=[SM] + [ANY] * 4 + [VM, VM] + [SM] * 3,
-        out_specs=[VM, VM, VM],
+        out_specs=[VM] * 5,
         scratch_shapes=_half_scratch(rows, half)
         + [pltpu.VMEM((rows, 768), F32), pltpu.VMEM((TPD * TILE + 8, 768), F32)],
         compiler_params=pltpu.CompilerParams(vmem_limit_bytes=24 * MIB),
@@ -310,92 +310,145 @@
 CAND = 768
 
 
-def attend(pos, queries, full, from_near, from_far, tables):
+def _clear_rest(cand):
+    cand[pl.ds(TILE + NB * WIN, CAND - TILE - NB * WIN), :] = jnp.zeros(
+        (CAND - TILE - NB * WIN, 384), BF16
+    )
+    for j in range(NB):
+        cand[pl.ds(TILE + j * WIN + SLAB, WIN - SLAB), :] = jnp.zeros((WIN - SLAB, 384), BF16)
+
+
+def _collect(p, pos_ref, slot, neighbour, first, full_ref, near_ref, far_ref, cand, side):
+    block, blocks = pos_ref[3], pos_ref[6]
+    cols = slice(side * 384, side * 384 + 384)
+    tile = _tile_at(slot, block, p)
+    own = pl.multiple_of(p * TILE, TILE)
+    cand[pl.ds(0, TILE), :] = full_ref[pl.ds(own, TILE), cols]
+    up = 1 - 2 * pos_ref[2]
+    near_block = (block + up + blocks) % blocks
+    far_block = (block - up + blocks) % blocks
+    seen_near = jnp.int32(0)
+    seen_far = jnp.int32(0)
+    places = []
+    for j in range(NB):
+        other = neighbour[j, tile]
+        at = other // TPD
+        is_near = at == near_block
+        is_far = at == far_block
+        s = first[j, tile]
+        al = _aligned(s)
+        c0 = TILE + j * WIN
+        begin = slot[0, other] % TPD * TILE + al
+        away = jnp.logical_or(is_near, is_far)
+
+        @pl.when(is_near)
+        def _(c0=c0, seen=seen_near):
+            row = pl.multiple_of((p * 2 + seen) * SLAB, SLAB)
+            cand[pl.ds(c0, SLAB), :] = near_ref[pl.ds(row, SLAB), :]
+
+        @pl.when(is_far)
+        def _(c0=c0, seen=seen_far):
+            row = pl.multiple_of((p * 2 + seen) * SLAB, SLAB)
+            cand[pl.ds(c0, SLAB), :] = far_ref[pl.ds(row, SLAB), :]
+
+        @pl.when(jnp.logical_not(away))
+        def _(c0=c0, begin=begin):
+            cand[pl.ds(c0, WIN), :] = full_ref[pl.ds(pl.multiple_of(begin, 16), WIN), cols]
+
+        places.append(c0 + jnp.where(away, 0, s - al))
+        seen_near = seen_near + is_near.astype(jnp.int32)
+        seen_far = seen_far + is_far.astype(jnp.int32)
+    return tile, places
+
+
+def weigh(pos, queries, full, near_k, far_k, tables):
     scale = 1.0 / math.sqrt(HD)
 
     def body(pos_ref, q_ref, full_ref, near_ref, far_ref, slot, neighbour, first, length,
-             low, high, out, cand):
+             low, high, prob, total, cand):
         p = pl.program_id(0)
-        block, blocks = pos_ref[3], pos_ref[6]
 
         @pl.when(p == 0)
         def _():
-            cand[pl.ds(TILE + NB * WIN, CAND - TILE - NB * WIN), :] = jnp.zeros(
-                (CAND - TILE - NB * WIN, 768), BF16
-            )
-            for j in range(NB):
-                cand[pl.ds(TILE + j * WIN + SLAB, WIN - SLAB), :] = jnp.zeros(
-                    (WIN - SLAB, 768), BF16
-                )
-
-        tile = _tile_at(slot, block, p)
-        own = pl.multiple_of(p * TILE, TILE)
-        cand[pl.ds(0, TILE), :] = full_ref[pl.ds(own, TILE), :]
+            _clear_rest(cand)
+
+        tile, places = _collect(
+            p, pos_ref, slot, neighbour, first, full_ref, near_ref, far_ref, cand, 0
+        )
         col = lax.broadcasted_iota(jnp.int32, (8, CAND), 1)
         lows = jnp.where(col < TILE, 0, TILE)
         highs = jnp.where(col < TILE, TILE, 0)
-        up = 1 - 2 * pos_ref[2]
-        near_block = (block + up + blocks) % blocks
-        far_block = (block - up + blocks) % blocks
-        seen_near = jnp.int32(0)
-        seen_far = jnp.int32(0)
         for j in range(NB):
-            other = neighbour[j, tile]
-            at = other // TPD
-            is_near = at == near_block
-            is_far = at == far_block
-            s = first[j, tile]
-            al = _aligned(s)
-            c0 = TILE + j * WIN
-            begin = slot[0, other] % TPD * TILE + al
-
-            @pl.when(is_near)
-            def _(c0=c0, seen_near=seen_near):
-                at = pl.multiple_of((p * 2 + seen_near) * SLAB, SLAB)
-                cand[pl.ds(c0, SLAB), :] = near_ref[pl.ds(at, SLAB), :]
-
-            @pl.when(is_far)
-            def _(c0=c0, seen_far=seen_far):
-                at = pl.multiple_of((p * 2 + seen_far) * SLAB, SLAB)
-                cand[pl.ds(c0, SLAB), :] = far_ref[pl.ds(at, SLAB), :]
-
-            away = jnp.logical_or(is_near, is_far)
-
-            @pl.when(jnp.logical_not(away))
-            def _(c0=c0, begin=begin):
-                cand[pl.ds(c0, WIN), :] = full_ref[pl.ds(pl.multiple_of(begin, 16), WIN), :]
-
-            rem = jnp.where(away, 0, s - al)
-            seen_near = seen_near + is_near.astype(jnp.int32)
-            seen_far = seen_far + is_far.astype(jnp.int32)
-            valid = jnp.logical_and(col >= c0 + rem, col < c0 + rem + length[j, tile])
+            valid = jnp.logical_and(col >= places[j], col < places[j] + length[j, tile])
             lows = jnp.where(valid, low[j, tile], lows)
             highs = jnp.where(valid, high[j, tile], highs)
         row = lax.broadcasted_iota(jnp.int32, (TILE, CAND), 0)
         allowed = jnp.logical_and(row >= lows[0:1, :], row < highs[0:1, :])
         for h in range(3):
-            q = q_ref[:, h * HD : (h + 1) * HD]
-            k = cand[:, h * HD : (h + 1) * HD]
-            v = cand[:, 384 + h * HD : 384 + (h + 1) * HD]
+            cols = slice(h * HD, h * HD + HD)
             scores = lax.dot_general(
-                q, k, (((1,), (1,)), ((), ())), preferred_element_type=F32
+                q_ref[:, cols],
+                cand[:, cols],
+                (((1,), (1,)), ((), ())),
+                preferred_element_type=F32,
             ) * scale
             scores = jnp.where(allowed, scores, -jnp.inf)
             top = jnp.max(scores, axis=-1, keepdims=True)
             weights = jnp.exp(scores - top)
-            total = jnp.sum(weights, axis=-1, keepdims=True)
-            mixed = jnp.dot(weights.astype(BF16), v, preferred_element_type=F32)
-            out[:, h * HD : (h + 1) * HD] = (mixed / total).astype(BF16)
+            total[:, cols] = jnp.broadcast_to(
+                jnp.sum(weights, axis=-1, keepdims=True), (TILE, HD)
+            )
+            prob[0, h] = weights.astype(BF16)
 
     return pl.pallas_call(
         body,
         grid=(TPD,),
-        out_shape=jax.ShapeDtypeStruct(queries.shape, BF16),
+        out_shape=[
+            jax.ShapeDtypeStruct((TPD, 3, TILE, CAND), BF16),
+            jax.ShapeDtypeStruct((TPD * TILE, 384), F32),
+        ],
         in_specs=[SM, pl.BlockSpec((TILE, 384), lambda p: (p, 0)), VM, VM, VM] + [SM] * 6,
+        out_specs=[
+            pl.BlockSpec((1, 3, TILE, CAND), lambda p: (p, 0, 0, 0)),
+            pl.BlockSpec((TILE, 384), lambda p: (p, 0)),
+        ],
+        scratch_shapes=[pltpu.VMEM((CAND, 384), BF16)],
+        compiler_params=pltpu.CompilerParams(vmem_limit_bytes=24 * MIB),
+    )(pos, queries, full, near_k, far_k, *tables)
+
+
+def mix(pos, prob, total, full, near_v, far_v, tables):
+    def body(pos_ref, prob_ref, total_ref, full_ref, near_ref, far_ref, slot, neighbour, first,
+             out, cand):
+        p = pl.program_id(0)
+
+        @pl.when(p == 0)
+        def _():
+            _clear_rest(cand)
+
+        _collect(p, pos_ref, slot, neighbour, first, full_ref, near_ref, far_ref, cand, 1)
+        for h in range(3):
+            cols = slice(h * HD, h * HD + HD)
+            mixed = jnp.dot(prob_ref[0, h], cand[:, cols], preferred_element_type=F32)
+            out[:, cols] = (mixed / total_ref[:, cols]).astype(BF16)
+
+    return pl.pallas_call(
+        body,
+        grid=(TPD,),
+        out_shape=jax.ShapeDtypeStruct((TPD * TILE, 384), BF16),
+        in_specs=[
+            SM,
+            pl.BlockSpec((1, 3, TILE, CAND), lambda p: (p, 0, 0, 0)),
+            pl.BlockSpec((TILE, 384), lambda p: (p, 0)),
+            VM,
+            VM,
+            VM,
+        ]
+        + [SM] * 3,
         out_specs=pl.BlockSpec((TILE, 384), lambda p: (p, 0)),
-        scratch_shapes=[pltpu.VMEM((CAND, 768), BF16)],
+        scratch_shapes=[pltpu.VMEM((CAND, 384), BF16)],
         compiler_params=pltpu.CompilerParams(vmem_limit_bytes=24 * MIB),
-    )(pos, queries, full, from_near, from_far, *tables)
+    )(pos, prob, total, full, near_v, far_v, *tables)
 
 
 def per_device(
@@ -426,32 +479,45 @@
     )
 
     h = tokens.shape[1] // 2
-    w = join(w_key, w_value)
-    pair = join(w, send(w, dc=1))
+    w = join(w_key, w_value, space=HBM)
+    wc = send(w, dc=1)
     ya = send(tokens, dy=1)
-    z1 = send(pair, sz=1)
+    z1w = send(w, sz=1)
     yb = send(tokens, dy=-1)
-    xa1 = send(pair, sx=1)
+    z1c = send(wc, sz=1)
+    xw1 = send(w, sx=1)
+    xc1 = send(wc, sx=1)
+    z2 = send(z1w, sz=1)
+    xw2 = send(xw1, sx=1)
     tl, tr = tokens[:, :h], tokens[:, h:]
-    xa2 = send(xa1[: 2 * fs], sx=1)
-    z2 = send(z1[: 2 * fs], sz=1)
     z_l = send(tl, dzl=1)
+    near = join(z1w, z1c, z2)
+    xn1 = send(near, sx=1)
+    far = send(near, dc=1)
     z_r = send(tr, dzl=1)
-    near = join(z1, z2)
-    both = join(near, send(near, dc=1))
-    xb1 = send(both, sx=1)
+    xf1 = send(far, sx=1)
     yo_l = send(ya[:, :h], dy=1)
     yo_r = send(yb[:, h:], dy=-1)
+    xn2 = send(xn1, sx=1)
     ua_l = send(z_l, dy=1)
     ub_l = send(z_l, dy=-1)
-    xb2 = send(xb1[: 6 * fs], sx=1)
     uo_l = send(yo_l, dzl=1)
     uo_r = send(yo_r, dzl=1)
     ua_r = send(z_r, dy=1)
     ub_r = send(z_r, dy=-1)
-    pieces = [(pair, 0, False, 0, PAIR), (both, 0, False, 0, BOTH)]
+    pieces = [
+        (w, 0, False, 0, SAME),
+        (wc, 0, False, 0, OTHER),
+        (near, 0, False, 0, NEAR),
+        (far, 0, False, 0, FAR),
+    ]
     for p, xrel, signed, plan in (
-        (xa1, 1, True, PAIR), (xa2, 2, False, PAIR[:1]), (xb1, 1, True, BOTH), (xb2, 2, False, NEAR)
+        (xw1, 1, True, SAME),
+        (xc1, 1, True, OTHER),
+        (xw2, 2, False, SAME),
+        (xn1, 1, True, NEAR),
+        (xf1, 1, True, FAR),
+        (xn2, 2, False, NEAR),
     ):
         pieces += [(p, xrel, signed, 0, plan), (send(p, dc=1), xrel, signed, 1, plan)]
 
@@ -460,7 +526,7 @@
     at = ((0, 0), (n, 0), (2 * n, 0), (3 * n, 0), (3 * n, h), (4 * n, 0), (4 * n, h))
     kv1, w_all = project(pos, toks, at, 5 * n, pieces, fs)
     part = project_half((ua_l, ub_l, uo_l), w_all)
-    full, to_near, to_far = project_last(
+    full, *slabs = project_last(
         pos,
         (ua_r, ub_r, uo_r),
         w_all,
@@ -470,9 +536,13 @@
         ((1, -1), (1, 1), (1, 2)),
         tables[:3],
     )
-    from_far = lax.ppermute(to_far, AXES, _far_moves())
-    from_near = lax.ppermute(to_near, AXES, _moves(dc=1))
-    return attend(pos, queries, full, from_near, from_far, tables)
+    near_k, near_v, far_k, far_v = slabs
+    far_k = send(far_k, far=1)
+    near_k = send(near_k, dc=1)
+    far_v = send(far_v, far=1)
+    near_v = send(near_v, dc=1)
+    prob, total = weigh(pos, queries, full, near_k, far_k, tables)
+    return mix(pos, prob, total, full, near_v, far_v, tables[:3])
 
 
 def solution(mesh):

time: 188 us -> 178 us (0.947); the launches traced: 186 us -> 178 us
  waiting for transfers between devices: 103 us -> 76.5 us
  starting transfers between devices: 32.5 us -> 54.7 us
  local copies, waits for them, and re-layouts: 18.1 us -> 9.64 us
  Pallas kernels: 32.1 us -> 36.7 us
    ppermute x26 -> x33, waiting for transfers between devices: 103 us -> 76.5 us  [send(): lax.ppermute(a, AXES, _far_moves() if 'far' in step else _moves(**step))]
    ppermute x26 -> x33, starting transfers between devices: 32.5 us -> 54.7 us  [send(): lax.ppermute(a, AXES, _far_moves() if 'far' in step else _moves(**step))]
    unnamed x60 -> x66, local copies, waits for them, and re-layouts: 17.7 us -> 7.61 us
    pallas_call x1, Pallas kernels: 9.96 us -> 12.8 us  [project(): pl.pallas_call(body, out_shape=[jax.ShapeDtypeStruct((rows, 768), BF16),...]
    pallas_call x1 -> x2, Pallas kernels: 9.54 us -> 11.3 us  [the longest x1 6.92 us: weigh(): pl.pallas_call(body, grid=(TPD,), out_shape=[jax.ShapeDtypeStruct((TPD, 3...]
  transfers between devices with their start and end apart: 26 -> 33, of which waited for: 13 -> 11; matrix products, arithmetic and copies ran while one was open for 0% -> 1% of each run, Pallas kernels for 8% -> 15%
where the time goes in v1:
time: 178 us
  waiting for transfers between devices  76.5 us (43%)
  starting transfers between devices  54.7 us (31%)
  Pallas kernels  36.7 us (21%)
  local copies, waits for them, and re-layouts  9.64 us (5%)
    ppermute x33, waiting for transfers between devices, send(): lax.ppermute(a, AXES, _far_moves() if 'far' in step else _moves(**step))  76.5 us
    ppermute x33, starting transfers between devices, send(): lax.ppermute(a, AXES, _far_moves() if 'far' in step else _moves(**step))  54.7 us
    pallas_call x1, Pallas kernels, project(): pl.pallas_call(body, out_shape=[jax.ShapeDtypeStruct((rows, 768), BF16),...  12.8 us
    unnamed x66, local copies, waits for them, and re-layouts  7.61 us
    pallas_call x1, Pallas kernels, weigh(): pl.pallas_call(body, grid=(TPD,), out_shape=[jax.ShapeDtypeStruct((TPD, 3...  6.92 us
    pallas_call x1, Pallas kernels, project_last(): pl.pallas_call(body, out_shape=[jax.ShapeDtypeStruct((TPD * TILE, 768), B...  6.02 us
    pallas_call x1, Pallas kernels, project_half(): pl.pallas_call(body, out_shape=jax.ShapeDtypeStruct((rows, 768), F32), in...  5.45 us
    pallas_call x1, Pallas kernels, mix(): pl.pallas_call(body, grid=(TPD,), out_shape=jax.ShapeDtypeStruct((TPD * T...  4.34 us
  transfers between devices with their start and end apart: 33, of which 11 were waited for; matrix products, arithmetic and copies ran while one was open for 1% of the time, Pallas kernels for 15%

profile of v1, /device:TPU:32, one launch (start us, length us, event | category | flops | bytes accessed | tf_op | source)
XLA Modules:
  0.0 178.0 jit_solution(12897586998657445641)
XLA Ops:
  2.2 3.3 %collective-permute-start.10 = (bf16[320,384]{1,0:T(8,128)(2,1)S(1)}, bf16[320,384]{1,0:T(8,128)(2,1)S(1)}, u32[]{:S(2)}, u32[]{:S(2)}) collective-permute-start(bf16[320,384]{1,0:T(8,128)(2,1)S(1)} %shard_map.100.refs_8_), channel_id=1, source_target_pairs={{0,16},{1,17},{2,18},{3,19},{4,20},{5,21},{6,22},{7,23},{8,56},{9,... | collective-permute-start | bytes 737288 | tf_op jit(solution)/shard_map/ppermute | solution.py:61
  8.7 4.5 %collective-permute-start.11 = (bf16[320,384]{1,0:T(8,128)(2,1)S(1)}, bf16[320,384]{1,0:T(8,128)(2,1)S(1)}, u32[]{:S(2)}, u32[]{:S(2)}) collective-permute-start(bf16[320,384]{1,0:T(8,128)(2,1)S(1)} %collective-permute-done.9.refs_9_), channel_id=1, source_target_pairs={{0,16},{1,17},{2,18},{3,19},{4,20},{5,21},{6,22},{7,23},{8,56},{9,... | collective-permute-start | bytes 737288 | tf_op jit(solution)/shard_map/ppermute | solution.py:61
  17.9 17.3 %collective-permute-start.15 = (bf16[320,384]{1,0:T(8,128)(2,1)S(1)}, bf16[320,384]{1,0:T(8,128)(2,1)S(1)}, u32[]{:S(2)}, u32[]{:S(2)}) collective-permute-start(bf16[320,384]{1,0:T(8,128)(2,1)S(1)} %collective-permute-done.14.refs_12_), channel_id=1, source_target_pairs={{0,8},{1,9},{2,10},{3,11},{4,12},{5,13},{6,14},{7,15},{8,0},{9,1},... | collective-permute-start | bytes 737288 | tf_op jit(solution)/shard_map/ppermute | solution.py:61
  35.2 1.9 %collective-permute-start.3 = (bf16[128,5120]{1,0:T(8,128)(2,1)S(1)}, bf16[128,5120]{1,0:T(8,128)(2,1)S(1)}, u32[]{:S(2)}, u32[]{:S(2)}) collective-permute-start(bf16[128,5120]{1,0:T(8,128)(2,1)S(1)} %copy-done.15), channel_id=1, source_target_pairs={{0,3},{1,0},{2,1},{3,2},{4,7},{5,4},{6,5},{7,6},{8,11},{9,8},{10,9... | collective-permute-start | bytes 3932168 | tf_op jit(solution)/shard_map/ppermute | solution.py:61
  37.1 6.0 %collective-permute-start.8 = (bf16[128,2560]{1,0:T(8,128)(2,1)S(1)}, bf16[128,2560]{1,0:T(8,128)(2,1)}, u32[]{:S(2)}, u32[]{:S(2)}) collective-permute-start(bf16[128,2560]{1,0:T(8,128)(2,1)S(1)} %get-tuple-element.23), channel_id=1, source_target_pairs={{0,4},{1,5},{2,6},{3,7},{4,0},{5,1},{6,2},{7,3},{8,12},{9,13},{10,... | collective-permute-start | bytes 1966088 | tf_op jit(solution)/shard_map/ppermute | solution.py:61
  44.2 1.6 collective-permute-start.20
  46.4 9.8 %collective-permute-done.8.refs_6_ = bf16[128,2560]{1,0:T(8,128)(2,1)} collective-permute-done((bf16[128,2560]{1,0:T(8,128)(2,1)S(1)}, bf16[128,2560]{1,0:T(8,128)(2,1)}, u32[]{:S(2)}, u32[]{:S(2)}) %collective-permute-start.8) | collective-permute-done | bytes 655392 | tf_op jit(solution)/shard_map/ppermute | solution.py:61
  59.3 5.9 %collective-permute-done.3.refs_3_ = bf16[128,5120]{1,0:T(8,128)(2,1)S(1)} collective-permute-done((bf16[128,5120]{1,0:T(8,128)(2,1)S(1)}, bf16[128,5120]{1,0:T(8,128)(2,1)S(1)}, u32[]{:S(2)}, u32[]{:S(2)}) %collective-permute-start.3) | collective-permute-done | bytes 1310752 | tf_op jit(solution)/shard_map/ppermute | solution.py:61
  65.2 1.8 collective-permute-start.19
  67.0 12.3 %collective-permute-done.6.refs_2_ = bf16[128,5120]{1,0:T(8,128)(2,1)S(1)} collective-permute-done((bf16[128,5120]{1,0:T(8,128)(2,1)S(1)}, bf16[128,5120]{1,0:T(8,128)(2,1)S(1)}, u32[]{:S(2)}, u32[]{:S(2)}) %collective-permute-start.6) | collective-permute-done | bytes 1310752 | tf_op jit(solution)/shard_map/ppermute | solution.py:61
  80.3 13.1 %collective-permute-done.26.t0 = bf16[128,2560]{1,0:T(8,128)(2,1)S(1)} collective-permute-done((bf16[128,2560]{1,0:T(8,128)(2,1)}, bf16[128,2560]{1,0:T(8,128)(2,1)S(1)}, u32[]{:S(2)}, u32[]{:S(2)}) %collective-permute-start.26) | collective-permute-done | bytes 655392 | tf_op jit(solution)/shard_map/ppermute | solution.py:61
  93.5 13.0 %collective-permute-done.7.refs_4_ = bf16[128,2560]{1,0:T(8,128)(2,1)} collective-permute-done((bf16[128,2560]{1,0:T(8,128)(2,1)S(1)}, bf16[128,2560]{1,0:T(8,128)(2,1)}, u32[]{:S(2)}, u32[]{:S(2)}) %collective-permute-start.7) | collective-permute-done | bytes 655392 | tf_op jit(solution)/shard_map/ppermute | solution.py:61
  106.5 4.6 %collective-permute-done.4.refs_5_ = bf16[128,2560]{1,0:T(8,128)(2,1)} collective-permute-done((bf16[128,2560]{1,0:T(8,128)(2,1)S(1)}, bf16[128,2560]{1,0:T(8,128)(2,1)}, u32[]{:S(2)}, u32[]{:S(2)}) %collective-permute-start.4) | collective-permute-done | bytes 655392 | tf_op jit(solution)/shard_map/ppermute | solution.py:61
  111.1 3.3 %collective-permute-start.2 = (bf16[128,2560]{1,0:T(8,128)(2,1)}, bf16[128,2560]{1,0:T(8,128)(2,1)S(1)}, u32[]{:S(2)}, u32[]{:S(2)}) collective-permute-start(bf16[128,2560]{1,0:T(8,128)(2,1)} %collective-permute-done.refs_7_), channel_id=1, source_target_pairs={{0,3},{1,0},{2,1},{3,2},{4,7},{5,4},{6,5},{7,6},{8,11},{9,8},{10,9... | collective-permute-start | bytes 1966088 | tf_op jit(solution)/shard_map/ppermute | solution.py:61
  115.9 12.8 %shard_map.102 = (bf16[640,768]{1,0:T(8,128)(2,1)}, bf16[5120,768]{1,0:T(8,128)(2,1)}) custom-call(s32[7]{0:T(128)} %stack.27.refs_0_.pos_ref, bf16[128,5120]{1,0:T(8,128)(2,1)} %refs_1_.3, bf16[128,5120]{1,0:T(8,128)(2,1)} %copy-done.17, bf16[128,5120]{1,0:T(8,128)(2,1)} %copy-done.16, bf16[128,2560]{1,0:T(8,128)(2,1)} %collective-permute-done.7.refs_4_, ...), custom_call_target="tpu_custom_call" | custom-call | tf_op jit(solution)/shard_map/pallas_call | solution.py:156
  128.7 5.5 %shard_map.103.acc_ref = f32[384,768]{1,0:T(8,128)} custom-call(bf16[128,2560]{1,0:T(8,128)(2,1)} %copy-done.25, bf16[128,2560]{1,0:T(8,128)(2,1)} %collective-permute-done.27.t1, bf16[128,2560]{1,0:T(8,128)(2,1)} %collective-permute-done.28.t2, bf16[5120,768]{1,0:T(8,128)(2,1)} %get-tuple-element.14.w_ref), custom_call_target="tpu_custom_call" | custom-call | tf_op jit(solution)/shard_map/pallas_call | solution.py:224
  134.2 1.9 %collective-permute-done.2.t1 = bf16[128,2560]{1,0:T(8,128)(2,1)S(1)} collective-permute-done((bf16[128,2560]{1,0:T(8,128)(2,1)}, bf16[128,2560]{1,0:T(8,128)(2,1)S(1)}, u32[]{:S(2)}, u32[]{:S(2)}) %collective-permute-start.2) | collective-permute-done | bytes 655392 | tf_op jit(solution)/shard_map/ppermute | solution.py:61
  136.4 3.2 %copy-done = bf16[5120,768]{1,0:T(8,128)(2,1)S(1)} copy-done((bf16[5120,768]{1,0:T(8,128)(2,1)S(1)}, bf16[5120,768]{1,0:T(8,128)(2,1)}, u32[]{:S(2)}) %copy-start) | copy-done | bytes 7864344
  140.9 6.0 %shard_map.104 = (bf16[1024,768]{1,0:T(8,128)(2,1)S(1)}, bf16[512,384]{1,0:T(8,128)(2,1)S(1)}, bf16[512,384]{1,0:T(8,128)(2,1)S(1)}, bf16[512,384]{1,0:T(8,128)(2,1)S(1)}, bf16[512,384]{1,0:T(8,128)(2,1)S(1)}) custom-call(s32[7]{0:T(128)S(1)} %copy-done.10, bf16[128,2560]{1,0:T(8,128)(2,1)S(1)} %collective-permute-done.1.t0, ...), custom_call_target="tpu_custom_call" | custom-call | tf_op jit(solution)/shard_map/pallas_call | solution.py:298
  147.0 4.1 %collective-permute-start.30 = (bf16[512,384]{1,0:T(8,128)(2,1)S(1)}, bf16[512,384]{1,0:T(8,128)(2,1)S(1)}, u32[]{:S(2)}, u32[]{:S(2)}) collective-permute-start(bf16[512,384]{1,0:T(8,128)(2,1)S(1)} %get-tuple-element.18), channel_id=1, source_target_pairs={{0,248},{1,249},{2,250},{3,251},{4,252},{5,253},{6,254},{7,255},{8... | collective-permute-start | bytes 1179656 | tf_op jit(solution)/shard_map/ppermute | solution.py:61
  151.2 1.9 %collective-permute-start.32 = (bf16[512,384]{1,0:T(8,128)(2,1)S(1)}, bf16[512,384]{1,0:T(8,128)(2,1)S(1)}, u32[]{:S(2)}, u32[]{:S(2)}) collective-permute-start(bf16[512,384]{1,0:T(8,128)(2,1)S(1)} %get-tuple-element.22), channel_id=1, source_target_pairs={{0,248},{1,249},{2,250},{3,251},{4,252},{5,253},{6,254},{7,255},{8... | collective-permute-start | bytes 1179656 | tf_op jit(solution)/shard_map/ppermute | solution.py:61
  153.1 13.6 %collective-permute-done.30.far_ref = bf16[512,384]{1,0:T(8,128)(2,1)S(1)} collective-permute-done((bf16[512,384]{1,0:T(8,128)(2,1)S(1)}, bf16[512,384]{1,0:T(8,128)(2,1)S(1)}, u32[]{:S(2)}, u32[]{:S(2)}) %collective-permute-start.30) | collective-permute-done | bytes 393248 | tf_op jit(solution)/shard_map/ppermute | solution.py:61
  166.7 6.9 %shard_map.105 = (bf16[4,3,256,768]{3,2,1,0:T(8,128)(2,1)S(1)}, f32[1024,384]{1,0:T(8,128)S(1)}) custom-call(s32[7]{0:T(128)S(1)} %copy-done.10, bf16[1024,384]{1,0:T(8,128)(2,1)S(1)} %copy-done.5, bf16[1024,768]{1,0:T(8,128)(2,1)S(1)} %get-tuple-element.16.full_ref, bf16[512,384]{1,0:T(8,128)(2,1)S(1)} %collective-permute-done.29.near_ref, ...), custom_call_target="tpu_custom_call" | custom-call | tf_op jit(solution)/shard_map/pallas_call | solution.py:403
  173.7 4.3 %shard_map.106 = bf16[1024,384]{1,0:T(8,128)(2,1)} custom-call(s32[7]{0:T(128)S(1)} %copy-done.10, bf16[4,3,256,768]{3,2,1,0:T(8,128)(2,1)S(1)} %get-tuple-element.19.prob_ref, f32[1024,384]{1,0:T(8,128)S(1)} %get-tuple-element.20.total_ref, bf16[1024,768]{1,0:T(8,128)(2,1)S(1)} %get-tuple-element.16.full_ref, ...), custom_call_target="tpu_custom_call" | custom-call | tf_op jit(solution)/shard_map/pallas_call | solution.py:435
  (119 shorter events, 18.9 us)
Async XLA Ops:
  7.0 39.5 %collective-permute-start = (bf16[128,2560]{1,0:T(8,128)(2,1)S(1)}, bf16[128,2560]{1,0:T(8,128)(2,1)}, u32[]{:S(2)}, u32[]{:S(2)}) collective-permute-start(bf16[128,2560]{1,0:T(8,128)(2,1)S(1)} %get-tuple-element.24), channel_id=1, source_target_pairs={{0,4},{1,5},{2,6},{3,7},{4,0},{5,1},{6,2},{7,3},{8,12},{9,13},{10,... | collective-permute-start | bytes 1966088 | tf_op jit(solution)/shard_map/ppermute | solution.py:61
  14.5 20.7 %collective-permute-start.12 = (bf16[320,384]{1,0:T(8,128)(2,1)S(1)}, bf16[320,384]{1,0:T(8,128)(2,1)S(1)}, u32[]{:S(2)}, u32[]{:S(2)}) collective-permute-start(bf16[320,384]{1,0:T(8,128)(2,1)S(1)} %collective-permute-done.10.refs_0_), channel_id=1, source_target_pairs={{0,16},{1,17},{2,18},{3,19},{4,20},{5,21},{6,22},{7,23},{8,56},{9,... | collective-permute-start | bytes 737288 | tf_op jit(solution)/shard_map/ppermute | solution.py:61
  14.9 22.3 %collective-permute-start.16 = (bf16[320,384]{1,0:T(8,128)(2,1)S(1)}, bf16[320,384]{1,0:T(8,128)(2,1)S(1)}, u32[]{:S(2)}, u32[]{:S(2)}) collective-permute-start(bf16[320,384]{1,0:T(8,128)(2,1)S(1)} %collective-permute-done.9.refs_9_), channel_id=1, source_target_pairs={{0,64},{1,65},{2,66},{3,67},{4,68},{5,69},{6,70},{7,71},{8,200},{9... | collective-permute-start | bytes 737288 | tf_op jit(solution)/shard_map/ppermute | solution.py:61
  16.4 27.8 %collective-permute-start.18 = (bf16[320,384]{1,0:T(8,128)(2,1)S(1)}, bf16[320,384]{1,0:T(8,128)(2,1)S(1)}, u32[]{:S(2)}, u32[]{:S(2)}) collective-permute-start(bf16[320,384]{1,0:T(8,128)(2,1)S(1)} %collective-permute-done.14.refs_12_), channel_id=1, source_target_pairs={{0,64},{1,65},{2,66},{3,67},{4,68},{5,69},{6,70},{7,71},{8,200},{9... | collective-permute-start | bytes 737288 | tf_op jit(solution)/shard_map/ppermute | solution.py:61
  17.9 27.9 %collective-permute-start.15 = (bf16[320,384]{1,0:T(8,128)(2,1)S(1)}, bf16[320,384]{1,0:T(8,128)(2,1)S(1)}, u32[]{:S(2)}, u32[]{:S(2)}) collective-permute-start(bf16[320,384]{1,0:T(8,128)(2,1)S(1)} %collective-permute-done.14.refs_12_), channel_id=1, source_target_pairs={{0,8},{1,9},{2,10},{3,11},{4,12},{5,13},{6,14},{7,15},{8,0},{9,1},... | collective-permute-start | bytes 737288 | tf_op jit(solution)/shard_map/ppermute | solution.py:61
  35.2 30.0 %collective-permute-start.3 = (bf16[128,5120]{1,0:T(8,128)(2,1)S(1)}, bf16[128,5120]{1,0:T(8,128)(2,1)S(1)}, u32[]{:S(2)}, u32[]{:S(2)}) collective-permute-start(bf16[128,5120]{1,0:T(8,128)(2,1)S(1)} %copy-done.15), channel_id=1, source_target_pairs={{0,3},{1,0},{2,1},{3,2},{4,7},{5,4},{6,5},{7,6},{8,11},{9,8},{10,9... | collective-permute-start | bytes 3932168 | tf_op jit(solution)/shard_map/ppermute | solution.py:61
  37.1 19.1 %collective-permute-start.8 = (bf16[128,2560]{1,0:T(8,128)(2,1)S(1)}, bf16[128,2560]{1,0:T(8,128)(2,1)}, u32[]{:S(2)}, u32[]{:S(2)}) collective-permute-start(bf16[128,2560]{1,0:T(8,128)(2,1)S(1)} %get-tuple-element.23), channel_id=1, source_target_pairs={{0,4},{1,5},{2,6},{3,7},{4,0},{5,1},{6,2},{7,3},{8,12},{9,13},{10,... | collective-permute-start | bytes 1966088 | tf_op jit(solution)/shard_map/ppermute | solution.py:61
  46.4 32.9 %collective-permute-start.6 = (bf16[128,5120]{1,0:T(8,128)(2,1)S(1)}, bf16[128,5120]{1,0:T(8,128)(2,1)S(1)}, u32[]{:S(2)}, u32[]{:S(2)}) collective-permute-start(bf16[128,5120]{1,0:T(8,128)(2,1)S(1)} %copy-done.15), channel_id=1, source_target_pairs={{0,1},{1,2},{2,3},{3,0},{4,5},{5,6},{6,7},{7,4},{8,9},{9,10},{10,1... | collective-permute-start | bytes 3932168 | tf_op jit(solution)/shard_map/ppermute | solution.py:61
  56.9 22.4 %collective-permute-start.24 = (bf16[960,384]{1,0:T(8,128)(2,1)S(1)}, bf16[960,384]{1,0:T(8,128)(2,1)S(1)}, u32[]{:S(2)}, u32[]{:S(2)}) collective-permute-start(bf16[960,384]{1,0:T(8,128)(2,1)S(1)} %collective-permute-done.20.refs_18_), channel_id=1, source_target_pairs={{0,64},{1,65},{2,66},{3,67},{4,68},{5,69},{6,70},{7,71},{8,200},{9... | collective-permute-start | bytes 2211848 | tf_op jit(solution)/shard_map/ppermute | solution.py:61
  57.8 22.0 %collective-permute-start.22 = (bf16[960,384]{1,0:T(8,128)(2,1)S(1)}, bf16[960,384]{1,0:T(8,128)(2,1)S(1)}, u32[]{:S(2)}, u32[]{:S(2)}) collective-permute-start(bf16[960,384]{1,0:T(8,128)(2,1)S(1)} %collective-permute-done.13.refs_11_), channel_id=1, source_target_pairs={{0,64},{1,65},{2,66},{3,67},{4,68},{5,69},{6,70},{7,71},{8,200},{9... | collective-permute-start | bytes 2211848 | tf_op jit(solution)/shard_map/ppermute | solution.py:61
  59.3 34.0 %collective-permute-start.26 = (bf16[128,2560]{1,0:T(8,128)(2,1)}, bf16[128,2560]{1,0:T(8,128)(2,1)S(1)}, u32[]{:S(2)}, u32[]{:S(2)}) collective-permute-start(bf16[128,2560]{1,0:T(8,128)(2,1)} %collective-permute-done.8.refs_6_), channel_id=1, source_target_pairs={{0,1},{1,2},{2,3},{3,0},{4,5},{5,6},{6,7},{7,4},{8,9},{9,10},{10,1... | collective-permute-start | bytes 1966088 | tf_op jit(solution)/shard_map/ppermute | solution.py:61
  65.2 15.0 %collective-permute-start.19 = (bf16[320,384]{1,0:T(8,128)(2,1)S(1)}, bf16[320,384]{1,0:T(8,128)(2,1)S(1)}, u32[]{:S(2)}, u32[]{:S(2)}) collective-permute-start(bf16[320,384]{1,0:T(8,128)(2,1)S(1)} %collective-permute-done.18.refs_16_), channel_id=1, source_target_pairs={{0,8},{1,9},{2,10},{3,11},{4,12},{5,13},{6,14},{7,15},{8,0},{9,1},... | collective-permute-start | bytes 737288 | tf_op jit(solution)/shard_map/ppermute | solution.py:61
  79.3 31.7 %collective-permute-start.25 = (bf16[960,384]{1,0:T(8,128)(2,1)S(1)}, bf16[960,384]{1,0:T(8,128)(2,1)S(1)}, u32[]{:S(2)}, u32[]{:S(2)}) collective-permute-start(bf16[960,384]{1,0:T(8,128)(2,1)S(1)} %collective-permute-done.24.refs_22_), channel_id=1, source_target_pairs={{0,8},{1,9},{2,10},{3,11},{4,12},{5,13},{6,14},{7,15},{8,0},{9,1},... | collective-permute-start | bytes 2211848 | tf_op jit(solution)/shard_map/ppermute | solution.py:61
  79.8 34.5 %collective-permute-start.23 = (bf16[960,384]{1,0:T(8,128)(2,1)S(1)}, bf16[960,384]{1,0:T(8,128)(2,1)S(1)}, u32[]{:S(2)}, u32[]{:S(2)}) collective-permute-start(bf16[960,384]{1,0:T(8,128)(2,1)S(1)} %collective-permute-done.22.refs_20_), channel_id=1, source_target_pairs={{0,8},{1,9},{2,10},{3,11},{4,12},{5,13},{6,14},{7,15},{8,0},{9,1},... | collective-permute-start | bytes 2211848 | tf_op jit(solution)/shard_map/ppermute | solution.py:61
  80.2 26.2 %collective-permute-start.7 = (bf16[128,2560]{1,0:T(8,128)(2,1)S(1)}, bf16[128,2560]{1,0:T(8,128)(2,1)}, u32[]{:S(2)}, u32[]{:S(2)}) collective-permute-start(bf16[128,2560]{1,0:T(8,128)(2,1)S(1)} %slice.17), channel_id=1, source_target_pairs={{0,1},{1,2},{2,3},{3,0},{4,5},{5,6},{6,7},{7,4},{8,9},{9,10},{10,1... | collective-permute-start | bytes 1966088 | tf_op jit(solution)/shard_map/ppermute | solution.py:61
  93.3 17.7 %collective-permute-start.4 = (bf16[128,2560]{1,0:T(8,128)(2,1)S(1)}, bf16[128,2560]{1,0:T(8,128)(2,1)}, u32[]{:S(2)}, u32[]{:S(2)}) collective-permute-start(bf16[128,2560]{1,0:T(8,128)(2,1)S(1)} %slice.16), channel_id=1, source_target_pairs={{0,3},{1,0},{2,1},{3,2},{4,7},{5,4},{6,5},{7,6},{8,11},{9,8},{10,9... | collective-permute-start | bytes 1966088 | tf_op jit(solution)/shard_map/ppermute | solution.py:61
  93.4 35.3 %collective-permute-start.27 = (bf16[128,2560]{1,0:T(8,128)(2,1)}, bf16[128,2560]{1,0:T(8,128)(2,1)}, u32[]{:S(2)}, u32[]{:S(2)}) collective-permute-start(bf16[128,2560]{1,0:T(8,128)(2,1)} %collective-permute-done.8.refs_6_), channel_id=1, source_target_pairs={{0,3},{1,0},{2,1},{3,2},{4,7},{5,4},{6,5},{7,6},{8,11},{9,8},{10,9... | collective-permute-start | bytes 1966088 | tf_op jit(solution)/shard_map/ppermute | solution.py:61
  106.4 22.2 %collective-permute-start.28 = (bf16[128,2560]{1,0:T(8,128)(2,1)}, bf16[128,2560]{1,0:T(8,128)(2,1)}, u32[]{:S(2)}, u32[]{:S(2)}) collective-permute-start(bf16[128,2560]{1,0:T(8,128)(2,1)} %collective-permute-done.7.refs_4_), channel_id=1, source_target_pairs={{0,4},{1,5},{2,6},{3,7},{4,0},{5,1},{6,2},{7,3},{8,12},{9,13},{10,... | collective-permute-start | bytes 1966088 | tf_op jit(solution)/shard_map/ppermute | solution.py:61
  111.1 23.1 %collective-permute-start.1 = (bf16[128,2560]{1,0:T(8,128)(2,1)}, bf16[128,2560]{1,0:T(8,128)(2,1)S(1)}, u32[]{:S(2)}, u32[]{:S(2)}) collective-permute-start(bf16[128,2560]{1,0:T(8,128)(2,1)} %collective-permute-done.refs_7_), channel_id=1, source_target_pairs={{0,1},{1,2},{2,3},{3,0},{4,5},{5,6},{6,7},{7,4},{8,9},{9,10},{10,1... | collective-permute-start | bytes 1966088 | tf_op jit(solution)/shard_map/ppermute | solution.py:61
  111.1 25.0 %collective-permute-start.2 = (bf16[128,2560]{1,0:T(8,128)(2,1)}, bf16[128,2560]{1,0:T(8,128)(2,1)S(1)}, u32[]{:S(2)}, u32[]{:S(2)}) collective-permute-start(bf16[128,2560]{1,0:T(8,128)(2,1)} %collective-permute-done.refs_7_), channel_id=1, source_target_pairs={{0,3},{1,0},{2,1},{3,2},{4,7},{5,4},{6,5},{7,6},{8,11},{9,8},{10,9... | collective-permute-start | bytes 1966088 | tf_op jit(solution)/shard_map/ppermute | solution.py:61
  114.4 22.0 %collective-permute-start.5 = (bf16[128,2560]{1,0:T(8,128)(2,1)}, bf16[128,2560]{1,0:T(8,128)(2,1)S(1)}, u32[]{:S(2)}, u32[]{:S(2)}) collective-permute-start(bf16[128,2560]{1,0:T(8,128)(2,1)} %collective-permute-done.4.refs_5_), channel_id=1, source_target_pairs={{0,4},{1,5},{2,6},{3,7},{4,0},{5,1},{6,2},{7,3},{8,12},{9,13},{10,... | collective-permute-start | bytes 1966088 | tf_op jit(solution)/shard_map/ppermute | solution.py:61
  147.0 19.7 %collective-permute-start.30 = (bf16[512,384]{1,0:T(8,128)(2,1)S(1)}, bf16[512,384]{1,0:T(8,128)(2,1)S(1)}, u32[]{:S(2)}, u32[]{:S(2)}) collective-permute-start(bf16[512,384]{1,0:T(8,128)(2,1)S(1)} %get-tuple-element.18), channel_id=1, source_target_pairs={{0,248},{1,249},{2,250},{3,251},{4,252},{5,253},{6,254},{7,255},{8... | collective-permute-start | bytes 1179656 | tf_op jit(solution)/shard_map/ppermute | solution.py:61
  151.2 22.5 %collective-permute-start.31 = (bf16[512,384]{1,0:T(8,128)(2,1)S(1)}, bf16[512,384]{1,0:T(8,128)(2,1)S(1)}, u32[]{:S(2)}, u32[]{:S(2)}) collective-permute-start(bf16[512,384]{1,0:T(8,128)(2,1)S(1)} %get-tuple-element.21), channel_id=1, source_target_pairs={{0,8},{1,9},{2,10},{3,11},{4,12},{5,13},{6,14},{7,15},{8,0},{9,1},... | collective-permute-start | bytes 1179656 | tf_op jit(solution)/shard_map/ppermute | solution.py:61
  151.2 22.5 %collective-permute-start.32 = (bf16[512,384]{1,0:T(8,128)(2,1)S(1)}, bf16[512,384]{1,0:T(8,128)(2,1)S(1)}, u32[]{:S(2)}, u32[]{:S(2)}) collective-permute-start(bf16[512,384]{1,0:T(8,128)(2,1)S(1)} %get-tuple-element.22), channel_id=1, source_target_pairs={{0,248},{1,249},{2,250},{3,251},{4,252},{5,253},{6,254},{7,255},{8... | collective-permute-start | bytes 1179656 | tf_op jit(solution)/shard_map/ppermute | solution.py:61
  (42 other events, 822.0 us)

commit v2 on v1

--- a/solution.py
+++ b/solution.py
@@ -173,7 +173,7 @@
     )(pos, *toks, *[p[0] for p in pieces])
 
 
-def _half_product(toks, w, row0, t_buf, w_buf, t_sem, w_sem):
+def _half_product(toks, w, row0, cols, t_buf, w_buf, t_sem, w_sem):
     n = toks[0].shape[0]
     half = toks[0].shape[1]
     step = half // 2
@@ -182,7 +182,9 @@
         waits.append(pltpu.make_async_copy(ref, t_buf.at[pl.ds(i * n, n), :], t_sem.at[i]))
     loads = [
         pltpu.make_async_copy(
-            w.at[pl.ds(row0 + i * step, step), :], w_buf.at[pl.ds(i * step, step), :], w_sem.at[i]
+            w.at[pl.ds(row0 + i * step, step), pl.ds(*cols)],
+            w_buf.at[pl.ds(i * step, step), :],
+            w_sem.at[i],
         )
         for i in range(2)
     ]
@@ -203,10 +205,10 @@
     return product
 
 
-def _half_scratch(rows, half):
+def _half_scratch(rows, half, width):
     return [
         pltpu.VMEM((rows, half), BF16),
-        pltpu.VMEM((half, 768), BF16),
+        pltpu.VMEM((half, width), BF16),
         pltpu.SemaphoreType.DMA((3,)),
         pltpu.SemaphoreType.DMA((2,)),
     ]
@@ -217,7 +219,7 @@
     half = toks[0].shape[1]
 
     def body(t0, t1, t2, w_ref, acc, t_buf, w_buf, t_sem, w_sem):
-        product = _half_product((t0, t1, t2), w_ref, 0, t_buf, w_buf, t_sem, w_sem)
+        product = _half_product((t0, t1, t2), w_ref, 0, (0, 768), t_buf, w_buf, t_sem, w_sem)
         acc[...] = jnp.zeros_like(acc)
         product(acc)
 
@@ -226,8 +228,8 @@
         out_shape=jax.ShapeDtypeStruct((rows, 768), F32),
         in_specs=[ANY] * 4,
         out_specs=VM,
-        scratch_shapes=_half_scratch(rows, half),
-        compiler_params=pltpu.CompilerParams(vmem_limit_bytes=60 * MIB),
+        scratch_shapes=_half_scratch(rows, half, 768),
+        compiler_params=pltpu.CompilerParams(vmem_limit_bytes=57 * MIB),
     )(*toks, w)
 
 
@@ -242,35 +244,38 @@
     return jnp.minimum(start // 16 * 16, TILE - WIN)
 
 
-def project_last(pos, toks, w, acc_in, done, done_places, places, tables):
+def project_last(side, pos, toks, w, acc_in, done, done_places, places, tables):
     rows = sum(t.shape[0] for t in toks)
     half = toks[0].shape[1]
     n = toks[0].shape[0]
 
     def body(pos_ref, t0, t1, t2, w_ref, acc_ref, done_ref, slot, neighbour, first,
-             full, near_k, near_v, far_k, far_v, t_buf, w_buf, t_sem, w_sem, acc, wide):
+             full, near, far, t_buf, w_buf, t_sem, w_sem, acc, wide, a_sem):
         block, zl, y, blocks = pos_ref[3], pos_ref[4], pos_ref[5], pos_ref[6]
-        product = _half_product((t0, t1, t2), w_ref, half, t_buf, w_buf, t_sem, w_sem)
+        cols = (side * 384, 384)
+        begin = pltpu.make_async_copy(acc_ref.at[:, pl.ds(*cols)], acc, a_sem)
+        begin.start()
+        product = _half_product((t0, t1, t2), w_ref, half, cols, t_buf, w_buf, t_sem, w_sem)
 
         def row_of(place):
             dzl, dy = place
             return pl.multiple_of(((zl + dzl) % NZL * NY + (y + dy + NY) % NY) * n, n)
 
         for i, place in enumerate(done_places):
-            part = done_ref[i * n : (i + 1) * n, :]
+            part = done_ref[i * n : (i + 1) * n, side * 384 : side * 384 + 384]
             full[pl.ds(row_of(place), n), :] = part
             wide[pl.ds(row_of(place), n), :] = part.astype(F32)
-        acc[...] = acc_ref[...]
+        begin.wait()
         product(acc)
         for i, place in enumerate(places):
             part = acc[i * n : (i + 1) * n, :].astype(BF16)
             full[pl.ds(row_of(place), n), :] = part
             wide[pl.ds(row_of(place), n), :] = part.astype(F32)
         up = 1 - 2 * pos_ref[2]
-        for keys, values, step in ((far_k, far_v, -up), (near_k, near_v, up)):
+        for out, step in ((far, -up), (near, up)):
             target = (block + step + blocks) % blocks
 
-            def pick(p, carry, keys=keys, values=values, target=target):
+            def pick(p, carry, out=out, target=target):
                 tile = _tile_at(slot, target, p)
                 seen = jnp.int32(0)
                 starts = [jnp.int32(0), jnp.int32(0)]
@@ -289,21 +294,21 @@
                         wide[pl.ds(al, SLAB + 8), :], (SLAB + 8 - rem) % (SLAB + 8), 0
                     )
                     at = pl.multiple_of((p * 2 + o) * SLAB, SLAB)
-                    keys[pl.ds(at, SLAB), :] = window[:SLAB, :384].astype(BF16)
-                    values[pl.ds(at, SLAB), :] = window[:SLAB, 384:].astype(BF16)
+                    out[pl.ds(at, SLAB), :] = window[:SLAB].astype(BF16)
                 return carry
 
             lax.fori_loop(0, TPD, pick, 0)
 
     return pl.pallas_call(
         body,
-        out_shape=[jax.ShapeDtypeStruct((TPD * TILE, 768), BF16)]
-        + [jax.ShapeDtypeStruct((HALO, 384), BF16)] * 4,
-        in_specs=[SM] + [ANY] * 4 + [VM, VM] + [SM] * 3,
-        out_specs=[VM] * 5,
-        scratch_shapes=_half_scratch(rows, half)
-        + [pltpu.VMEM((rows, 768), F32), pltpu.VMEM((TPD * TILE + 8, 768), F32)],
-        compiler_params=pltpu.CompilerParams(vmem_limit_bytes=24 * MIB),
+        out_shape=[jax.ShapeDtypeStruct((TPD * TILE, 384), BF16)]
+        + [jax.ShapeDtypeStruct((HALO, 384), BF16)] * 2,
+        in_specs=[SM] + [ANY] * 5 + [VM] + [SM] * 3,
+        out_specs=[VM] * 3,
+        scratch_shapes=_half_scratch(rows, half, 384)
+        + [pltpu.VMEM((rows, 384), F32), pltpu.VMEM((TPD * TILE + 8, 384), F32)]
+        + [pltpu.SemaphoreType.DMA],
+        compiler_params=pltpu.CompilerParams(vmem_limit_bytes=48 * MIB),
     )(pos, *toks, w, acc_in, done, *tables)
 
 
@@ -318,12 +323,11 @@
         cand[pl.ds(TILE + j * WIN + SLAB, WIN - SLAB), :] = jnp.zeros((WIN - SLAB, 384), BF16)
 
 
-def _collect(p, pos_ref, slot, neighbour, first, full_ref, near_ref, far_ref, cand, side):
+def _collect(p, pos_ref, slot, neighbour, first, full_ref, near_ref, far_ref, cand):
     block, blocks = pos_ref[3], pos_ref[6]
-    cols = slice(side * 384, side * 384 + 384)
     tile = _tile_at(slot, block, p)
     own = pl.multiple_of(p * TILE, TILE)
-    cand[pl.ds(0, TILE), :] = full_ref[pl.ds(own, TILE), cols]
+    cand[pl.ds(0, TILE), :] = full_ref[pl.ds(own, TILE), :]
     up = 1 - 2 * pos_ref[2]
     near_block = (block + up + blocks) % blocks
     far_block = (block - up + blocks) % blocks
@@ -353,7 +357,7 @@
 
         @pl.when(jnp.logical_not(away))
         def _(c0=c0, begin=begin):
-            cand[pl.ds(c0, WIN), :] = full_ref[pl.ds(pl.multiple_of(begin, 16), WIN), cols]
+            cand[pl.ds(c0, WIN), :] = full_ref[pl.ds(pl.multiple_of(begin, 16), WIN), :]
 
         places.append(c0 + jnp.where(away, 0, s - al))
         seen_near = seen_near + is_near.astype(jnp.int32)
@@ -373,7 +377,7 @@
             _clear_rest(cand)
 
         tile, places = _collect(
-            p, pos_ref, slot, neighbour, first, full_ref, near_ref, far_ref, cand, 0
+            p, pos_ref, slot, neighbour, first, full_ref, near_ref, far_ref, cand
         )
         col = lax.broadcasted_iota(jnp.int32, (8, CAND), 1)
         lows = jnp.where(col < TILE, 0, TILE)
@@ -426,7 +430,7 @@
         def _():
             _clear_rest(cand)
 
-        _collect(p, pos_ref, slot, neighbour, first, full_ref, near_ref, far_ref, cand, 1)
+        _collect(p, pos_ref, slot, neighbour, first, full_ref, near_ref, far_ref, cand)
         for h in range(3):
             cols = slice(h * HD, h * HD + HD)
             mixed = jnp.dot(prob_ref[0, h], cand[:, cols], preferred_element_type=F32)
@@ -526,23 +530,22 @@
     at = ((0, 0), (n, 0), (2 * n, 0), (3 * n, 0), (3 * n, h), (4 * n, 0), (4 * n, h))
     kv1, w_all = project(pos, toks, at, 5 * n, pieces, fs)
     part = project_half((ua_l, ub_l, uo_l), w_all)
-    full, *slabs = project_last(
-        pos,
-        (ua_r, ub_r, uo_r),
-        w_all,
-        part,
+    last = (
         kv1,
         ((0, 0), (0, -1), (0, 1), (0, 2), (1, 0)),
         ((1, -1), (1, 1), (1, 2)),
         tables[:3],
     )
-    near_k, near_v, far_k, far_v = slabs
+    rest = (ua_r, ub_r, uo_r)
+    keys, near_k, far_k = project_last(0, pos, rest, w_all, part, *last)
+    part = lax.optimization_barrier((part, far_k))[0]
     far_k = send(far_k, far=1)
     near_k = send(near_k, dc=1)
+    values, near_v, far_v = project_last(1, pos, rest, w_all, part, *last)
     far_v = send(far_v, far=1)
     near_v = send(near_v, dc=1)
-    prob, total = weigh(pos, queries, full, near_k, far_k, tables)
-    return mix(pos, prob, total, full, near_v, far_v, tables[:3])
+    prob, total = weigh(pos, queries, keys, near_k, far_k, tables)
+    return mix(pos, prob, total, values, near_v, far_v, tables[:3])
 
 
 def solution(mesh):

time: 178 us -> 172 us (0.966)
  waiting for transfers between devices: 76.5 us -> 69.7 us
  Pallas kernels: 36.7 us -> 40.1 us
  local copies, waits for them, and re-layouts: 9.64 us -> 6.41 us
    ppermute x33, waiting for transfers between devices: 76.5 us -> 69.7 us  [send(): lax.ppermute(a, AXES, _far_moves() if 'far' in step else _moves(**step))]
    pallas_call x1 -> x2, Pallas kernels: 6.02 us -> 9.3 us  [project_last(): pl.pallas_call(body, out_shape=[jax.ShapeDtypeStruct((TPD * TILE, 384), B...]
    unnamed x66 -> x64, local copies, waits for them, and re-layouts: 7.61 us -> 4.38 us
  transfers between devices with their start and end apart: 33 -> 33, of which waited for: 11 -> 12; matrix products, arithmetic and copies ran while one was open for 1% -> 1% of each run, Pallas kernels for 15% -> 18%
where the time goes in v2:
time: 172 us; the launch traced here: 171 us
  waiting for transfers between devices  69.7 us (41%)
  starting transfers between devices  54.9 us (32%)
  Pallas kernels  40.1 us (23%)
  local copies, waits for them, and re-layouts  6.41 us (4%)
    ppermute x33, waiting for transfers between devices, send(): lax.ppermute(a, AXES, _far_moves() if 'far' in step else _moves(**step))  69.7 us
    ppermute x33, starting transfers between devices, send(): lax.ppermute(a, AXES, _far_moves() if 'far' in step else _moves(**step))  54.9 us
    pallas_call x1, Pallas kernels, project(): pl.pallas_call(body, out_shape=[jax.ShapeDtypeStruct((rows, 768), BF16),...  12.8 us
    pallas_call x2, Pallas kernels, project_last(): pl.pallas_call(body, out_shape=[jax.ShapeDtypeStruct((TPD * TILE, 384), B...  9.3 us
    pallas_call x1, Pallas kernels, weigh(): pl.pallas_call(body, grid=(TPD,), out_shape=[jax.ShapeDtypeStruct((TPD, 3...  6.99 us
    pallas_call x1, Pallas kernels, project_half(): pl.pallas_call(body, out_shape=jax.ShapeDtypeStruct((rows, 768), F32), in...  5.45 us
    unnamed x64, local copies, waits for them, and re-layouts  4.38 us
    pallas_call x1, Pallas kernels, mix(): pl.pallas_call(body, grid=(TPD,), out_shape=jax.ShapeDtypeStruct((TPD * T...  4.33 us
  transfers between devices with their start and end apart: 33, of which 12 were waited for; matrix products, arithmetic and copies ran while one was open for 1% of the time, Pallas kernels for 18%

profile of v2, /device:TPU:32, one launch (start us, length us, event | category | flops | bytes accessed | tf_op | source)
XLA Modules:
  0.0 171.5 jit_solution(18150961470104222651)
XLA Ops:
  2.2 3.3 %collective-permute-start.10 = (bf16[320,384]{1,0:T(8,128)(2,1)S(1)}, bf16[320,384]{1,0:T(8,128)(2,1)S(1)}, u32[]{:S(2)}, u32[]{:S(2)}) collective-permute-start(bf16[320,384]{1,0:T(8,128)(2,1)S(1)} %shard_map.100.refs_8_), channel_id=1, source_target_pairs={{0,16},{1,17},{2,18},{3,19},{4,20},{5,21},{6,22},{7,23},{8,56},{9,... | collective-permute-start | bytes 737288 | tf_op jit(solution)/shard_map/ppermute | solution.py:61
  8.7 4.5 %collective-permute-start.11 = (bf16[320,384]{1,0:T(8,128)(2,1)S(1)}, bf16[320,384]{1,0:T(8,128)(2,1)S(1)}, u32[]{:S(2)}, u32[]{:S(2)}) collective-permute-start(bf16[320,384]{1,0:T(8,128)(2,1)S(1)} %collective-permute-done.9.refs_9_), channel_id=1, source_target_pairs={{0,16},{1,17},{2,18},{3,19},{4,20},{5,21},{6,22},{7,23},{8,56},{9,... | collective-permute-start | bytes 737288 | tf_op jit(solution)/shard_map/ppermute | solution.py:61
  17.9 17.3 %collective-permute-start.15 = (bf16[320,384]{1,0:T(8,128)(2,1)S(1)}, bf16[320,384]{1,0:T(8,128)(2,1)S(1)}, u32[]{:S(2)}, u32[]{:S(2)}) collective-permute-start(bf16[320,384]{1,0:T(8,128)(2,1)S(1)} %collective-permute-done.14.refs_12_), channel_id=1, source_target_pairs={{0,8},{1,9},{2,10},{3,11},{4,12},{5,13},{6,14},{7,15},{8,0},{9,1},... | collective-permute-start | bytes 737288 | tf_op jit(solution)/shard_map/ppermute | solution.py:61
  35.2 1.9 %collective-permute-start.3 = (bf16[128,5120]{1,0:T(8,128)(2,1)S(1)}, bf16[128,5120]{1,0:T(8,128)(2,1)S(1)}, u32[]{:S(2)}, u32[]{:S(2)}) collective-permute-start(bf16[128,5120]{1,0:T(8,128)(2,1)S(1)} %copy-done.14), channel_id=1, source_target_pairs={{0,3},{1,0},{2,1},{3,2},{4,7},{5,4},{6,5},{7,6},{8,11},{9,8},{10,9... | collective-permute-start | bytes 3932168 | tf_op jit(solution)/shard_map/ppermute | solution.py:61
  37.1 6.0 %collective-permute-start.8 = (bf16[128,2560]{1,0:T(8,128)(2,1)S(1)}, bf16[128,2560]{1,0:T(8,128)(2,1)}, u32[]{:S(2)}, u32[]{:S(2)}) collective-permute-start(bf16[128,2560]{1,0:T(8,128)(2,1)S(1)} %get-tuple-element.27), channel_id=1, source_target_pairs={{0,4},{1,5},{2,6},{3,7},{4,0},{5,1},{6,2},{7,3},{8,12},{9,13},{10,... | collective-permute-start | bytes 1966088 | tf_op jit(solution)/shard_map/ppermute | solution.py:61
  44.2 1.6 collective-permute-start.20
  46.4 9.8 %collective-permute-done.8.refs_6_ = bf16[128,2560]{1,0:T(8,128)(2,1)} collective-permute-done((bf16[128,2560]{1,0:T(8,128)(2,1)S(1)}, bf16[128,2560]{1,0:T(8,128)(2,1)}, u32[]{:S(2)}, u32[]{:S(2)}) %collective-permute-start.8) | collective-permute-done | bytes 655392 | tf_op jit(solution)/shard_map/ppermute | solution.py:61
  59.3 5.9 %collective-permute-done.3.refs_3_ = bf16[128,5120]{1,0:T(8,128)(2,1)S(1)} collective-permute-done((bf16[128,5120]{1,0:T(8,128)(2,1)S(1)}, bf16[128,5120]{1,0:T(8,128)(2,1)S(1)}, u32[]{:S(2)}, u32[]{:S(2)}) %collective-permute-start.3) | collective-permute-done | bytes 1310752 | tf_op jit(solution)/shard_map/ppermute | solution.py:61
  65.2 1.8 %collective-permute-start.19 = (bf16[320,384]{1,0:T(8,128)(2,1)S(1)}, bf16[320,384]{1,0:T(8,128)(2,1)S(1)}, u32[]{:S(2)}, u32[]{:S(2)}) collective-permute-start(bf16[320,384]{1,0:T(8,128)(2,1)S(1)} %collective-permute-done.18.refs_16_), channel_id=1, source_target_pairs={{0,8},{1,9},{2,10},{3,11},{4,12},{5,13},{6,14},{7,15},{8,0},{9,1},... | collective-permute-start | bytes 737288 | tf_op jit(solution)/shard_map/ppermute | solution.py:61
  67.0 12.3 %collective-permute-done.6.refs_2_ = bf16[128,5120]{1,0:T(8,128)(2,1)S(1)} collective-permute-done((bf16[128,5120]{1,0:T(8,128)(2,1)S(1)}, bf16[128,5120]{1,0:T(8,128)(2,1)S(1)}, u32[]{:S(2)}, u32[]{:S(2)}) %collective-permute-start.6) | collective-permute-done | bytes 1310752 | tf_op jit(solution)/shard_map/ppermute | solution.py:61
  80.3 13.1 %collective-permute-done.26.t0 = bf16[128,2560]{1,0:T(8,128)(2,1)S(1)} collective-permute-done((bf16[128,2560]{1,0:T(8,128)(2,1)}, bf16[128,2560]{1,0:T(8,128)(2,1)S(1)}, u32[]{:S(2)}, u32[]{:S(2)}) %collective-permute-start.26) | collective-permute-done | bytes 655392 | tf_op jit(solution)/shard_map/ppermute | solution.py:61
  93.5 13.0 %collective-permute-done.7.refs_4_ = bf16[128,2560]{1,0:T(8,128)(2,1)} collective-permute-done((bf16[128,2560]{1,0:T(8,128)(2,1)S(1)}, bf16[128,2560]{1,0:T(8,128)(2,1)}, u32[]{:S(2)}, u32[]{:S(2)}) %collective-permute-start.7) | collective-permute-done | bytes 655392 | tf_op jit(solution)/shard_map/ppermute | solution.py:61
  106.5 4.6 %collective-permute-done.4.refs_5_ = bf16[128,2560]{1,0:T(8,128)(2,1)} collective-permute-done((bf16[128,2560]{1,0:T(8,128)(2,1)S(1)}, bf16[128,2560]{1,0:T(8,128)(2,1)}, u32[]{:S(2)}, u32[]{:S(2)}) %collective-permute-start.4) | collective-permute-done | bytes 655392 | tf_op jit(solution)/shard_map/ppermute | solution.py:61
  111.1 3.3 %collective-permute-start.2 = (bf16[128,2560]{1,0:T(8,128)(2,1)}, bf16[128,2560]{1,0:T(8,128)(2,1)S(1)}, u32[]{:S(2)}, u32[]{:S(2)}) collective-permute-start(bf16[128,2560]{1,0:T(8,128)(2,1)} %collective-permute-done.refs_7_), channel_id=1, source_target_pairs={{0,3},{1,0},{2,1},{3,2},{4,7},{5,4},{6,5},{7,6},{8,11},{9,8},{10,9... | collective-permute-start | bytes 1966088 | tf_op jit(solution)/shard_map/ppermute | solution.py:61
  115.9 12.8 %shard_map.102 = (bf16[640,768]{1,0:T(8,128)(2,1)}, bf16[5120,768]{1,0:T(8,128)(2,1)}) custom-call(s32[7]{0:T(128)} %stack.27.refs_0_.pos_ref, bf16[128,5120]{1,0:T(8,128)(2,1)} %refs_1_.3, bf16[128,5120]{1,0:T(8,128)(2,1)} %copy-done.16, bf16[128,5120]{1,0:T(8,128)(2,1)} %copy-done.15, bf16[128,2560]{1,0:T(8,128)(2,1)} %collective-permute-done.7.refs_4_, ...), custom_call_target="tpu_custom_call" | custom-call | tf_op jit(solution)/shard_map/pallas_call | solution.py:156
  128.7 5.5 %shard_map.103.acc_ref = f32[384,768]{1,0:T(8,128)} custom-call(bf16[128,2560]{1,0:T(8,128)(2,1)} %copy-done.24, bf16[128,2560]{1,0:T(8,128)(2,1)} %collective-permute-done.27.t1, bf16[128,2560]{1,0:T(8,128)(2,1)} %collective-permute-done.28.t2, bf16[5120,768]{1,0:T(8,128)(2,1)} %get-tuple-element.16.w_ref), custom_call_target="tpu_custom_call" | custom-call | tf_op jit(solution)/shard_map/pallas_call | solution.py:226
  134.2 1.9 %collective-permute-done.2.t1 = bf16[128,2560]{1,0:T(8,128)(2,1)S(1)} collective-permute-done((bf16[128,2560]{1,0:T(8,128)(2,1)}, bf16[128,2560]{1,0:T(8,128)(2,1)S(1)}, u32[]{:S(2)}, u32[]{:S(2)}) %collective-permute-start.2) | collective-permute-done | bytes 655392 | tf_op jit(solution)/shard_map/ppermute | solution.py:61
  137.7 4.6 %shard_map.104 = (bf16[1024,384]{1,0:T(8,128)(2,1)S(1)}, bf16[512,384]{1,0:T(8,128)(2,1)S(1)}, bf16[512,384]{1,0:T(8,128)(2,1)S(1)}) custom-call(s32[7]{0:T(128)S(1)} %copy-done.9, bf16[128,2560]{1,0:T(8,128)(2,1)S(1)} %collective-permute-done.1.t0, bf16[128,2560]{1,0:T(8,128)(2,1)S(1)} %collective-permute-done.2.t1, ...), custom_call_target="tpu_custom_call" | custom-call | tf_op jit(solution)/shard_map/pallas_call | solution.py:302
  142.5 4.2 %collective-permute-start.30 = (bf16[512,384]{1,0:T(8,128)(2,1)S(1)}, bf16[512,384]{1,0:T(8,128)(2,1)S(1)}, u32[]{:S(2)}, u32[]{:S(2)}) collective-permute-start(bf16[512,384]{1,0:T(8,128)(2,1)S(1)} %get-tuple-element.20), channel_id=1, source_target_pairs={{0,248},{1,249},{2,250},{3,251},{4,252},{5,253},{6,254},{7,255},{8... | collective-permute-start | bytes 1179656 | tf_op jit(solution)/shard_map/ppermute | solution.py:61
  146.7 4.6 %shard_map.106 = (bf16[1024,384]{1,0:T(8,128)(2,1)S(1)}, bf16[512,384]{1,0:T(8,128)(2,1)S(1)}, bf16[512,384]{1,0:T(8,128)(2,1)S(1)}) custom-call(s32[7]{0:T(128)S(1)} %copy-done.9, bf16[128,2560]{1,0:T(8,128)(2,1)S(1)} %collective-permute-done.1.t0, bf16[128,2560]{1,0:T(8,128)(2,1)S(1)} %collective-permute-done.2.t1, ...), custom_call_target="tpu_custom_call" | custom-call | tf_op jit(solution)/shard_map/pallas_call | solution.py:302
  151.4 1.9 %collective-permute-start.32 = (bf16[512,384]{1,0:T(8,128)(2,1)S(1)}, bf16[512,384]{1,0:T(8,128)(2,1)S(1)}, u32[]{:S(2)}, u32[]{:S(2)}) collective-permute-start(bf16[512,384]{1,0:T(8,128)(2,1)S(1)} %get-tuple-element.26), channel_id=1, source_target_pairs={{0,248},{1,249},{2,250},{3,251},{4,252},{5,253},{6,254},{7,255},{8... | collective-permute-start | bytes 1179656 | tf_op jit(solution)/shard_map/ppermute | solution.py:61
  153.4 6.0 %collective-permute-done.30.far_ref = bf16[512,384]{1,0:T(8,128)(2,1)S(1)} collective-permute-done((bf16[512,384]{1,0:T(8,128)(2,1)S(1)}, bf16[512,384]{1,0:T(8,128)(2,1)S(1)}, u32[]{:S(2)}, u32[]{:S(2)}) %collective-permute-start.30) | collective-permute-done | bytes 393248 | tf_op jit(solution)/shard_map/ppermute | solution.py:61
  159.4 7.0 %shard_map.105 = (bf16[4,3,256,768]{3,2,1,0:T(8,128)(2,1)S(1)}, f32[1024,384]{1,0:T(8,128)S(1)}) custom-call(s32[7]{0:T(128)S(1)} %copy-done.9, bf16[1024,384]{1,0:T(8,128)(2,1)S(1)} %copy-done.4, bf16[1024,384]{1,0:T(8,128)(2,1)S(1)} %get-tuple-element.18.full_ref, bf16[512,384]{1,0:T(8,128)(2,1)S(1)} %collective-permute-done.29.near_ref, ...), custom_call_target="tpu_custom_call" | custom-call | tf_op jit(solution)/shard_map/pallas_call | solution.py:407
  167.1 4.3 %shard_map.107 = bf16[1024,384]{1,0:T(8,128)(2,1)} custom-call(s32[7]{0:T(128)S(1)} %copy-done.9, bf16[4,3,256,768]{3,2,1,0:T(8,128)(2,1)S(1)} %get-tuple-element.21.prob_ref, f32[1024,384]{1,0:T(8,128)S(1)} %get-tuple-element.22.total_ref, bf16[1024,384]{1,0:T(8,128)(2,1)S(1)} %get-tuple-element.24.full_ref, ...), custom_call_target="tpu_custom_call" | custom-call | tf_op jit(solution)/shard_map/pallas_call | solution.py:439
  (118 shorter events, 19.7 us)
Async XLA Ops:
  7.0 39.5 %collective-permute-start = (bf16[128,2560]{1,0:T(8,128)(2,1)S(1)}, bf16[128,2560]{1,0:T(8,128)(2,1)}, u32[]{:S(2)}, u32[]{:S(2)}) collective-permute-start(bf16[128,2560]{1,0:T(8,128)(2,1)S(1)} %get-tuple-element.28), channel_id=1, source_target_pairs={{0,4},{1,5},{2,6},{3,7},{4,0},{5,1},{6,2},{7,3},{8,12},{9,13},{10,... | collective-permute-start | bytes 1966088 | tf_op jit(solution)/shard_map/ppermute | solution.py:61
  14.5 20.7 %collective-permute-start.12 = (bf16[320,384]{1,0:T(8,128)(2,1)S(1)}, bf16[320,384]{1,0:T(8,128)(2,1)S(1)}, u32[]{:S(2)}, u32[]{:S(2)}) collective-permute-start(bf16[320,384]{1,0:T(8,128)(2,1)S(1)} %collective-permute-done.10.refs_0_), channel_id=1, source_target_pairs={{0,16},{1,17},{2,18},{3,19},{4,20},{5,21},{6,22},{7,23},{8,56},{9,... | collective-permute-start | bytes 737288 | tf_op jit(solution)/shard_map/ppermute | solution.py:61
  14.9 22.3 %collective-permute-start.16 = (bf16[320,384]{1,0:T(8,128)(2,1)S(1)}, bf16[320,384]{1,0:T(8,128)(2,1)S(1)}, u32[]{:S(2)}, u32[]{:S(2)}) collective-permute-start(bf16[320,384]{1,0:T(8,128)(2,1)S(1)} %collective-permute-done.9.refs_9_), channel_id=1, source_target_pairs={{0,64},{1,65},{2,66},{3,67},{4,68},{5,69},{6,70},{7,71},{8,200},{9... | collective-permute-start | bytes 737288 | tf_op jit(solution)/shard_map/ppermute | solution.py:61
  16.4 27.8 %collective-permute-start.18 = (bf16[320,384]{1,0:T(8,128)(2,1)S(1)}, bf16[320,384]{1,0:T(8,128)(2,1)S(1)}, u32[]{:S(2)}, u32[]{:S(2)}) collective-permute-start(bf16[320,384]{1,0:T(8,128)(2,1)S(1)} %collective-permute-done.14.refs_12_), channel_id=1, source_target_pairs={{0,64},{1,65},{2,66},{3,67},{4,68},{5,69},{6,70},{7,71},{8,200},{9... | collective-permute-start | bytes 737288 | tf_op jit(solution)/shard_map/ppermute | solution.py:61
  17.9 27.9 %collective-permute-start.15 = (bf16[320,384]{1,0:T(8,128)(2,1)S(1)}, bf16[320,384]{1,0:T(8,128)(2,1)S(1)}, u32[]{:S(2)}, u32[]{:S(2)}) collective-permute-start(bf16[320,384]{1,0:T(8,128)(2,1)S(1)} %collective-permute-done.14.refs_12_), channel_id=1, source_target_pairs={{0,8},{1,9},{2,10},{3,11},{4,12},{5,13},{6,14},{7,15},{8,0},{9,1},... | collective-permute-start | bytes 737288 | tf_op jit(solution)/shard_map/ppermute | solution.py:61
  35.2 30.0 %collective-permute-start.3 = (bf16[128,5120]{1,0:T(8,128)(2,1)S(1)}, bf16[128,5120]{1,0:T(8,128)(2,1)S(1)}, u32[]{:S(2)}, u32[]{:S(2)}) collective-permute-start(bf16[128,5120]{1,0:T(8,128)(2,1)S(1)} %copy-done.14), channel_id=1, source_target_pairs={{0,3},{1,0},{2,1},{3,2},{4,7},{5,4},{6,5},{7,6},{8,11},{9,8},{10,9... | collective-permute-start | bytes 3932168 | tf_op jit(solution)/shard_map/ppermute | solution.py:61
  37.1 19.1 %collective-permute-start.8 = (bf16[128,2560]{1,0:T(8,128)(2,1)S(1)}, bf16[128,2560]{1,0:T(8,128)(2,1)}, u32[]{:S(2)}, u32[]{:S(2)}) collective-permute-start(bf16[128,2560]{1,0:T(8,128)(2,1)S(1)} %get-tuple-element.27), channel_id=1, source_target_pairs={{0,4},{1,5},{2,6},{3,7},{4,0},{5,1},{6,2},{7,3},{8,12},{9,13},{10,... | collective-permute-start | bytes 1966088 | tf_op jit(solution)/shard_map/ppermute | solution.py:61
  46.4 32.9 %collective-permute-start.6 = (bf16[128,5120]{1,0:T(8,128)(2,1)S(1)}, bf16[128,5120]{1,0:T(8,128)(2,1)S(1)}, u32[]{:S(2)}, u32[]{:S(2)}) collective-permute-start(bf16[128,5120]{1,0:T(8,128)(2,1)S(1)} %copy-done.14), channel_id=1, source_target_pairs={{0,1},{1,2},{2,3},{3,0},{4,5},{5,6},{6,7},{7,4},{8,9},{9,10},{10,1... | collective-permute-start | bytes 3932168 | tf_op jit(solution)/shard_map/ppermute | solution.py:61
  56.9 22.4 %collective-permute-start.24 = (bf16[960,384]{1,0:T(8,128)(2,1)S(1)}, bf16[960,384]{1,0:T(8,128)(2,1)S(1)}, u32[]{:S(2)}, u32[]{:S(2)}) collective-permute-start(bf16[960,384]{1,0:T(8,128)(2,1)S(1)} %collective-permute-done.20.refs_18_), channel_id=1, source_target_pairs={{0,64},{1,65},{2,66},{3,67},{4,68},{5,69},{6,70},{7,71},{8,200},{9... | collective-permute-start | bytes 2211848 | tf_op jit(solution)/shard_map/ppermute | solution.py:61
  57.8 22.1 %collective-permute-start.22 = (bf16[960,384]{1,0:T(8,128)(2,1)S(1)}, bf16[960,384]{1,0:T(8,128)(2,1)S(1)}, u32[]{:S(2)}, u32[]{:S(2)}) collective-permute-start(bf16[960,384]{1,0:T(8,128)(2,1)S(1)} %collective-permute-done.13.refs_11_), channel_id=1, source_target_pairs={{0,64},{1,65},{2,66},{3,67},{4,68},{5,69},{6,70},{7,71},{8,200},{9... | collective-permute-start | bytes 2211848 | tf_op jit(solution)/shard_map/ppermute | solution.py:61
  59.3 34.0 %collective-permute-start.26 = (bf16[128,2560]{1,0:T(8,128)(2,1)}, bf16[128,2560]{1,0:T(8,128)(2,1)S(1)}, u32[]{:S(2)}, u32[]{:S(2)}) collective-permute-start(bf16[128,2560]{1,0:T(8,128)(2,1)} %collective-permute-done.8.refs_6_), channel_id=1, source_target_pairs={{0,1},{1,2},{2,3},{3,0},{4,5},{5,6},{6,7},{7,4},{8,9},{9,10},{10,1... | collective-permute-start | bytes 1966088 | tf_op jit(solution)/shard_map/ppermute | solution.py:61
  65.2 15.0 %collective-permute-start.19 = (bf16[320,384]{1,0:T(8,128)(2,1)S(1)}, bf16[320,384]{1,0:T(8,128)(2,1)S(1)}, u32[]{:S(2)}, u32[]{:S(2)}) collective-permute-start(bf16[320,384]{1,0:T(8,128)(2,1)S(1)} %collective-permute-done.18.refs_16_), channel_id=1, source_target_pairs={{0,8},{1,9},{2,10},{3,11},{4,12},{5,13},{6,14},{7,15},{8,0},{9,1},... | collective-permute-start | bytes 737288 | tf_op jit(solution)/shard_map/ppermute | solution.py:61
  79.3 31.7 %collective-permute-start.25 = (bf16[960,384]{1,0:T(8,128)(2,1)S(1)}, bf16[960,384]{1,0:T(8,128)(2,1)S(1)}, u32[]{:S(2)}, u32[]{:S(2)}) collective-permute-start(bf16[960,384]{1,0:T(8,128)(2,1)S(1)} %collective-permute-done.24.refs_22_), channel_id=1, source_target_pairs={{0,8},{1,9},{2,10},{3,11},{4,12},{5,13},{6,14},{7,15},{8,0},{9,1},... | collective-permute-start | bytes 2211848 | tf_op jit(solution)/shard_map/ppermute | solution.py:61
  79.9 34.5 %collective-permute-start.23 = (bf16[960,384]{1,0:T(8,128)(2,1)S(1)}, bf16[960,384]{1,0:T(8,128)(2,1)S(1)}, u32[]{:S(2)}, u32[]{:S(2)}) collective-permute-start(bf16[960,384]{1,0:T(8,128)(2,1)S(1)} %collective-permute-done.22.refs_20_), channel_id=1, source_target_pairs={{0,8},{1,9},{2,10},{3,11},{4,12},{5,13},{6,14},{7,15},{8,0},{9,1},... | collective-permute-start | bytes 2211848 | tf_op jit(solution)/shard_map/ppermute | solution.py:61
  80.2 26.2 %collective-permute-start.7 = (bf16[128,2560]{1,0:T(8,128)(2,1)S(1)}, bf16[128,2560]{1,0:T(8,128)(2,1)}, u32[]{:S(2)}, u32[]{:S(2)}) collective-permute-start(bf16[128,2560]{1,0:T(8,128)(2,1)S(1)} %slice.17), channel_id=1, source_target_pairs={{0,1},{1,2},{2,3},{3,0},{4,5},{5,6},{6,7},{7,4},{8,9},{9,10},{10,1... | collective-permute-start | bytes 1966088 | tf_op jit(solution)/shard_map/ppermute | solution.py:61
  93.3 17.7 %collective-permute-start.4 = (bf16[128,2560]{1,0:T(8,128)(2,1)S(1)}, bf16[128,2560]{1,0:T(8,128)(2,1)}, u32[]{:S(2)}, u32[]{:S(2)}) collective-permute-start(bf16[128,2560]{1,0:T(8,128)(2,1)S(1)} %slice.16), channel_id=1, source_target_pairs={{0,3},{1,0},{2,1},{3,2},{4,7},{5,4},{6,5},{7,6},{8,11},{9,8},{10,9... | collective-permute-start | bytes 1966088 | tf_op jit(solution)/shard_map/ppermute | solution.py:61
  93.4 35.3 %collective-permute-start.27 = (bf16[128,2560]{1,0:T(8,128)(2,1)}, bf16[128,2560]{1,0:T(8,128)(2,1)}, u32[]{:S(2)}, u32[]{:S(2)}) collective-permute-start(bf16[128,2560]{1,0:T(8,128)(2,1)} %collective-permute-done.8.refs_6_), channel_id=1, source_target_pairs={{0,3},{1,0},{2,1},{3,2},{4,7},{5,4},{6,5},{7,6},{8,11},{9,8},{10,9... | collective-permute-start | bytes 1966088 | tf_op jit(solution)/shard_map/ppermute | solution.py:61
  106.4 22.2 %collective-permute-start.28 = (bf16[128,2560]{1,0:T(8,128)(2,1)}, bf16[128,2560]{1,0:T(8,128)(2,1)}, u32[]{:S(2)}, u32[]{:S(2)}) collective-permute-start(bf16[128,2560]{1,0:T(8,128)(2,1)} %collective-permute-done.7.refs_4_), channel_id=1, source_target_pairs={{0,4},{1,5},{2,6},{3,7},{4,0},{5,1},{6,2},{7,3},{8,12},{9,13},{10,... | collective-permute-start | bytes 1966088 | tf_op jit(solution)/shard_map/ppermute | solution.py:61
  111.1 23.1 %collective-permute-start.1 = (bf16[128,2560]{1,0:T(8,128)(2,1)}, bf16[128,2560]{1,0:T(8,128)(2,1)S(1)}, u32[]{:S(2)}, u32[]{:S(2)}) collective-permute-start(bf16[128,2560]{1,0:T(8,128)(2,1)} %collective-permute-done.refs_7_), channel_id=1, source_target_pairs={{0,1},{1,2},{2,3},{3,0},{4,5},{5,6},{6,7},{7,4},{8,9},{9,10},{10,1... | collective-permute-start | bytes 1966088 | tf_op jit(solution)/shard_map/ppermute | solution.py:61
  111.1 25.0 %collective-permute-start.2 = (bf16[128,2560]{1,0:T(8,128)(2,1)}, bf16[128,2560]{1,0:T(8,128)(2,1)S(1)}, u32[]{:S(2)}, u32[]{:S(2)}) collective-permute-start(bf16[128,2560]{1,0:T(8,128)(2,1)} %collective-permute-done.refs_7_), channel_id=1, source_target_pairs={{0,3},{1,0},{2,1},{3,2},{4,7},{5,4},{6,5},{7,6},{8,11},{9,8},{10,9... | collective-permute-start | bytes 1966088 | tf_op jit(solution)/shard_map/ppermute | solution.py:61
  114.4 22.0 %collective-permute-start.5 = (bf16[128,2560]{1,0:T(8,128)(2,1)}, bf16[128,2560]{1,0:T(8,128)(2,1)S(1)}, u32[]{:S(2)}, u32[]{:S(2)}) collective-permute-start(bf16[128,2560]{1,0:T(8,128)(2,1)} %collective-permute-done.4.refs_5_), channel_id=1, source_target_pairs={{0,4},{1,5},{2,6},{3,7},{4,0},{5,1},{6,2},{7,3},{8,12},{9,13},{10,... | collective-permute-start | bytes 1966088 | tf_op jit(solution)/shard_map/ppermute | solution.py:61
  142.5 16.9 %collective-permute-start.30 = (bf16[512,384]{1,0:T(8,128)(2,1)S(1)}, bf16[512,384]{1,0:T(8,128)(2,1)S(1)}, u32[]{:S(2)}, u32[]{:S(2)}) collective-permute-start(bf16[512,384]{1,0:T(8,128)(2,1)S(1)} %get-tuple-element.20), channel_id=1, source_target_pairs={{0,248},{1,249},{2,250},{3,251},{4,252},{5,253},{6,254},{7,255},{8... | collective-permute-start | bytes 1179656 | tf_op jit(solution)/shard_map/ppermute | solution.py:61
  151.3 15.1 %collective-permute-start.31 = (bf16[512,384]{1,0:T(8,128)(2,1)S(1)}, bf16[512,384]{1,0:T(8,128)(2,1)S(1)}, u32[]{:S(2)}, u32[]{:S(2)}) collective-permute-start(bf16[512,384]{1,0:T(8,128)(2,1)S(1)} %get-tuple-element.25), channel_id=1, source_target_pairs={{0,8},{1,9},{2,10},{3,11},{4,12},{5,13},{6,14},{7,15},{8,0},{9,1},... | collective-permute-start | bytes 1179656 | tf_op jit(solution)/shard_map/ppermute | solution.py:61
  151.4 15.7 %collective-permute-start.32 = (bf16[512,384]{1,0:T(8,128)(2,1)S(1)}, bf16[512,384]{1,0:T(8,128)(2,1)S(1)}, u32[]{:S(2)}, u32[]{:S(2)}) collective-permute-start(bf16[512,384]{1,0:T(8,128)(2,1)S(1)} %get-tuple-element.26), channel_id=1, source_target_pairs={{0,248},{1,249},{2,250},{3,251},{4,252},{5,253},{6,254},{7,255},{8... | collective-permute-start | bytes 1179656 | tf_op jit(solution)/shard_map/ppermute | solution.py:61
  (41 other events, 754.7 us)

commit v3 on v2

--- a/solution.py
+++ b/solution.py
@@ -110,66 +110,73 @@
         piece_refs = refs[1 + nt : 1 + nt + np_]
         out, w_out, t_buf, w_buf, acc, t_sem, w_sem, o_sem = refs[1 + nt + np_ :]
         x, zh, c = pos_ref[0], pos_ref[1], pos_ref[2]
-        waits = []
-        for ref, (_, xrel, signed, flip, plan) in zip(piece_refs, pieces):
-            core = (c + flip) % NC
-            sign = 2 * core - 1
-            xs = (x + (sign * xrel if signed else xrel) + NX) % NX
-            for i, (zrel, zsigned, other) in enumerate(plan):
-                zs = (zh + (sign * zrel if zsigned else zrel) + NZH) % NZH
-                place = pl.multiple_of(((xs * NZH + zs) * NC + (core + other) % NC) * fs, 32)
-                for kv in range(2):
-                    cp = pltpu.make_async_copy(
-                        ref.at[pl.ds((2 * i + kv) * fs, fs), :],
-                        w_buf.at[pl.ds(place, fs), pl.ds(kv * 384, 384)],
-                        w_sem.at[len(waits)],
-                    )
-                    cp.start()
-                    waits.append(cp)
-        for i, (ref, (r0, c0)) in enumerate(zip(tok_refs, tok_at)):
-            cp = pltpu.make_async_copy(
-                ref,
-                t_buf.at[pl.ds(r0, ref.shape[0]), pl.ds(c0, ref.shape[1])],
-                t_sem.at[i],
-            )
-            cp.start()
-            waits.append(cp)
-        for cp in waits:
-            cp.wait()
-        back = pltpu.make_async_copy(w_buf, w_out, o_sem)
-        back.start()
+        steps = (0, 2 * c - 1, 1 - 2 * c, 2)
+        at = [(x + step + NX) % NX for step in steps]
+        waits = [[] for _ in steps]
+        count = 0
+        for group in range(NX):
+            for ref, (_, xrel, signed, flip, plan) in zip(piece_refs, pieces):
+                if (1 + flip if signed else xrel // 2 * 3) != group:
+                    continue
+                core = (c + flip) % NC
+                sign = 2 * core - 1
+                for i, (zrel, zsigned, other) in enumerate(plan):
+                    zs = (zh + (sign * zrel if zsigned else zrel) + NZH) % NZH
+                    place = pl.multiple_of((zs * NC + (core + other) % NC) * fs, 32)
+                    for kv in range(2):
+                        cp = pltpu.make_async_copy(
+                            ref.at[pl.ds((2 * i + kv) * fs, fs), :],
+                            w_buf.at[at[group], pl.ds(place, fs), pl.ds(kv * 384, 384)],
+                            w_sem.at[count],
+                        )
+                        cp.start()
+                        waits[group].append(cp)
+                        count += 1
+            if group == 0:
+                for i, (ref, (r0, c0)) in enumerate(zip(tok_refs, tok_at)):
+                    for k in range(ref.shape[1] // quarter):
+                        cp = pltpu.make_async_copy(
+                            ref.at[:, pl.ds(k * quarter, quarter)],
+                            t_buf.at[c0 // quarter + k, pl.ds(r0, ref.shape[0]), :],
+                            t_sem.at[i, k],
+                        )
+                        cp.start()
+                        waits[0].append(cp)
+        backs = []
         for q in range(NX):
-            part = jnp.dot(
-                t_buf[:, q * quarter : (q + 1) * quarter],
-                w_buf[q * quarter : (q + 1) * quarter, :],
-                preferred_element_type=F32,
-            )
+            for cp in waits[q]:
+                cp.wait()
+            back = pltpu.make_async_copy(w_buf.at[at[q]], w_out.at[at[q]], o_sem.at[q])
+            back.start()
+            backs.append(back)
+            part = jnp.dot(t_buf[at[q]], w_buf[at[q]], preferred_element_type=F32)
             if q == 0:
                 acc[...] = part
             elif q < NX - 1:
                 acc[...] += part
             else:
                 out[...] = (acc[...] + part).astype(BF16)
-        back.wait()
+        for back in backs:
+            back.wait()
 
     n_copies = 2 * sum(len(p[4]) for p in pieces)
     return pl.pallas_call(
         body,
         out_shape=[
             jax.ShapeDtypeStruct((rows, 768), BF16),
-            jax.ShapeDtypeStruct((features, 768), BF16),
+            jax.ShapeDtypeStruct((NX, quarter, 768), BF16),
         ],
         in_specs=[SM] + [HBM] * (nt + np_),
         out_specs=[VM, ANY],
         scratch_shapes=[
-            pltpu.VMEM((rows, features), BF16),
-            pltpu.VMEM((features, 768), BF16),
+            pltpu.VMEM((NX, rows, quarter), BF16),
+            pltpu.VMEM((NX, quarter, 768), BF16),
             pltpu.VMEM((rows, 768), F32),
-            pltpu.SemaphoreType.DMA((nt,)),
+            pltpu.SemaphoreType.DMA((nt, NX)),
             pltpu.SemaphoreType.DMA((n_copies,)),
-            pltpu.SemaphoreType.DMA,
+            pltpu.SemaphoreType.DMA((NX,)),
         ],
-        compiler_params=pltpu.CompilerParams(vmem_limit_bytes=60 * MIB),
+        compiler_params=pltpu.CompilerParams(vmem_limit_bytes=36 * MIB),
     )(pos, *toks, *[p[0] for p in pieces])
 
 
@@ -229,7 +236,7 @@
         in_specs=[ANY] * 4,
         out_specs=VM,
         scratch_shapes=_half_scratch(rows, half, 768),
-        compiler_params=pltpu.CompilerParams(vmem_limit_bytes=57 * MIB),
+        compiler_params=pltpu.CompilerParams(vmem_limit_bytes=48 * MIB),
     )(*toks, w)
 
 
@@ -492,6 +499,7 @@
     xw1 = send(w, sx=1)
     xc1 = send(wc, sx=1)
     z2 = send(z1w, sz=1)
+    xw1, pos = lax.optimization_barrier((xw1, pos))
     xw2 = send(xw1, sx=1)
     tl, tr = tokens[:, :h], tokens[:, h:]
     z_l = send(tl, dzl=1)
@@ -529,6 +537,7 @@
     toks = (tokens, ya, yb, yo_l, yo_r, z_l, z_r)
     at = ((0, 0), (n, 0), (2 * n, 0), (3 * n, 0), (3 * n, h), (4 * n, 0), (4 * n, h))
     kv1, w_all = project(pos, toks, at, 5 * n, pieces, fs)
+    w_all = w_all.reshape(tokens.shape[1], 768)
     part = project_half((ua_l, ub_l, uo_l), w_all)
     last = (
         kv1,

time: 172 us -> 171 us (level)
  waiting for transfers between devices: 69.7 us -> 73.1 us
  Pallas kernels: 40.1 us -> 37.1 us
  local copies, waits for them, and re-layouts: 6.41 us -> 4.45 us
    ppermute x33, waiting for transfers between devices: 69.7 us -> 73.1 us  [send(): lax.ppermute(a, AXES, _far_moves() if 'far' in step else _moves(**step))]
    unnamed x64 -> x20, local copies, waits for them, and re-layouts: 4.38 us -> 1.85 us
  transfers between devices with their start and end apart: 33 -> 33, of which waited for: 12 -> 10; matrix products, arithmetic and copies ran while one was open for 1% -> 2% of each run, Pallas kernels for 18% -> 16%
where the time goes in v3:
time: 171 us; the launch traced here: 170 us
  waiting for transfers between devices  73.1 us (43%)
  starting transfers between devices  55 us (32%)
  Pallas kernels  37.1 us (22%)
  local copies, waits for them, and re-layouts  4.45 us (3%)
    ppermute x33, waiting for transfers between devices, send(): lax.ppermute(a, AXES, _far_moves() if 'far' in step else _moves(**step))  73.1 us
    ppermute x33, starting transfers between devices, send(): lax.ppermute(a, AXES, _far_moves() if 'far' in step else _moves(**step))  55 us
    pallas_call x1, Pallas kernels, project(): pl.pallas_call(body, out_shape=[jax.ShapeDtypeStruct((rows, 768), BF16),...  11.4 us
    pallas_call x2, Pallas kernels, project_last(): pl.pallas_call(body, out_shape=[jax.ShapeDtypeStruct((TPD * TILE, 384), B...  9.3 us
    pallas_call x1, Pallas kernels, weigh(): pl.pallas_call(body, grid=(TPD,), out_shape=[jax.ShapeDtypeStruct((TPD, 3...  6.98 us
    pallas_call x1, Pallas kernels, mix(): pl.pallas_call(body, grid=(TPD,), out_shape=jax.ShapeDtypeStruct((TPD * T...  4.33 us
    pallas_call x1, Pallas kernels, project_half(): pl.pallas_call(body, out_shape=jax.ShapeDtypeStruct((rows, 768), F32), in...  3.85 us
  transfers between devices with their start and end apart: 33, of which 10 were waited for; matrix products, arithmetic and copies ran while one was open for 2% of the time, Pallas kernels for 16%

profile of v3, /device:TPU:32, one launch (start us, length us, event | category | flops | bytes accessed | tf_op | source)
XLA Modules:
  0.0 169.9 jit_solution(16305025762097076878)
XLA Ops:
  4.5 3.3 %collective-permute-start.11 = (bf16[320,384]{1,0:T(8,128)(2,1)S(1)}, bf16[320,384]{1,0:T(8,128)(2,1)S(1)}, u32[]{:S(2)}, u32[]{:S(2)}) collective-permute-start(bf16[320,384]{1,0:T(8,128)(2,1)S(1)} %shard_map.100.refs_8_), channel_id=1, source_target_pairs={{0,16},{1,17},{2,18},{3,19},{4,20},{5,21},{6,22},{7,23},{8,56},{9,... | collective-permute-start | bytes 737288 | tf_op jit(solution)/shard_map/ppermute | solution.py:61
  7.8 2.4 %fusion = (bf16[128,2560]{1,0:T(8,128)(2,1)}, bf16[128,2560]{1,0:T(8,128)(2,1)}) fusion(bf16[128,5120]{1,0:T(8,128)(2,1)} %refs_1_.3), kind=kLoop, calls=%fused_computation | loop fusion | bytes 2621440 | tf_op jit(solution)/shard_map/slice | solution.py:504
  11.1 4.5 %collective-permute-start.12 = (bf16[320,384]{1,0:T(8,128)(2,1)S(1)}, bf16[320,384]{1,0:T(8,128)(2,1)S(1)}, u32[]{:S(2)}, u32[]{:S(2)}) collective-permute-start(bf16[320,384]{1,0:T(8,128)(2,1)S(1)} %collective-permute-done.10.refs_9_), channel_id=1, source_target_pairs={{0,16},{1,17},{2,18},{3,19},{4,20},{5,21},{6,22},{7,23},{8,56},{9,... | collective-permute-start | bytes 737288 | tf_op jit(solution)/shard_map/ppermute | solution.py:61
  17.1 3.1 %collective-permute-start.15 = (bf16[320,384]{1,0:T(8,128)(2,1)S(1)}, bf16[320,384]{1,0:T(8,128)(2,1)S(1)}, u32[]{:S(2)}, u32[]{:S(2)}) collective-permute-start(bf16[320,384]{1,0:T(8,128)(2,1)S(1)} %collective-permute-done.refs_12_), channel_id=1, source_target_pairs={{0,8},{1,9},{2,10},{3,11},{4,12},{5,13},{6,14},{7,15},{8,0},{9,1},... | collective-permute-start | bytes 737288 | tf_op jit(solution)/shard_map/ppermute | solution.py:61
  20.2 6.4 %collective-permute-start.16 = (bf16[320,384]{1,0:T(8,128)(2,1)S(1)}, bf16[320,384]{1,0:T(8,128)(2,1)S(1)}, u32[]{:S(2)}, u32[]{:S(2)}) collective-permute-start(bf16[320,384]{1,0:T(8,128)(2,1)S(1)} %collective-permute-done.10.refs_9_), channel_id=1, source_target_pairs={{0,64},{1,65},{2,66},{3,67},{4,68},{5,69},{6,70},{7,71},{8,200},{9... | collective-permute-start | bytes 737288 | tf_op jit(solution)/shard_map/ppermute | solution.py:61
  26.7 3.0 %collective-permute-start.4 = (bf16[128,5120]{1,0:T(8,128)(2,1)S(1)}, bf16[128,5120]{1,0:T(8,128)(2,1)S(1)}, u32[]{:S(2)}, u32[]{:S(2)}) collective-permute-start(bf16[128,5120]{1,0:T(8,128)(2,1)S(1)} %copy-done), channel_id=1, source_target_pairs={{0,3},{1,0},{2,1},{3,2},{4,7},{5,4},{6,5},{7,6},{8,11},{9,8},{10,9... | collective-permute-start | bytes 3932168 | tf_op jit(solution)/shard_map/ppermute | solution.py:61
  29.7 13.5 %collective-permute-start.9 = (bf16[128,2560]{1,0:T(8,128)(2,1)}, bf16[128,2560]{1,0:T(8,128)(2,1)S(1)}, u32[]{:S(2)}, u32[]{:S(2)}) collective-permute-start(bf16[128,2560]{1,0:T(8,128)(2,1)} %get-tuple-element.31), channel_id=1, source_target_pairs={{0,4},{1,5},{2,6},{3,7},{4,0},{5,1},{6,2},{7,3},{8,12},{9,13},{10,... | collective-permute-start | bytes 1966088 | tf_op jit(solution)/shard_map/ppermute | solution.py:61
  46.2 9.4 %collective-permute-done.9.refs_6_ = bf16[128,2560]{1,0:T(8,128)(2,1)S(1)} collective-permute-done((bf16[128,2560]{1,0:T(8,128)(2,1)}, bf16[128,2560]{1,0:T(8,128)(2,1)S(1)}, u32[]{:S(2)}, u32[]{:S(2)}) %collective-permute-start.9) | collective-permute-done | bytes 655392 | tf_op jit(solution)/shard_map/ppermute | solution.py:61
  59.6 18.2 %collective-permute-done.7.refs_2_ = bf16[128,5120]{1,0:T(8,128)(2,1)S(1)} collective-permute-done((bf16[128,5120]{1,0:T(8,128)(2,1)S(1)}, bf16[128,5120]{1,0:T(8,128)(2,1)S(1)}, u32[]{:S(2)}, u32[]{:S(2)}) %collective-permute-start.7) | collective-permute-done | bytes 1310752 | tf_op jit(solution)/shard_map/ppermute | solution.py:61
  78.8 13.0 %collective-permute-done.26.t0 = bf16[128,2560]{1,0:T(8,128)(2,1)S(1)} collective-permute-done((bf16[128,2560]{1,0:T(8,128)(2,1)S(1)}, bf16[128,2560]{1,0:T(8,128)(2,1)S(1)}, u32[]{:S(2)}, u32[]{:S(2)}) %collective-permute-start.26) | collective-permute-done | bytes 655392 | tf_op jit(solution)/shard_map/ppermute | solution.py:61
  94.0 11.3 %collective-permute-done.8.refs_4_ = bf16[128,2560]{1,0:T(8,128)(2,1)S(1)} collective-permute-done((bf16[128,2560]{1,0:T(8,128)(2,1)S(1)}, bf16[128,2560]{1,0:T(8,128)(2,1)S(1)}, u32[]{:S(2)}, u32[]{:S(2)}) %collective-permute-start.8) | collective-permute-done | bytes 655392 | tf_op jit(solution)/shard_map/ppermute | solution.py:61
  105.4 4.1 %collective-permute-done.5.refs_5_ = bf16[128,2560]{1,0:T(8,128)(2,1)S(1)} collective-permute-done((bf16[128,2560]{1,0:T(8,128)(2,1)S(1)}, bf16[128,2560]{1,0:T(8,128)(2,1)S(1)}, u32[]{:S(2)}, u32[]{:S(2)}) %collective-permute-start.5) | collective-permute-done | bytes 655392 | tf_op jit(solution)/shard_map/ppermute | solution.py:61
  109.5 3.2 %collective-permute-start.3 = (bf16[128,2560]{1,0:T(8,128)(2,1)S(1)}, bf16[128,2560]{1,0:T(8,128)(2,1)S(1)}, u32[]{:S(2)}, u32[]{:S(2)}) collective-permute-start(bf16[128,2560]{1,0:T(8,128)(2,1)S(1)} %collective-permute-done.1.refs_7_), channel_id=1, source_target_pairs={{0,3},{1,0},{2,1},{3,2},{4,7},{5,4},{6,5},{7,6},{8,11},{9,8},{10,9... | collective-permute-start | bytes 1966088 | tf_op jit(solution)/shard_map/ppermute | solution.py:61
  112.8 11.4 %shard_map.102 = (bf16[640,768]{1,0:T(8,128)(2,1)S(1)}, bf16[4,1280,768]{2,1,0:T(8,128)(2,1)}) custom-call(s32[7]{0:T(128)S(1)} %stack.27.refs_0_.pos_ref, bf16[128,5120]{1,0:T(8,128)(2,1)S(1)} %copy-done, bf16[128,5120]{1,0:T(8,128)(2,1)S(1)} %collective-permute-done.7.refs_2_, bf16[128,5120]{1,0:T(8,128)(2,1)S(1)} %collective-permute-done.4.refs_3_, ...), custom_call_target="tpu_custom_call" | custom-call | tf_op jit(solution)/shard_map/pallas_call | solution.py:163
  124.2 3.9 %shard_map.103.acc_ref = f32[384,768]{1,0:T(8,128)S(1)} custom-call(bf16[128,2560]{1,0:T(8,128)(2,1)S(1)} %collective-permute-done.26.t0, bf16[128,2560]{1,0:T(8,128)(2,1)S(1)} %collective-permute-done.27.t1, bf16[128,2560]{1,0:T(8,128)(2,1)S(1)} %collective-permute-done.28.t2, bf16[5120,768]{1,0:T(8,128)(2,1)} %bitcast.28), custom_call_target="tpu_custom_call" | custom-call | tf_op jit(solution)/shard_map/pallas_call | solution.py:233
  128.1 7.6 %collective-permute-done.3.t1 = bf16[128,2560]{1,0:T(8,128)(2,1)S(1)} collective-permute-done((bf16[128,2560]{1,0:T(8,128)(2,1)S(1)}, bf16[128,2560]{1,0:T(8,128)(2,1)S(1)}, u32[]{:S(2)}, u32[]{:S(2)}) %collective-permute-start.3) | collective-permute-done | bytes 655392 | tf_op jit(solution)/shard_map/ppermute | solution.py:61
  135.7 4.7 %shard_map.104 = (bf16[1024,384]{1,0:T(8,128)(2,1)S(1)}, bf16[512,384]{1,0:T(8,128)(2,1)S(1)}, bf16[512,384]{1,0:T(8,128)(2,1)S(1)}) custom-call(s32[7]{0:T(128)S(1)} %stack.27.refs_0_.pos_ref, bf16[128,2560]{1,0:T(8,128)(2,1)S(1)} %collective-permute-done.2.t0, bf16[128,2560]{1,0:T(8,128)(2,1)S(1)} %collective-permute-done.3.t1, ...), custom_call_target="tpu_custom_call" | custom-call | tf_op jit(solution)/shard_map/pallas_call | solution.py:309
  140.5 4.6 %collective-permute-start.30 = (bf16[512,384]{1,0:T(8,128)(2,1)S(1)}, bf16[512,384]{1,0:T(8,128)(2,1)S(1)}, u32[]{:S(2)}, u32[]{:S(2)}) collective-permute-start(bf16[512,384]{1,0:T(8,128)(2,1)S(1)} %get-tuple-element.24), channel_id=1, source_target_pairs={{0,248},{1,249},{2,250},{3,251},{4,252},{5,253},{6,254},{7,255},{8... | collective-permute-start | bytes 1179656 | tf_op jit(solution)/shard_map/ppermute | solution.py:61
  145.1 4.6 %shard_map.106 = (bf16[1024,384]{1,0:T(8,128)(2,1)S(1)}, bf16[512,384]{1,0:T(8,128)(2,1)S(1)}, bf16[512,384]{1,0:T(8,128)(2,1)S(1)}) custom-call(s32[7]{0:T(128)S(1)} %stack.27.refs_0_.pos_ref, bf16[128,2560]{1,0:T(8,128)(2,1)S(1)} %collective-permute-done.2.t0, bf16[128,2560]{1,0:T(8,128)(2,1)S(1)} %collective-permute-done.3.t1, ...), custom_call_target="tpu_custom_call" | custom-call | tf_op jit(solution)/shard_map/pallas_call | solution.py:309
  149.9 1.7 %collective-permute-start.32 = (bf16[512,384]{1,0:T(8,128)(2,1)S(1)}, bf16[512,384]{1,0:T(8,128)(2,1)S(1)}, u32[]{:S(2)}, u32[]{:S(2)}) collective-permute-start(bf16[512,384]{1,0:T(8,128)(2,1)S(1)} %get-tuple-element.30), channel_id=1, source_target_pairs={{0,248},{1,249},{2,250},{3,251},{4,252},{5,253},{6,254},{7,255},{8... | collective-permute-start | bytes 1179656 | tf_op jit(solution)/shard_map/ppermute | solution.py:61
  151.6 4.4 %collective-permute-done.30.far_ref = bf16[512,384]{1,0:T(8,128)(2,1)S(1)} collective-permute-done((bf16[512,384]{1,0:T(8,128)(2,1)S(1)}, bf16[512,384]{1,0:T(8,128)(2,1)S(1)}, u32[]{:S(2)}, u32[]{:S(2)}) %collective-permute-start.30) | collective-permute-done | bytes 393248 | tf_op jit(solution)/shard_map/ppermute | solution.py:61
  156.0 7.0 %shard_map.105 = (bf16[4,3,256,768]{3,2,1,0:T(8,128)(2,1)S(1)}, f32[1024,384]{1,0:T(8,128)S(1)}) custom-call(s32[7]{0:T(128)S(1)} %stack.27.refs_0_.pos_ref, bf16[1024,384]{1,0:T(8,128)(2,1)S(1)} %copy-done.1, bf16[1024,384]{1,0:T(8,128)(2,1)S(1)} %get-tuple-element.22.full_ref, bf16[512,384]{1,0:T(8,128)(2,1)S(1)} %collective-permute-done.29.near_ref, ...), custom_call_target="tpu_custom_call" | custom-call | tf_op jit(solution)/shard_map/pallas_call | solution.py:414
  163.0 2.6 %collective-permute-done.32.far_ref = bf16[512,384]{1,0:T(8,128)(2,1)S(1)} collective-permute-done((bf16[512,384]{1,0:T(8,128)(2,1)S(1)}, bf16[512,384]{1,0:T(8,128)(2,1)S(1)}, u32[]{:S(2)}, u32[]{:S(2)}) %collective-permute-start.32) | collective-permute-done | bytes 393248 | tf_op jit(solution)/shard_map/ppermute | solution.py:61
  165.6 4.3 %shard_map.107 = bf16[1024,384]{1,0:T(8,128)(2,1)} custom-call(s32[7]{0:T(128)S(1)} %stack.27.refs_0_.pos_ref, bf16[4,3,256,768]{3,2,1,0:T(8,128)(2,1)S(1)} %get-tuple-element.25.prob_ref, f32[1024,384]{1,0:T(8,128)S(1)} %get-tuple-element.26.total_ref, bf16[1024,384]{1,0:T(8,128)(2,1)S(1)} %get-tuple-element.28.full_ref, ...), custom_call_target="tpu_custom_call" | custom-call | tf_op jit(solution)/shard_map/pallas_call | solution.py:446
  (74 shorter events, 17.4 us)
Async XLA Ops:
  10.2 34.7 %collective-permute-start.1 = (bf16[128,2560]{1,0:T(8,128)(2,1)}, bf16[128,2560]{1,0:T(8,128)(2,1)S(1)}, u32[]{:S(2)}, u32[]{:S(2)}) collective-permute-start(bf16[128,2560]{1,0:T(8,128)(2,1)} %get-tuple-element.32), channel_id=1, source_target_pairs={{0,4},{1,5},{2,6},{3,7},{4,0},{5,1},{6,2},{7,3},{8,12},{9,13},{10,... | collective-permute-start | bytes 1966088 | tf_op jit(solution)/shard_map/ppermute | solution.py:61
  11.1 15.5 %collective-permute-start.12 = (bf16[320,384]{1,0:T(8,128)(2,1)S(1)}, bf16[320,384]{1,0:T(8,128)(2,1)S(1)}, u32[]{:S(2)}, u32[]{:S(2)}) collective-permute-start(bf16[320,384]{1,0:T(8,128)(2,1)S(1)} %collective-permute-done.10.refs_9_), channel_id=1, source_target_pairs={{0,16},{1,17},{2,18},{3,19},{4,20},{5,21},{6,22},{7,23},{8,56},{9,... | collective-permute-start | bytes 737288 | tf_op jit(solution)/shard_map/ppermute | solution.py:61
  17.1 27.0 %collective-permute-start.15 = (bf16[320,384]{1,0:T(8,128)(2,1)S(1)}, bf16[320,384]{1,0:T(8,128)(2,1)S(1)}, u32[]{:S(2)}, u32[]{:S(2)}) collective-permute-start(bf16[320,384]{1,0:T(8,128)(2,1)S(1)} %collective-permute-done.refs_12_), channel_id=1, source_target_pairs={{0,8},{1,9},{2,10},{3,11},{4,12},{5,13},{6,14},{7,15},{8,0},{9,1},... | collective-permute-start | bytes 737288 | tf_op jit(solution)/shard_map/ppermute | solution.py:61
  20.2 24.7 %collective-permute-start.16 = (bf16[320,384]{1,0:T(8,128)(2,1)S(1)}, bf16[320,384]{1,0:T(8,128)(2,1)S(1)}, u32[]{:S(2)}, u32[]{:S(2)}) collective-permute-start(bf16[320,384]{1,0:T(8,128)(2,1)S(1)} %collective-permute-done.10.refs_9_), channel_id=1, source_target_pairs={{0,64},{1,65},{2,66},{3,67},{4,68},{5,69},{6,70},{7,71},{8,200},{9... | collective-permute-start | bytes 737288 | tf_op jit(solution)/shard_map/ppermute | solution.py:61
  26.7 32.7 %collective-permute-start.4 = (bf16[128,5120]{1,0:T(8,128)(2,1)S(1)}, bf16[128,5120]{1,0:T(8,128)(2,1)S(1)}, u32[]{:S(2)}, u32[]{:S(2)}) collective-permute-start(bf16[128,5120]{1,0:T(8,128)(2,1)S(1)} %copy-done), channel_id=1, source_target_pairs={{0,3},{1,0},{2,1},{3,2},{4,7},{5,4},{6,5},{7,6},{8,11},{9,8},{10,9... | collective-permute-start | bytes 3932168 | tf_op jit(solution)/shard_map/ppermute | solution.py:61
  29.7 25.9 %collective-permute-start.9 = (bf16[128,2560]{1,0:T(8,128)(2,1)}, bf16[128,2560]{1,0:T(8,128)(2,1)S(1)}, u32[]{:S(2)}, u32[]{:S(2)}) collective-permute-start(bf16[128,2560]{1,0:T(8,128)(2,1)} %get-tuple-element.31), channel_id=1, source_target_pairs={{0,4},{1,5},{2,6},{3,7},{4,0},{5,1},{6,2},{7,3},{8,12},{9,13},{10,... | collective-permute-start | bytes 1966088 | tf_op jit(solution)/shard_map/ppermute | solution.py:61
  44.9 32.9 %collective-permute-start.7 = (bf16[128,5120]{1,0:T(8,128)(2,1)S(1)}, bf16[128,5120]{1,0:T(8,128)(2,1)S(1)}, u32[]{:S(2)}, u32[]{:S(2)}) collective-permute-start(bf16[128,5120]{1,0:T(8,128)(2,1)S(1)} %copy-done), channel_id=1, source_target_pairs={{0,1},{1,2},{2,3},{3,0},{4,5},{5,6},{6,7},{7,4},{8,9},{9,10},{10,1... | collective-permute-start | bytes 3932168 | tf_op jit(solution)/shard_map/ppermute | solution.py:61
  56.9 21.0 %collective-permute-start.24 = (bf16[960,384]{1,0:T(8,128)(2,1)S(1)}, bf16[960,384]{1,0:T(8,128)(2,1)S(1)}, u32[]{:S(2)}, u32[]{:S(2)}) collective-permute-start(bf16[960,384]{1,0:T(8,128)(2,1)S(1)} %collective-permute-done.20.refs_18_), channel_id=1, source_target_pairs={{0,64},{1,65},{2,66},{3,67},{4,68},{5,69},{6,70},{7,71},{8,200},{9... | collective-permute-start | bytes 2211848 | tf_op jit(solution)/shard_map/ppermute | solution.py:61
  56.9 21.5 %collective-permute-start.22 = (bf16[960,384]{1,0:T(8,128)(2,1)S(1)}, bf16[960,384]{1,0:T(8,128)(2,1)S(1)}, u32[]{:S(2)}, u32[]{:S(2)}) collective-permute-start(bf16[960,384]{1,0:T(8,128)(2,1)S(1)} %collective-permute-done.14.refs_11_), channel_id=1, source_target_pairs={{0,64},{1,65},{2,66},{3,67},{4,68},{5,69},{6,70},{7,71},{8,200},{9... | collective-permute-start | bytes 2211848 | tf_op jit(solution)/shard_map/ppermute | solution.py:61
  58.0 33.9 %collective-permute-start.26 = (bf16[128,2560]{1,0:T(8,128)(2,1)S(1)}, bf16[128,2560]{1,0:T(8,128)(2,1)S(1)}, u32[]{:S(2)}, u32[]{:S(2)}) collective-permute-start(bf16[128,2560]{1,0:T(8,128)(2,1)S(1)} %collective-permute-done.9.refs_6_), channel_id=1, source_target_pairs={{0,1},{1,2},{2,3},{3,0},{4,5},{5,6},{6,7},{7,4},{8,9},{9,10},{10,1... | collective-permute-start | bytes 1966088 | tf_op jit(solution)/shard_map/ppermute | solution.py:61
  59.4 19.2 %collective-permute-start.17 = (bf16[320,384]{1,0:T(8,128)(2,1)S(1)}, bf16[320,384]{1,0:T(8,128)(2,1)S(1)}, u32[]{:S(2)}, u32[]{:S(2)}) collective-permute-start(bf16[320,384]{1,0:T(8,128)(2,1)S(1)} %collective-permute-done.16.refs_14_), channel_id=1, source_target_pairs={{0,8},{1,9},{2,10},{3,11},{4,12},{5,13},{6,14},{7,15},{8,0},{9,1},... | collective-permute-start | bytes 737288 | tf_op jit(solution)/shard_map/ppermute | solution.py:61
  77.8 15.5 %collective-permute-start.21 = (bf16[960,384]{1,0:T(8,128)(2,1)S(1)}, bf16[960,384]{1,0:T(8,128)(2,1)S(1)}, u32[]{:S(2)}, u32[]{:S(2)}) collective-permute-start(bf16[960,384]{1,0:T(8,128)(2,1)S(1)} %collective-permute-done.20.refs_18_), channel_id=1, source_target_pairs={{0,8},{1,9},{2,10},{3,11},{4,12},{5,13},{6,14},{7,15},{8,0},{9,1},... | collective-permute-start | bytes 2211848 | tf_op jit(solution)/shard_map/ppermute | solution.py:61
  77.8 31.6 %collective-permute-start.25 = (bf16[960,384]{1,0:T(8,128)(2,1)S(1)}, bf16[960,384]{1,0:T(8,128)(2,1)S(1)}, u32[]{:S(2)}, u32[]{:S(2)}) collective-permute-start(bf16[960,384]{1,0:T(8,128)(2,1)S(1)} %collective-permute-done.24.refs_22_), channel_id=1, source_target_pairs={{0,8},{1,9},{2,10},{3,11},{4,12},{5,13},{6,14},{7,15},{8,0},{9,1},... | collective-permute-start | bytes 2211848 | tf_op jit(solution)/shard_map/ppermute | solution.py:61
  78.4 34.4 %collective-permute-start.23 = (bf16[960,384]{1,0:T(8,128)(2,1)S(1)}, bf16[960,384]{1,0:T(8,128)(2,1)S(1)}, u32[]{:S(2)}, u32[]{:S(2)}) collective-permute-start(bf16[960,384]{1,0:T(8,128)(2,1)S(1)} %collective-permute-done.22.refs_20_), channel_id=1, source_target_pairs={{0,8},{1,9},{2,10},{3,11},{4,12},{5,13},{6,14},{7,15},{8,0},{9,1},... | collective-permute-start | bytes 2211848 | tf_op jit(solution)/shard_map/ppermute | solution.py:61
  78.6 26.8 %collective-permute-start.8 = (bf16[128,2560]{1,0:T(8,128)(2,1)S(1)}, bf16[128,2560]{1,0:T(8,128)(2,1)S(1)}, u32[]{:S(2)}, u32[]{:S(2)}) collective-permute-start(bf16[128,2560]{1,0:T(8,128)(2,1)S(1)} %slice.17), channel_id=1, source_target_pairs={{0,1},{1,2},{2,3},{3,0},{4,5},{5,6},{6,7},{7,4},{8,9},{9,10},{10,1... | collective-permute-start | bytes 1966088 | tf_op jit(solution)/shard_map/ppermute | solution.py:61
  91.9 17.6 %collective-permute-start.5 = (bf16[128,2560]{1,0:T(8,128)(2,1)S(1)}, bf16[128,2560]{1,0:T(8,128)(2,1)S(1)}, u32[]{:S(2)}, u32[]{:S(2)}) collective-permute-start(bf16[128,2560]{1,0:T(8,128)(2,1)S(1)} %slice.16), channel_id=1, source_target_pairs={{0,3},{1,0},{2,1},{3,2},{4,7},{5,4},{6,5},{7,6},{8,11},{9,8},{10,9... | collective-permute-start | bytes 1966088 | tf_op jit(solution)/shard_map/ppermute | solution.py:61
  93.3 30.9 %collective-permute-start.27 = (bf16[128,2560]{1,0:T(8,128)(2,1)S(1)}, bf16[128,2560]{1,0:T(8,128)(2,1)S(1)}, u32[]{:S(2)}, u32[]{:S(2)}) collective-permute-start(bf16[128,2560]{1,0:T(8,128)(2,1)S(1)} %collective-permute-done.9.refs_6_), channel_id=1, source_target_pairs={{0,3},{1,0},{2,1},{3,2},{4,7},{5,4},{6,5},{7,6},{8,11},{9,8},{10,9... | collective-permute-start | bytes 1966088 | tf_op jit(solution)/shard_map/ppermute | solution.py:61
  105.4 18.8 %collective-permute-start.28 = (bf16[128,2560]{1,0:T(8,128)(2,1)S(1)}, bf16[128,2560]{1,0:T(8,128)(2,1)S(1)}, u32[]{:S(2)}, u32[]{:S(2)}) collective-permute-start(bf16[128,2560]{1,0:T(8,128)(2,1)S(1)} %collective-permute-done.8.refs_4_), channel_id=1, source_target_pairs={{0,4},{1,5},{2,6},{3,7},{4,0},{5,1},{6,2},{7,3},{8,12},{9,13},{10,... | collective-permute-start | bytes 1966088 | tf_op jit(solution)/shard_map/ppermute | solution.py:61
  109.5 18.6 %collective-permute-start.2 = (bf16[128,2560]{1,0:T(8,128)(2,1)S(1)}, bf16[128,2560]{1,0:T(8,128)(2,1)S(1)}, u32[]{:S(2)}, u32[]{:S(2)}) collective-permute-start(bf16[128,2560]{1,0:T(8,128)(2,1)S(1)} %collective-permute-done.1.refs_7_), channel_id=1, source_target_pairs={{0,1},{1,2},{2,3},{3,0},{4,5},{5,6},{6,7},{7,4},{8,9},{9,10},{10,1... | collective-permute-start | bytes 1966088 | tf_op jit(solution)/shard_map/ppermute | solution.py:61
  109.5 26.2 %collective-permute-start.3 = (bf16[128,2560]{1,0:T(8,128)(2,1)S(1)}, bf16[128,2560]{1,0:T(8,128)(2,1)S(1)}, u32[]{:S(2)}, u32[]{:S(2)}) collective-permute-start(bf16[128,2560]{1,0:T(8,128)(2,1)S(1)} %collective-permute-done.1.refs_7_), channel_id=1, source_target_pairs={{0,3},{1,0},{2,1},{3,2},{4,7},{5,4},{6,5},{7,6},{8,11},{9,8},{10,9... | collective-permute-start | bytes 1966088 | tf_op jit(solution)/shard_map/ppermute | solution.py:61
  112.7 22.9 %collective-permute-start.6 = (bf16[128,2560]{1,0:T(8,128)(2,1)S(1)}, bf16[128,2560]{1,0:T(8,128)(2,1)S(1)}, u32[]{:S(2)}, u32[]{:S(2)}) collective-permute-start(bf16[128,2560]{1,0:T(8,128)(2,1)S(1)} %collective-permute-done.5.refs_5_), channel_id=1, source_target_pairs={{0,4},{1,5},{2,6},{3,7},{4,0},{5,1},{6,2},{7,3},{8,12},{9,13},{10,... | collective-permute-start | bytes 1966088 | tf_op jit(solution)/shard_map/ppermute | solution.py:61
  140.5 15.5 %collective-permute-start.30 = (bf16[512,384]{1,0:T(8,128)(2,1)S(1)}, bf16[512,384]{1,0:T(8,128)(2,1)S(1)}, u32[]{:S(2)}, u32[]{:S(2)}) collective-permute-start(bf16[512,384]{1,0:T(8,128)(2,1)S(1)} %get-tuple-element.24), channel_id=1, source_target_pairs={{0,248},{1,249},{2,250},{3,251},{4,252},{5,253},{6,254},{7,255},{8... | collective-permute-start | bytes 1179656 | tf_op jit(solution)/shard_map/ppermute | solution.py:61
  149.8 13.2 %collective-permute-start.31 = (bf16[512,384]{1,0:T(8,128)(2,1)S(1)}, bf16[512,384]{1,0:T(8,128)(2,1)S(1)}, u32[]{:S(2)}, u32[]{:S(2)}) collective-permute-start(bf16[512,384]{1,0:T(8,128)(2,1)S(1)} %get-tuple-element.29), channel_id=1, source_target_pairs={{0,8},{1,9},{2,10},{3,11},{4,12},{5,13},{6,14},{7,15},{8,0},{9,1},... | collective-permute-start | bytes 1179656 | tf_op jit(solution)/shard_map/ppermute | solution.py:61
  149.9 15.7 %collective-permute-start.32 = (bf16[512,384]{1,0:T(8,128)(2,1)S(1)}, bf16[512,384]{1,0:T(8,128)(2,1)S(1)}, u32[]{:S(2)}, u32[]{:S(2)}) collective-permute-start(bf16[512,384]{1,0:T(8,128)(2,1)S(1)} %get-tuple-element.30), channel_id=1, source_target_pairs={{0,248},{1,249},{2,250},{3,251},{4,252},{5,253},{6,254},{7,255},{8... | collective-permute-start | bytes 1179656 | tf_op jit(solution)/shard_map/ppermute | solution.py:61
  (19 other events, 212.1 us)

commit v4 on v3

--- a/solution.py
+++ b/solution.py
@@ -180,44 +180,45 @@
     )(pos, *toks, *[p[0] for p in pieces])
 
 
+CHUNKS = 4
+
+
 def _half_product(toks, w, row0, cols, t_buf, w_buf, t_sem, w_sem):
     n = toks[0].shape[0]
-    half = toks[0].shape[1]
-    step = half // 2
-    waits = []
-    for i, ref in enumerate(toks):
-        waits.append(pltpu.make_async_copy(ref, t_buf.at[pl.ds(i * n, n), :], t_sem.at[i]))
-    loads = [
-        pltpu.make_async_copy(
-            w.at[pl.ds(row0 + i * step, step), pl.ds(*cols)],
-            w_buf.at[pl.ds(i * step, step), :],
-            w_sem.at[i],
+    step = toks[0].shape[1] // CHUNKS
+
+    def copies(k):
+        at = k * step if isinstance(k, int) else pl.multiple_of(k * step, 128)
+        yield pltpu.make_async_copy(
+            w.at[pl.ds(row0 + at, step), pl.ds(*cols)], w_buf.at[k], w_sem.at[k]
         )
-        for i in range(2)
-    ]
-    for cp in loads[:1] + waits + loads[1:]:
-        cp.start()
+        for i, ref in enumerate(toks):
+            yield pltpu.make_async_copy(
+                ref.at[:, pl.ds(at, step)], t_buf.at[k, pl.ds(i * n, n), :], t_sem.at[k, i]
+            )
+
+    for k in range(CHUNKS):
+        for cp in copies(k):
+            cp.start()
 
     def product(acc):
-        for cp in waits:
-            cp.wait()
-        for i in range(2):
-            loads[i].wait()
-            acc[...] += jnp.dot(
-                t_buf[:, i * step : (i + 1) * step],
-                w_buf[i * step : (i + 1) * step, :],
-                preferred_element_type=F32,
-            )
+        def one(k, carry):
+            for cp in copies(k):
+                cp.wait()
+            acc[...] += jnp.dot(t_buf[k], w_buf[k], preferred_element_type=F32)
+            return carry
+
+        lax.fori_loop(0, CHUNKS, one, 0)
 
     return product
 
 
-def _half_scratch(rows, half, width):
+def _half_scratch(rows, half, width, ntok):
     return [
-        pltpu.VMEM((rows, half), BF16),
-        pltpu.VMEM((half, width), BF16),
-        pltpu.SemaphoreType.DMA((3,)),
-        pltpu.SemaphoreType.DMA((2,)),
+        pltpu.VMEM((CHUNKS, rows, half // CHUNKS), BF16),
+        pltpu.VMEM((CHUNKS, half // CHUNKS, width), BF16),
+        pltpu.SemaphoreType.DMA((CHUNKS, ntok)),
+        pltpu.SemaphoreType.DMA((CHUNKS,)),
     ]
 
 
@@ -235,9 +236,32 @@
         out_shape=jax.ShapeDtypeStruct((rows, 768), F32),
         in_specs=[ANY] * 4,
         out_specs=VM,
-        scratch_shapes=_half_scratch(rows, half, 768),
+        scratch_shapes=_half_scratch(rows, half, 768, 3),
         compiler_params=pltpu.CompilerParams(vmem_limit_bytes=48 * MIB),
     )(*toks, w)
+
+
+def project_rest(toks, w, acc_in):
+    rows = sum(t.shape[0] for t in toks)
+    half = toks[0].shape[1]
+
+    def body(t0, t1, w_ref, acc_ref, out, t_buf, w_buf, t_sem, w_sem, acc, a_sem):
+        begin = pltpu.make_async_copy(acc_ref.at[pl.ds(0, rows), :], acc, a_sem)
+        begin.start()
+        product = _half_product((t0, t1), w_ref, half, (0, 768), t_buf, w_buf, t_sem, w_sem)
+        begin.wait()
+        product(acc)
+        out[...] = acc[...].astype(BF16)
+
+    return pl.pallas_call(
+        body,
+        out_shape=jax.ShapeDtypeStruct((rows, 768), BF16),
+        in_specs=[ANY] * 4,
+        out_specs=VM,
+        scratch_shapes=_half_scratch(rows, half, 768, 2)
+        + [pltpu.VMEM((rows, 768), F32), pltpu.SemaphoreType.DMA],
+        compiler_params=pltpu.CompilerParams(vmem_limit_bytes=48 * MIB),
+    )(*toks, w, acc_in)
 
 
 def _tile_at(slot_ref, block, p):
@@ -251,33 +275,32 @@
     return jnp.minimum(start // 16 * 16, TILE - WIN)
 
 
-def project_last(side, pos, toks, w, acc_in, done, done_places, places, tables):
-    rows = sum(t.shape[0] for t in toks)
-    half = toks[0].shape[1]
-    n = toks[0].shape[0]
-
-    def body(pos_ref, t0, t1, t2, w_ref, acc_ref, done_ref, slot, neighbour, first,
+def project_last(side, pos, tok, w, acc_in, done, done_places, place, tables):
+    n, half = tok.shape
+    row0 = acc_in.shape[0] - n
+
+    def body(pos_ref, t0, w_ref, acc_ref, done_a, done_b, slot, neighbour, first,
              full, near, far, t_buf, w_buf, t_sem, w_sem, acc, wide, a_sem):
         block, zl, y, blocks = pos_ref[3], pos_ref[4], pos_ref[5], pos_ref[6]
         cols = (side * 384, 384)
-        begin = pltpu.make_async_copy(acc_ref.at[:, pl.ds(*cols)], acc, a_sem)
+        begin = pltpu.make_async_copy(acc_ref.at[pl.ds(row0, n), pl.ds(*cols)], acc, a_sem)
         begin.start()
-        product = _half_product((t0, t1, t2), w_ref, half, cols, t_buf, w_buf, t_sem, w_sem)
+        product = _half_product((t0,), w_ref, half, cols, t_buf, w_buf, t_sem, w_sem)
 
         def row_of(place):
             dzl, dy = place
             return pl.multiple_of(((zl + dzl) % NZL * NY + (y + dy + NY) % NY) * n, n)
 
-        for i, place in enumerate(done_places):
-            part = done_ref[i * n : (i + 1) * n, side * 384 : side * 384 + 384]
-            full[pl.ds(row_of(place), n), :] = part
-            wide[pl.ds(row_of(place), n), :] = part.astype(F32)
+        for ref, at in zip((done_a, done_b), done_places):
+            for i, where in enumerate(at):
+                part = ref[i * n : (i + 1) * n, side * 384 : side * 384 + 384]
+                full[pl.ds(row_of(where), n), :] = part
+                wide[pl.ds(row_of(where), n), :] = part.astype(F32)
         begin.wait()
         product(acc)
-        for i, place in enumerate(places):
-            part = acc[i * n : (i + 1) * n, :].astype(BF16)
-            full[pl.ds(row_of(place), n), :] = part
-            wide[pl.ds(row_of(place), n), :] = part.astype(F32)
+        part = acc[...].astype(BF16)
+        full[pl.ds(row_of(place), n), :] = part
+        wide[pl.ds(row_of(place), n), :] = part.astype(F32)
         up = 1 - 2 * pos_ref[2]
         for out, step in ((far, -up), (near, up)):
             target = (block + step + blocks) % blocks
@@ -310,13 +333,13 @@
         body,
         out_shape=[jax.ShapeDtypeStruct((TPD * TILE, 384), BF16)]
         + [jax.ShapeDtypeStruct((HALO, 384), BF16)] * 2,
-        in_specs=[SM] + [ANY] * 5 + [VM] + [SM] * 3,
+        in_specs=[SM] + [ANY] * 3 + [VM] * 2 + [SM] * 3,
         out_specs=[VM] * 3,
-        scratch_shapes=_half_scratch(rows, half, 384)
-        + [pltpu.VMEM((rows, 384), F32), pltpu.VMEM((TPD * TILE + 8, 384), F32)]
+        scratch_shapes=_half_scratch(n, half, 384, 1)
+        + [pltpu.VMEM((n, 384), F32), pltpu.VMEM((TPD * TILE + 8, 384), F32)]
         + [pltpu.SemaphoreType.DMA],
         compiler_params=pltpu.CompilerParams(vmem_limit_bytes=48 * MIB),
-    )(pos, *toks, w, acc_in, done, *tables)
+    )(pos, tok, w, acc_in, *done, *tables)
 
 
 CAND = 768
@@ -393,8 +416,8 @@
             valid = jnp.logical_and(col >= places[j], col < places[j] + length[j, tile])
             lows = jnp.where(valid, low[j, tile], lows)
             highs = jnp.where(valid, high[j, tile], highs)
-        row = lax.broadcasted_iota(jnp.int32, (TILE, CAND), 0)
-        allowed = jnp.logical_and(row >= lows[0:1, :], row < highs[0:1, :])
+        row = lax.broadcasted_iota(jnp.int32, (TILE, CAND - TILE), 0)
+        allowed = jnp.logical_and(row >= lows[0:1, TILE:], row < highs[0:1, TILE:])
         for h in range(3):
             cols = slice(h * HD, h * HD + HD)
             scores = lax.dot_general(
@@ -403,13 +426,19 @@
                 (((1,), (1,)), ((), ())),
                 preferred_element_type=F32,
             ) * scale
-            scores = jnp.where(allowed, scores, -jnp.inf)
-            top = jnp.max(scores, axis=-1, keepdims=True)
-            weights = jnp.exp(scores - top)
+            own = scores[:, :TILE]
+            slabs = jnp.where(allowed, scores[:, TILE:], -jnp.inf)
+            top = jnp.maximum(
+                jnp.max(own, axis=-1, keepdims=True), jnp.max(slabs, axis=-1, keepdims=True)
+            )
+            own = jnp.exp(own - top)
+            slabs = jnp.exp(slabs - top)
             total[:, cols] = jnp.broadcast_to(
-                jnp.sum(weights, axis=-1, keepdims=True), (TILE, HD)
+                jnp.sum(own, axis=-1, keepdims=True) + jnp.sum(slabs, axis=-1, keepdims=True),
+                (TILE, HD),
             )
-            prob[0, h] = weights.astype(BF16)
+            prob[0, h, :, :TILE] = own.astype(BF16)
+            prob[0, h, :, TILE:] = slabs.astype(BF16)
 
     return pl.pallas_call(
         body,
@@ -539,18 +568,18 @@
     kv1, w_all = project(pos, toks, at, 5 * n, pieces, fs)
     w_all = w_all.reshape(tokens.shape[1], 768)
     part = project_half((ua_l, ub_l, uo_l), w_all)
+    kv2 = project_rest((ua_r, ub_r), w_all, part)
     last = (
-        kv1,
-        ((0, 0), (0, -1), (0, 1), (0, 2), (1, 0)),
-        ((1, -1), (1, 1), (1, 2)),
+        (kv1, kv2),
+        (((0, 0), (0, -1), (0, 1), (0, 2), (1, 0)), ((1, -1), (1, 1))),
+        (1, 2),
         tables[:3],
     )
-    rest = (ua_r, ub_r, uo_r)
-    keys, near_k, far_k = project_last(0, pos, rest, w_all, part, *last)
+    keys, near_k, far_k = project_last(0, pos, uo_r, w_all, part, *last)
     part = lax.optimization_barrier((part, far_k))[0]
     far_k = send(far_k, far=1)
     near_k = send(near_k, dc=1)
-    values, near_v, far_v = project_last(1, pos, rest, w_all, part, *last)
+    values, near_v, far_v = project_last(1, pos, uo_r, w_all, part, *last)
     far_v = send(far_v, far=1)
     near_v = send(near_v, dc=1)
     prob, total = weigh(pos, queries, keys, near_k, far_k, tables)

time: 171 us -> 176 us (1.029)
  starting transfers between devices: 55 us -> 77.2 us
  waiting for transfers between devices: 73.1 us -> 52.8 us
  Pallas kernels: 37.1 us -> 39.1 us
    ppermute x33, starting transfers between devices: 55 us -> 77.2 us  [send(): lax.ppermute(a, AXES, _far_moves() if 'far' in step else _moves(**step))]
    ppermute x33, waiting for transfers between devices: 73.1 us -> 52.8 us  [send(): lax.ppermute(a, AXES, _far_moves() if 'far' in step else _moves(**step))]
    pallas_call x0 -> x1, Pallas kernels: none -> 3.34 us  [project_rest(): pl.pallas_call(body, out_shape=jax.ShapeDtypeStruct((rows, 768), BF16), i...]
  transfers between devices with their start and end apart: 33 -> 33, of which waited for: 10 -> 10; matrix products, arithmetic and copies ran while one was open for 2% -> 1% of each run, Pallas kernels for 16% -> 18%
where the time goes in v4:
time: 176 us; the launch traced here: 174 us
  starting transfers between devices  77.2 us (44%)
  waiting for transfers between devices  52.8 us (30%)
  Pallas kernels  39.1 us (22%)
  local copies, waits for them, and re-layouts  4.43 us (3%)
    ppermute x33, starting transfers between devices, send(): lax.ppermute(a, AXES, _far_moves() if 'far' in step else _moves(**step))  77.2 us
    ppermute x33, waiting for transfers between devices, send(): lax.ppermute(a, AXES, _far_moves() if 'far' in step else _moves(**step))  52.8 us
    pallas_call x1, Pallas kernels, project(): pl.pallas_call(body, out_shape=[jax.ShapeDtypeStruct((rows, 768), BF16),...  11.3 us
    pallas_call x2, Pallas kernels, project_last(): pl.pallas_call(body, out_shape=[jax.ShapeDtypeStruct((TPD * TILE, 384), B...  8.06 us
    pallas_call x1, Pallas kernels, weigh(): pl.pallas_call(body, grid=(TPD,), out_shape=[jax.ShapeDtypeStruct((TPD, 3...  6.26 us
    pallas_call x1, Pallas kernels, mix(): pl.pallas_call(body, grid=(TPD,), out_shape=jax.ShapeDtypeStruct((TPD * T...  4.32 us
    pallas_call x1, Pallas kernels, project_half(): pl.pallas_call(body, out_shape=jax.ShapeDtypeStruct((rows, 768), F32), in...  3.9 us
  transfers between devices with their start and end apart: 33, of which 10 were waited for; matrix products, arithmetic and copies ran while one was open for 1% of the time, Pallas kernels for 18%

profile of v4, /device:TPU:32, one launch (start us, length us, event | category | flops | bytes accessed | tf_op | source)
XLA Modules:
  0.0 173.7 jit_solution(2948421270468052619)
XLA Ops:
  3.8 3.3 %collective-permute-start.9 = (bf16[320,384]{1,0:T(8,128)(2,1)S(1)}, bf16[320,384]{1,0:T(8,128)(2,1)S(1)}, u32[]{:S(2)}, u32[]{:S(2)}) collective-permute-start(bf16[320,384]{1,0:T(8,128)(2,1)S(1)} %shard_map.100.refs_8_), channel_id=1, source_target_pairs={{0,16},{1,17},{2,18},{3,19},{4,20},{5,21},{6,22},{7,23},{8,56},{9,... | collective-permute-start | bytes 737288 | tf_op jit(solution)/shard_map/ppermute | solution.py:61
  7.1 3.6 %collective-permute-start.10 = (bf16[320,384]{1,0:T(8,128)(2,1)}, bf16[320,384]{1,0:T(8,128)(2,1)S(1)}, u32[]{:S(2)}, u32[]{:S(2)}) collective-permute-start(bf16[320,384]{1,0:T(8,128)(2,1)} %collective-permute-done.8.refs_9_), channel_id=1, source_target_pairs={{0,16},{1,17},{2,18},{3,19},{4,20},{5,21},{6,22},{7,23},{8,56},{9,... | collective-permute-start | bytes 737288 | tf_op jit(solution)/shard_map/ppermute | solution.py:61
  14.1 3.2 %collective-permute-done.9.refs_0_ = bf16[320,384]{1,0:T(8,128)(2,1)S(1)} collective-permute-done((bf16[320,384]{1,0:T(8,128)(2,1)S(1)}, bf16[320,384]{1,0:T(8,128)(2,1)S(1)}, u32[]{:S(2)}, u32[]{:S(2)}) %collective-permute-start.9) | collective-permute-done | bytes 245792 | tf_op jit(solution)/shard_map/ppermute | solution.py:61
  18.1 2.6 %collective-permute-start.7 = (bf16[128,2560]{1,0:T(8,128)(2,1)}, bf16[128,2560]{1,0:T(8,128)(2,1)S(1)}, u32[]{:S(2)}, u32[]{:S(2)}) collective-permute-start(bf16[128,2560]{1,0:T(8,128)(2,1)} %get-tuple-element.31), channel_id=1, source_target_pairs={{0,4},{1,5},{2,6},{3,7},{4,0},{5,1},{6,2},{7,3},{8,12},{9,13},{10,... | collective-permute-start | bytes 1966088 | tf_op jit(solution)/shard_map/ppermute | solution.py:61
  20.7 4.4 %collective-permute-start.16 = (bf16[320,384]{1,0:T(8,128)(2,1)}, bf16[320,384]{1,0:T(8,128)(2,1)S(1)}, u32[]{:S(2)}, u32[]{:S(2)}) collective-permute-start(bf16[320,384]{1,0:T(8,128)(2,1)} %collective-permute-done.refs_12_), channel_id=1, source_target_pairs={{0,64},{1,65},{2,66},{3,67},{4,68},{5,69},{6,70},{7,71},{8,200},{9... | collective-permute-start | bytes 737288 | tf_op jit(solution)/shard_map/ppermute | solution.py:61
  31.6 15.2 %collective-permute-start.12 = (bf16[960,384]{1,0:T(8,128)(2,1)S(1)}, bf16[960,384]{1,0:T(8,128)(2,1)S(1)}, u32[]{:S(2)}, u32[]{:S(2)}) collective-permute-start(bf16[960,384]{1,0:T(8,128)(2,1)S(1)} %shard_map.101.refs_10_), channel_id=1, source_target_pairs={{0,8},{1,9},{2,10},{3,11},{4,12},{5,13},{6,14},{7,15},{8,0},{9,1},... | collective-permute-start | bytes 2211848 | tf_op jit(solution)/shard_map/ppermute | solution.py:61
  50.0 4.0 %collective-permute-done.7.refs_7_ = bf16[128,2560]{1,0:T(8,128)(2,1)S(1)} collective-permute-done((bf16[128,2560]{1,0:T(8,128)(2,1)}, bf16[128,2560]{1,0:T(8,128)(2,1)S(1)}, u32[]{:S(2)}, u32[]{:S(2)}) %collective-permute-start.7) | collective-permute-done | bytes 655392 | tf_op jit(solution)/shard_map/ppermute | solution.py:61
  59.9 17.3 %collective-permute-done.4.refs_2_ = bf16[128,5120]{1,0:T(8,128)(2,1)S(1)} collective-permute-done((bf16[128,5120]{1,0:T(8,128)(2,1)S(1)}, bf16[128,5120]{1,0:T(8,128)(2,1)S(1)}, u32[]{:S(2)}, u32[]{:S(2)}) %collective-permute-start.4) | collective-permute-done | bytes 1310752 | tf_op jit(solution)/shard_map/ppermute | solution.py:61
  77.2 5.1 %collective-permute-start.19 = (bf16[960,384]{1,0:T(8,128)(2,1)S(1)}, bf16[960,384]{1,0:T(8,128)(2,1)S(1)}, u32[]{:S(2)}, u32[]{:S(2)}) collective-permute-start(bf16[960,384]{1,0:T(8,128)(2,1)S(1)} %collective-permute-done.18.refs_18_), channel_id=1, source_target_pairs={{0,8},{1,9},{2,10},{3,11},{4,12},{5,13},{6,14},{7,15},{8,0},{9,1},... | collective-permute-start | bytes 2211848 | tf_op jit(solution)/shard_map/ppermute | solution.py:61
  83.3 8.0 %collective-permute-done.24.t0 = bf16[128,2560]{1,0:T(8,128)(2,1)S(1)} collective-permute-done((bf16[128,2560]{1,0:T(8,128)(2,1)S(1)}, bf16[128,2560]{1,0:T(8,128)(2,1)S(1)}, u32[]{:S(2)}, u32[]{:S(2)}) %collective-permute-start.24) | collective-permute-done | bytes 655392 | tf_op jit(solution)/shard_map/ppermute | solution.py:61
  93.8 11.4 %collective-permute-done.5.refs_4_ = bf16[128,2560]{1,0:T(8,128)(2,1)S(1)} collective-permute-done((bf16[128,2560]{1,0:T(8,128)(2,1)S(1)}, bf16[128,2560]{1,0:T(8,128)(2,1)S(1)}, u32[]{:S(2)}, u32[]{:S(2)}) %collective-permute-start.5) | collective-permute-done | bytes 655392 | tf_op jit(solution)/shard_map/ppermute | solution.py:61
  105.3 5.6 %collective-permute-start.26 = (bf16[128,2560]{1,0:T(8,128)(2,1)S(1)}, bf16[128,2560]{1,0:T(8,128)(2,1)S(1)}, u32[]{:S(2)}, u32[]{:S(2)}) collective-permute-start(bf16[128,2560]{1,0:T(8,128)(2,1)S(1)} %collective-permute-done.5.refs_4_), channel_id=1, source_target_pairs={{0,4},{1,5},{2,6},{3,7},{4,0},{5,1},{6,2},{7,3},{8,12},{9,13},{10,... | collective-permute-start | bytes 1966088 | tf_op jit(solution)/shard_map/ppermute | solution.py:61
  111.2 2.9 %collective-permute-start.28 = (bf16[128,2560]{1,0:T(8,128)(2,1)S(1)}, bf16[128,2560]{1,0:T(8,128)(2,1)S(1)}, u32[]{:S(2)}, u32[]{:S(2)}) collective-permute-start(bf16[128,2560]{1,0:T(8,128)(2,1)S(1)} %collective-permute-done.7.refs_7_), channel_id=1, source_target_pairs={{0,3},{1,0},{2,1},{3,2},{4,7},{5,4},{6,5},{7,6},{8,11},{9,8},{10,9... | collective-permute-start | bytes 1966088 | tf_op jit(solution)/shard_map/ppermute | solution.py:61
  114.1 7.0 %collective-permute-start.3 = (bf16[128,2560]{1,0:T(8,128)(2,1)S(1)}, bf16[128,2560]{1,0:T(8,128)(2,1)S(1)}, u32[]{:S(2)}, u32[]{:S(2)}) collective-permute-start(bf16[128,2560]{1,0:T(8,128)(2,1)S(1)} %collective-permute-done.2.refs_5_), channel_id=1, source_target_pairs={{0,4},{1,5},{2,6},{3,7},{4,0},{5,1},{6,2},{7,3},{8,12},{9,13},{10,... | collective-permute-start | bytes 1966088 | tf_op jit(solution)/shard_map/ppermute | solution.py:61
  121.2 11.3 %shard_map.102 = (bf16[640,768]{1,0:T(8,128)(2,1)S(1)}, bf16[4,1280,768]{2,1,0:T(8,128)(2,1)}) custom-call(s32[7]{0:T(128)S(1)} %stack.27.refs_0_.pos_ref, bf16[128,5120]{1,0:T(8,128)(2,1)S(1)} %copy-done, bf16[128,5120]{1,0:T(8,128)(2,1)S(1)} %collective-permute-done.4.refs_2_, bf16[128,5120]{1,0:T(8,128)(2,1)S(1)} %collective-permute-done.1.refs_3_, ...), custom_call_target="tpu_custom_call" | custom-call | tf_op jit(solution)/shard_map/pallas_call | solution.py:163
  132.5 3.9 %shard_map.103.acc_ref = f32[384,768]{1,0:T(8,128)S(1)} custom-call(bf16[128,2560]{1,0:T(8,128)(2,1)S(1)} %collective-permute-done.24.t0, bf16[128,2560]{1,0:T(8,128)(2,1)S(1)} %collective-permute-done.25.t1, bf16[128,2560]{1,0:T(8,128)(2,1)S(1)} %collective-permute-done.26.t2, bf16[5120,768]{1,0:T(8,128)(2,1)} %bitcast.28), custom_call_target="tpu_custom_call" | custom-call | tf_op jit(solution)/shard_map/pallas_call | solution.py:234
  136.4 3.3 %shard_map.104.done_b = bf16[256,768]{1,0:T(8,128)(2,1)S(1)} custom-call(bf16[128,2560]{1,0:T(8,128)(2,1)S(1)} %collective-permute-done.27.t0, bf16[128,2560]{1,0:T(8,128)(2,1)S(1)} %collective-permute-done.28.t1, bf16[5120,768]{1,0:T(8,128)(2,1)} %bitcast.29, f32[384,768]{1,0:T(8,128)S(1)} %shard_map.103.acc_ref), custom_call_target="tpu_custom_call" | custom-call | tf_op jit(solution)/shard_map/pallas_call | solution.py:256
  139.8 4.0 %shard_map.105 = (bf16[1024,384]{1,0:T(8,128)(2,1)S(1)}, bf16[512,384]{1,0:T(8,128)(2,1)S(1)}, bf16[512,384]{1,0:T(8,128)(2,1)S(1)}) custom-call(s32[7]{0:T(128)S(1)} %stack.27.refs_0_.pos_ref, bf16[128,2560]{1,0:T(8,128)(2,1)S(1)} %collective-permute-done.3.t0, bf16[5120,768]{1,0:T(8,128)(2,1)} %bitcast.30, f32[384,768]{1,0:T(8,128)S(1)} %shard_map.103.acc_ref, ...), custom_call_target="tpu_custom_call" | custom-call | tf_op jit(solution)/shard_map/pallas_call | solution.py:332
  144.6 6.1 %collective-permute-start.30 = (bf16[512,384]{1,0:T(8,128)(2,1)S(1)}, bf16[512,384]{1,0:T(8,128)(2,1)S(1)}, u32[]{:S(2)}, u32[]{:S(2)}) collective-permute-start(bf16[512,384]{1,0:T(8,128)(2,1)S(1)} %get-tuple-element.24), channel_id=1, source_target_pairs={{0,248},{1,249},{2,250},{3,251},{4,252},{5,253},{6,254},{7,255},{8... | collective-permute-start | bytes 1179656 | tf_op jit(solution)/shard_map/ppermute | solution.py:61
  150.6 4.0 %shard_map.107 = (bf16[1024,384]{1,0:T(8,128)(2,1)S(1)}, bf16[512,384]{1,0:T(8,128)(2,1)S(1)}, bf16[512,384]{1,0:T(8,128)(2,1)S(1)}) custom-call(s32[7]{0:T(128)S(1)} %stack.27.refs_0_.pos_ref, bf16[128,2560]{1,0:T(8,128)(2,1)S(1)} %collective-permute-done.3.t0, bf16[5120,768]{1,0:T(8,128)(2,1)} %bitcast.31, f32[384,768]{1,0:T(8,128)S(1)} %shard_map.103.acc_ref, ...), custom_call_target="tpu_custom_call" | custom-call | tf_op jit(solution)/shard_map/pallas_call | solution.py:332
  156.6 3.5 %collective-permute-done.30.far_ref = bf16[512,384]{1,0:T(8,128)(2,1)S(1)} collective-permute-done((bf16[512,384]{1,0:T(8,128)(2,1)S(1)}, bf16[512,384]{1,0:T(8,128)(2,1)S(1)}, u32[]{:S(2)}, u32[]{:S(2)}) %collective-permute-start.30) | collective-permute-done | bytes 393248 | tf_op jit(solution)/shard_map/ppermute | solution.py:61
  160.1 6.3 %shard_map.106 = (bf16[4,3,256,768]{3,2,1,0:T(8,128)(2,1)S(1)}, f32[1024,384]{1,0:T(8,128)S(1)}) custom-call(s32[7]{0:T(128)S(1)} %stack.27.refs_0_.pos_ref, bf16[1024,384]{1,0:T(8,128)(2,1)S(1)} %copy-done.1, bf16[1024,384]{1,0:T(8,128)(2,1)S(1)} %get-tuple-element.22.full_ref, bf16[512,384]{1,0:T(8,128)(2,1)S(1)} %collective-permute-done.29.near_ref, ...), custom_call_target="tpu_custom_call" | custom-call | tf_op jit(solution)/shard_map/pallas_call | solution.py:443
  166.4 3.0 %collective-permute-done.32.far_ref = bf16[512,384]{1,0:T(8,128)(2,1)S(1)} collective-permute-done((bf16[512,384]{1,0:T(8,128)(2,1)S(1)}, bf16[512,384]{1,0:T(8,128)(2,1)S(1)}, u32[]{:S(2)}, u32[]{:S(2)}) %collective-permute-start.32) | collective-permute-done | bytes 393248 | tf_op jit(solution)/shard_map/ppermute | solution.py:61
  169.4 4.3 %shard_map.108 = bf16[1024,384]{1,0:T(8,128)(2,1)} custom-call(s32[7]{0:T(128)S(1)} %stack.27.refs_0_.pos_ref, bf16[4,3,256,768]{3,2,1,0:T(8,128)(2,1)S(1)} %get-tuple-element.25.prob_ref, f32[1024,384]{1,0:T(8,128)S(1)} %get-tuple-element.26.total_ref, bf16[1024,384]{1,0:T(8,128)(2,1)S(1)} %get-tuple-element.28.full_ref, ...), custom_call_target="tpu_custom_call" | custom-call | tf_op jit(solution)/shard_map/pallas_call | solution.py:475
  (75 shorter events, 30.2 us)
Async XLA Ops:
  2.2 18.5 %collective-permute-start = (bf16[320,384]{1,0:T(8,128)(2,1)S(1)}, bf16[320,384]{1,0:T(8,128)(2,1)}, u32[]{:S(2)}, u32[]{:S(2)}) collective-permute-start(bf16[320,384]{1,0:T(8,128)(2,1)S(1)} %shard_map.100.refs_8_), channel_id=1, source_target_pairs={{0,64},{1,65},{2,66},{3,67},{4,68},{5,69},{6,70},{7,71},{8,200},{9... | collective-permute-start | bytes 737288 | tf_op jit(solution)/shard_map/ppermute | solution.py:61
  7.1 18.1 %collective-permute-start.10 = (bf16[320,384]{1,0:T(8,128)(2,1)}, bf16[320,384]{1,0:T(8,128)(2,1)S(1)}, u32[]{:S(2)}, u32[]{:S(2)}) collective-permute-start(bf16[320,384]{1,0:T(8,128)(2,1)} %collective-permute-done.8.refs_9_), channel_id=1, source_target_pairs={{0,16},{1,17},{2,18},{3,19},{4,20},{5,21},{6,22},{7,23},{8,56},{9,... | collective-permute-start | bytes 737288 | tf_op jit(solution)/shard_map/ppermute | solution.py:61
  13.1 35.3 %collective-permute-start.6 = (bf16[128,2560]{1,0:T(8,128)(2,1)}, bf16[128,2560]{1,0:T(8,128)(2,1)S(1)}, u32[]{:S(2)}, u32[]{:S(2)}) collective-permute-start(bf16[128,2560]{1,0:T(8,128)(2,1)} %get-tuple-element.32), channel_id=1, source_target_pairs={{0,4},{1,5},{2,6},{3,7},{4,0},{5,1},{6,2},{7,3},{8,12},{9,13},{10,... | collective-permute-start | bytes 1966088 | tf_op jit(solution)/shard_map/ppermute | solution.py:61
  18.1 35.9 %collective-permute-start.7 = (bf16[128,2560]{1,0:T(8,128)(2,1)}, bf16[128,2560]{1,0:T(8,128)(2,1)S(1)}, u32[]{:S(2)}, u32[]{:S(2)}) collective-permute-start(bf16[128,2560]{1,0:T(8,128)(2,1)} %get-tuple-element.31), channel_id=1, source_target_pairs={{0,4},{1,5},{2,6},{3,7},{4,0},{5,1},{6,2},{7,3},{8,12},{9,13},{10,... | collective-permute-start | bytes 1966088 | tf_op jit(solution)/shard_map/ppermute | solution.py:61
  26.1 20.7 %collective-permute-start.14 = (bf16[320,384]{1,0:T(8,128)(2,1)}, bf16[320,384]{1,0:T(8,128)(2,1)S(1)}, u32[]{:S(2)}, u32[]{:S(2)}) collective-permute-start(bf16[320,384]{1,0:T(8,128)(2,1)} %collective-permute-done.8.refs_9_), channel_id=1, source_target_pairs={{0,64},{1,65},{2,66},{3,67},{4,68},{5,69},{6,70},{7,71},{8,200},{9... | collective-permute-start | bytes 737288 | tf_op jit(solution)/shard_map/ppermute | solution.py:61
  29.2 26.4 %collective-permute-start.18 = (bf16[960,384]{1,0:T(8,128)(2,1)S(1)}, bf16[960,384]{1,0:T(8,128)(2,1)S(1)}, u32[]{:S(2)}, u32[]{:S(2)}) collective-permute-start(bf16[960,384]{1,0:T(8,128)(2,1)S(1)} %shard_map.101.refs_10_), channel_id=1, source_target_pairs={{0,64},{1,65},{2,66},{3,67},{4,68},{5,69},{6,70},{7,71},{8,200},{9... | collective-permute-start | bytes 2211848 | tf_op jit(solution)/shard_map/ppermute | solution.py:61
  31.6 25.5 %collective-permute-start.12 = (bf16[960,384]{1,0:T(8,128)(2,1)S(1)}, bf16[960,384]{1,0:T(8,128)(2,1)S(1)}, u32[]{:S(2)}, u32[]{:S(2)}) collective-permute-start(bf16[960,384]{1,0:T(8,128)(2,1)S(1)} %shard_map.101.refs_10_), channel_id=1, source_target_pairs={{0,8},{1,9},{2,10},{3,11},{4,12},{5,13},{6,14},{7,15},{8,0},{9,1},... | collective-permute-start | bytes 2211848 | tf_op jit(solution)/shard_map/ppermute | solution.py:61
  46.8 30.4 %collective-permute-start.4 = (bf16[128,5120]{1,0:T(8,128)(2,1)S(1)}, bf16[128,5120]{1,0:T(8,128)(2,1)S(1)}, u32[]{:S(2)}, u32[]{:S(2)}) collective-permute-start(bf16[128,5120]{1,0:T(8,128)(2,1)S(1)} %copy-done), channel_id=1, source_target_pairs={{0,1},{1,2},{2,3},{3,0},{4,5},{5,6},{6,7},{7,4},{8,9},{9,10},{10,1... | collective-permute-start | bytes 3932168 | tf_op jit(solution)/shard_map/ppermute | solution.py:61
  48.4 34.4 %collective-permute-start.1 = (bf16[128,5120]{1,0:T(8,128)(2,1)S(1)}, bf16[128,5120]{1,0:T(8,128)(2,1)S(1)}, u32[]{:S(2)}, u32[]{:S(2)}) collective-permute-start(bf16[128,5120]{1,0:T(8,128)(2,1)S(1)} %copy-done), channel_id=1, source_target_pairs={{0,3},{1,0},{2,1},{3,2},{4,7},{5,4},{6,5},{7,6},{8,11},{9,8},{10,9... | collective-permute-start | bytes 3932168 | tf_op jit(solution)/shard_map/ppermute | solution.py:61
  55.6 26.6 %collective-permute-start.22 = (bf16[960,384]{1,0:T(8,128)(2,1)S(1)}, bf16[960,384]{1,0:T(8,128)(2,1)S(1)}, u32[]{:S(2)}, u32[]{:S(2)}) collective-permute-start(bf16[960,384]{1,0:T(8,128)(2,1)S(1)} %collective-permute-done.18.refs_18_), channel_id=1, source_target_pairs={{0,64},{1,65},{2,66},{3,67},{4,68},{5,69},{6,70},{7,71},{8,200},{9... | collective-permute-start | bytes 2211848 | tf_op jit(solution)/shard_map/ppermute | solution.py:61
  57.1 25.2 %collective-permute-start.20 = (bf16[960,384]{1,0:T(8,128)(2,1)S(1)}, bf16[960,384]{1,0:T(8,128)(2,1)S(1)}, u32[]{:S(2)}, u32[]{:S(2)}) collective-permute-start(bf16[960,384]{1,0:T(8,128)(2,1)S(1)} %collective-permute-done.12.refs_11_), channel_id=1, source_target_pairs={{0,64},{1,65},{2,66},{3,67},{4,68},{5,69},{6,70},{7,71},{8,200},{9... | collective-permute-start | bytes 2211848 | tf_op jit(solution)/shard_map/ppermute | solution.py:61
  58.3 32.9 %collective-permute-start.24 = (bf16[128,2560]{1,0:T(8,128)(2,1)S(1)}, bf16[128,2560]{1,0:T(8,128)(2,1)S(1)}, u32[]{:S(2)}, u32[]{:S(2)}) collective-permute-start(bf16[128,2560]{1,0:T(8,128)(2,1)S(1)} %collective-permute-done.6.refs_6_), channel_id=1, source_target_pairs={{0,1},{1,2},{2,3},{3,0},{4,5},{5,6},{6,7},{7,4},{8,9},{9,10},{10,1... | collective-permute-start | bytes 1966088 | tf_op jit(solution)/shard_map/ppermute | solution.py:61
  77.2 15.9 %collective-permute-start.19 = (bf16[960,384]{1,0:T(8,128)(2,1)S(1)}, bf16[960,384]{1,0:T(8,128)(2,1)S(1)}, u32[]{:S(2)}, u32[]{:S(2)}) collective-permute-start(bf16[960,384]{1,0:T(8,128)(2,1)S(1)} %collective-permute-done.18.refs_18_), channel_id=1, source_target_pairs={{0,8},{1,9},{2,10},{3,11},{4,12},{5,13},{6,14},{7,15},{8,0},{9,1},... | collective-permute-start | bytes 2211848 | tf_op jit(solution)/shard_map/ppermute | solution.py:61
  82.3 28.9 %collective-permute-start.23 = (bf16[960,384]{1,0:T(8,128)(2,1)S(1)}, bf16[960,384]{1,0:T(8,128)(2,1)S(1)}, u32[]{:S(2)}, u32[]{:S(2)}) collective-permute-start(bf16[960,384]{1,0:T(8,128)(2,1)S(1)} %collective-permute-done.22.refs_22_), channel_id=1, source_target_pairs={{0,8},{1,9},{2,10},{3,11},{4,12},{5,13},{6,14},{7,15},{8,0},{9,1},... | collective-permute-start | bytes 2211848 | tf_op jit(solution)/shard_map/ppermute | solution.py:61
  82.3 31.9 %collective-permute-start.21 = (bf16[960,384]{1,0:T(8,128)(2,1)S(1)}, bf16[960,384]{1,0:T(8,128)(2,1)S(1)}, u32[]{:S(2)}, u32[]{:S(2)}) collective-permute-start(bf16[960,384]{1,0:T(8,128)(2,1)S(1)} %collective-permute-done.20.refs_20_), channel_id=1, source_target_pairs={{0,8},{1,9},{2,10},{3,11},{4,12},{5,13},{6,14},{7,15},{8,0},{9,1},... | collective-permute-start | bytes 2211848 | tf_op jit(solution)/shard_map/ppermute | solution.py:61
  82.8 22.4 %collective-permute-start.5 = (bf16[128,2560]{1,0:T(8,128)(2,1)S(1)}, bf16[128,2560]{1,0:T(8,128)(2,1)S(1)}, u32[]{:S(2)}, u32[]{:S(2)}) collective-permute-start(bf16[128,2560]{1,0:T(8,128)(2,1)S(1)} %slice.17), channel_id=1, source_target_pairs={{0,1},{1,2},{2,3},{3,0},{4,5},{5,6},{6,7},{7,4},{8,9},{9,10},{10,1... | collective-permute-start | bytes 1966088 | tf_op jit(solution)/shard_map/ppermute | solution.py:61
  91.2 19.6 %collective-permute-start.2 = (bf16[128,2560]{1,0:T(8,128)(2,1)S(1)}, bf16[128,2560]{1,0:T(8,128)(2,1)S(1)}, u32[]{:S(2)}, u32[]{:S(2)}) collective-permute-start(bf16[128,2560]{1,0:T(8,128)(2,1)S(1)} %slice.16), channel_id=1, source_target_pairs={{0,3},{1,0},{2,1},{3,2},{4,7},{5,4},{6,5},{7,6},{8,11},{9,8},{10,9... | collective-permute-start | bytes 1966088 | tf_op jit(solution)/shard_map/ppermute | solution.py:61
  93.1 39.4 %collective-permute-start.25 = (bf16[128,2560]{1,0:T(8,128)(2,1)S(1)}, bf16[128,2560]{1,0:T(8,128)(2,1)S(1)}, u32[]{:S(2)}, u32[]{:S(2)}) collective-permute-start(bf16[128,2560]{1,0:T(8,128)(2,1)S(1)} %collective-permute-done.6.refs_6_), channel_id=1, source_target_pairs={{0,3},{1,0},{2,1},{3,2},{4,7},{5,4},{6,5},{7,6},{8,11},{9,8},{10,9... | collective-permute-start | bytes 1966088 | tf_op jit(solution)/shard_map/ppermute | solution.py:61
  105.3 27.2 %collective-permute-start.26 = (bf16[128,2560]{1,0:T(8,128)(2,1)S(1)}, bf16[128,2560]{1,0:T(8,128)(2,1)S(1)}, u32[]{:S(2)}, u32[]{:S(2)}) collective-permute-start(bf16[128,2560]{1,0:T(8,128)(2,1)S(1)} %collective-permute-done.5.refs_4_), channel_id=1, source_target_pairs={{0,4},{1,5},{2,6},{3,7},{4,0},{5,1},{6,2},{7,3},{8,12},{9,13},{10,... | collective-permute-start | bytes 1966088 | tf_op jit(solution)/shard_map/ppermute | solution.py:61
  110.9 25.6 %collective-permute-start.27 = (bf16[128,2560]{1,0:T(8,128)(2,1)S(1)}, bf16[128,2560]{1,0:T(8,128)(2,1)S(1)}, u32[]{:S(2)}, u32[]{:S(2)}) collective-permute-start(bf16[128,2560]{1,0:T(8,128)(2,1)S(1)} %collective-permute-done.7.refs_7_), channel_id=1, source_target_pairs={{0,1},{1,2},{2,3},{3,0},{4,5},{5,6},{6,7},{7,4},{8,9},{9,10},{10,1... | collective-permute-start | bytes 1966088 | tf_op jit(solution)/shard_map/ppermute | solution.py:61
  111.2 25.3 %collective-permute-start.28 = (bf16[128,2560]{1,0:T(8,128)(2,1)S(1)}, bf16[128,2560]{1,0:T(8,128)(2,1)S(1)}, u32[]{:S(2)}, u32[]{:S(2)}) collective-permute-start(bf16[128,2560]{1,0:T(8,128)(2,1)S(1)} %collective-permute-done.7.refs_7_), channel_id=1, source_target_pairs={{0,3},{1,0},{2,1},{3,2},{4,7},{5,4},{6,5},{7,6},{8,11},{9,8},{10,9... | collective-permute-start | bytes 1966088 | tf_op jit(solution)/shard_map/ppermute | solution.py:61
  114.1 25.7 %collective-permute-start.3 = (bf16[128,2560]{1,0:T(8,128)(2,1)S(1)}, bf16[128,2560]{1,0:T(8,128)(2,1)S(1)}, u32[]{:S(2)}, u32[]{:S(2)}) collective-permute-start(bf16[128,2560]{1,0:T(8,128)(2,1)S(1)} %collective-permute-done.2.refs_5_), channel_id=1, source_target_pairs={{0,4},{1,5},{2,6},{3,7},{4,0},{5,1},{6,2},{7,3},{8,12},{9,13},{10,... | collective-permute-start | bytes 1966088 | tf_op jit(solution)/shard_map/ppermute | solution.py:61
  144.6 15.5 %collective-permute-start.30 = (bf16[512,384]{1,0:T(8,128)(2,1)S(1)}, bf16[512,384]{1,0:T(8,128)(2,1)S(1)}, u32[]{:S(2)}, u32[]{:S(2)}) collective-permute-start(bf16[512,384]{1,0:T(8,128)(2,1)S(1)} %get-tuple-element.24), channel_id=1, source_target_pairs={{0,248},{1,249},{2,250},{3,251},{4,252},{5,253},{6,254},{7,255},{8... | collective-permute-start | bytes 1179656 | tf_op jit(solution)/shard_map/ppermute | solution.py:61
  154.8 14.6 %collective-permute-start.32 = (bf16[512,384]{1,0:T(8,128)(2,1)S(1)}, bf16[512,384]{1,0:T(8,128)(2,1)S(1)}, u32[]{:S(2)}, u32[]{:S(2)}) collective-permute-start(bf16[512,384]{1,0:T(8,128)(2,1)S(1)} %get-tuple-element.30), channel_id=1, source_target_pairs={{0,248},{1,249},{2,250},{3,251},{4,252},{5,253},{6,254},{7,255},{8... | collective-permute-start | bytes 1179656 | tf_op jit(solution)/shard_map/ppermute | solution.py:61
  (19 other events, 178.8 us)

commit v5 on v4

--- a/solution.py
+++ b/solution.py
@@ -241,29 +241,6 @@
     )(*toks, w)
 
 
-def project_rest(toks, w, acc_in):
-    rows = sum(t.shape[0] for t in toks)
-    half = toks[0].shape[1]
-
-    def body(t0, t1, w_ref, acc_ref, out, t_buf, w_buf, t_sem, w_sem, acc, a_sem):
-        begin = pltpu.make_async_copy(acc_ref.at[pl.ds(0, rows), :], acc, a_sem)
-        begin.start()
-        product = _half_product((t0, t1), w_ref, half, (0, 768), t_buf, w_buf, t_sem, w_sem)
-        begin.wait()
-        product(acc)
-        out[...] = acc[...].astype(BF16)
-
-    return pl.pallas_call(
-        body,
-        out_shape=jax.ShapeDtypeStruct((rows, 768), BF16),
-        in_specs=[ANY] * 4,
-        out_specs=VM,
-        scratch_shapes=_half_scratch(rows, half, 768, 2)
-        + [pltpu.VMEM((rows, 768), F32), pltpu.SemaphoreType.DMA],
-        compiler_params=pltpu.CompilerParams(vmem_limit_bytes=48 * MIB),
-    )(*toks, w, acc_in)
-
-
 def _tile_at(slot_ref, block, p):
     tile = block * TPD
     for i in range(1, TPD):
@@ -275,32 +252,32 @@
     return jnp.minimum(start // 16 * 16, TILE - WIN)
 
 
-def project_last(side, pos, tok, w, acc_in, done, done_places, place, tables):
-    n, half = tok.shape
-    row0 = acc_in.shape[0] - n
-
-    def body(pos_ref, t0, w_ref, acc_ref, done_a, done_b, slot, neighbour, first,
+def project_last(side, pos, toks, w, acc_in, done, done_places, places, tables):
+    n, half = toks[0].shape
+    rows = n * len(toks)
+
+    def body(pos_ref, t0, t1, t2, w_ref, acc_ref, done_ref, slot, neighbour, first,
              full, near, far, t_buf, w_buf, t_sem, w_sem, acc, wide, a_sem):
         block, zl, y, blocks = pos_ref[3], pos_ref[4], pos_ref[5], pos_ref[6]
         cols = (side * 384, 384)
-        begin = pltpu.make_async_copy(acc_ref.at[pl.ds(row0, n), pl.ds(*cols)], acc, a_sem)
+        begin = pltpu.make_async_copy(acc_ref.at[:, pl.ds(*cols)], acc, a_sem)
         begin.start()
-        product = _half_product((t0,), w_ref, half, cols, t_buf, w_buf, t_sem, w_sem)
+        product = _half_product((t0, t1, t2), w_ref, half, cols, t_buf, w_buf, t_sem, w_sem)
 
         def row_of(place):
             dzl, dy = place
             return pl.multiple_of(((zl + dzl) % NZL * NY + (y + dy + NY) % NY) * n, n)
 
-        for ref, at in zip((done_a, done_b), done_places):
-            for i, where in enumerate(at):
-                part = ref[i * n : (i + 1) * n, side * 384 : side * 384 + 384]
-                full[pl.ds(row_of(where), n), :] = part
-                wide[pl.ds(row_of(where), n), :] = part.astype(F32)
+        for i, place in enumerate(done_places):
+            part = done_ref[i * n : (i + 1) * n, side * 384 : side * 384 + 384]
+            full[pl.ds(row_of(place), n), :] = part
+            wide[pl.ds(row_of(place), n), :] = part.astype(F32)
         begin.wait()
         product(acc)
-        part = acc[...].astype(BF16)
-        full[pl.ds(row_of(place), n), :] = part
-        wide[pl.ds(row_of(place), n), :] = part.astype(F32)
+        for i, place in enumerate(places):
+            part = acc[i * n : (i + 1) * n, :].astype(BF16)
+            full[pl.ds(row_of(place), n), :] = part
+            wide[pl.ds(row_of(place), n), :] = part.astype(F32)
         up = 1 - 2 * pos_ref[2]
         for out, step in ((far, -up), (near, up)):
             target = (block + step + blocks) % blocks
@@ -333,13 +310,13 @@
         body,
         out_shape=[jax.ShapeDtypeStruct((TPD * TILE, 384), BF16)]
         + [jax.ShapeDtypeStruct((HALO, 384), BF16)] * 2,
-        in_specs=[SM] + [ANY] * 3 + [VM] * 2 + [SM] * 3,
+        in_specs=[SM] + [ANY] * 5 + [VM] + [SM] * 3,
         out_specs=[VM] * 3,
-        scratch_shapes=_half_scratch(n, half, 384, 1)
-        + [pltpu.VMEM((n, 384), F32), pltpu.VMEM((TPD * TILE + 8, 384), F32)]
+        scratch_shapes=_half_scratch(rows, half, 384, 3)
+        + [pltpu.VMEM((rows, 384), F32), pltpu.VMEM((TPD * TILE + 8, 384), F32)]
         + [pltpu.SemaphoreType.DMA],
         compiler_params=pltpu.CompilerParams(vmem_limit_bytes=48 * MIB),
-    )(pos, tok, w, acc_in, *done, *tables)
+    )(pos, *toks, w, acc_in, done, *tables)
 
 
 CAND = 768
@@ -524,13 +501,13 @@
     ya = send(tokens, dy=1)
     z1w = send(w, sz=1)
     yb = send(tokens, dy=-1)
+    wc, tl, tr = lax.optimization_barrier((wc, tokens[:, :h], tokens[:, h:]))
     z1c = send(wc, sz=1)
     xw1 = send(w, sx=1)
     xc1 = send(wc, sx=1)
     z2 = send(z1w, sz=1)
     xw1, pos = lax.optimization_barrier((xw1, pos))
     xw2 = send(xw1, sx=1)
-    tl, tr = tokens[:, :h], tokens[:, h:]
     z_l = send(tl, dzl=1)
     near = join(z1w, z1c, z2)
     xn1 = send(near, sx=1)
@@ -568,18 +545,18 @@
     kv1, w_all = project(pos, toks, at, 5 * n, pieces, fs)
     w_all = w_all.reshape(tokens.shape[1], 768)
     part = project_half((ua_l, ub_l, uo_l), w_all)
-    kv2 = project_rest((ua_r, ub_r), w_all, part)
+    rest = (ua_r, ub_r, uo_r)
     last = (
-        (kv1, kv2),
-        (((0, 0), (0, -1), (0, 1), (0, 2), (1, 0)), ((1, -1), (1, 1))),
-        (1, 2),
+        kv1,
+        ((0, 0), (0, -1), (0, 1), (0, 2), (1, 0)),
+        ((1, -1), (1, 1), (1, 2)),
         tables[:3],
     )
-    keys, near_k, far_k = project_last(0, pos, uo_r, w_all, part, *last)
+    keys, near_k, far_k = project_last(0, pos, rest, w_all, part, *last)
     part = lax.optimization_barrier((part, far_k))[0]
     far_k = send(far_k, far=1)
     near_k = send(near_k, dc=1)
-    values, near_v, far_v = project_last(1, pos, uo_r, w_all, part, *last)
+    values, near_v, far_v = project_last(1, pos, rest, w_all, part, *last)
     far_v = send(far_v, far=1)
     near_v = send(near_v, dc=1)
     prob, total = weigh(pos, queries, keys, near_k, far_k, tables)

time: 176 us -> 157 us (0.89); the launches traced: 174 us -> 157 us
  starting transfers between devices: 77.2 us -> 38.7 us
  waiting for transfers between devices: 52.8 us -> 77.3 us
  Pallas kernels: 39.1 us -> 37 us
    ppermute x33, starting transfers between devices: 77.2 us -> 38.7 us  [send(): lax.ppermute(a, AXES, _far_moves() if 'far' in step else _moves(**step))]
    ppermute x33, waiting for transfers between devices: 52.8 us -> 77.3 us  [send(): lax.ppermute(a, AXES, _far_moves() if 'far' in step else _moves(**step))]
    pallas_call x1 -> x0, Pallas kernels: 3.34 us -> none  [project_rest(): pl.pallas_call(body, out_shape=jax.ShapeDtypeStruct((rows, 768), BF16), i...]
    pallas_call x2, Pallas kernels: 8.06 us -> 9.86 us  [project_last(): pl.pallas_call(body, out_shape=[jax.ShapeDtypeStruct((TPD * TILE, 384), B...]
  transfers between devices with their start and end apart: 33 -> 33, of which waited for: 10 -> 12; matrix products, arithmetic and copies ran while one was open for 1% -> 1% of each run, Pallas kernels for 18% -> 18%
where the time goes in v5:
time: 157 us
  waiting for transfers between devices  77.3 us (49%)
  starting transfers between devices  38.7 us (25%)
  Pallas kernels  37 us (24%)
  local copies, waits for them, and re-layouts  3.39 us (2%)
    ppermute x33, waiting for transfers between devices, send(): lax.ppermute(a, AXES, _far_moves() if 'far' in step else _moves(**step))  77.3 us
    ppermute x33, starting transfers between devices, send(): lax.ppermute(a, AXES, _far_moves() if 'far' in step else _moves(**step))  38.7 us
    pallas_call x1, Pallas kernels, project(): pl.pallas_call(body, out_shape=[jax.ShapeDtypeStruct((rows, 768), BF16),...  11.4 us
    pallas_call x2, Pallas kernels, project_last(): pl.pallas_call(body, out_shape=[jax.ShapeDtypeStruct((TPD * TILE, 384), B...  9.86 us
    pallas_call x1, Pallas kernels, weigh(): pl.pallas_call(body, grid=(TPD,), out_shape=[jax.ShapeDtypeStruct((TPD, 3...  6.26 us
    pallas_call x1, Pallas kernels, mix(): pl.pallas_call(body, grid=(TPD,), out_shape=jax.ShapeDtypeStruct((TPD * T...  4.33 us
    pallas_call x1, Pallas kernels, project_half(): pl.pallas_call(body, out_shape=jax.ShapeDtypeStruct((rows, 768), F32), in...  3.91 us
  transfers between devices with their start and end apart: 33, of which 12 were waited for; matrix products, arithmetic and copies ran while one was open for 1% of the time, Pallas kernels for 18%

profile of v5, /device:TPU:32, one launch (start us, length us, event | category | flops | bytes accessed | tf_op | source)
XLA Modules:
  0.0 156.6 jit_solution(5685303516881082056)
XLA Ops:
  4.5 3.3 %collective-permute-start.11 = (bf16[320,384]{1,0:T(8,128)(2,1)S(1)}, bf16[320,384]{1,0:T(8,128)(2,1)S(1)}, u32[]{:S(2)}, u32[]{:S(2)}) collective-permute-start(bf16[320,384]{1,0:T(8,128)(2,1)S(1)} %shard_map.100.refs_8_), channel_id=1, source_target_pairs={{0,16},{1,17},{2,18},{3,19},{4,20},{5,21},{6,22},{7,23},{8,56},{9,... | collective-permute-start | bytes 737288 | tf_op jit(solution)/shard_map/ppermute | solution.py:61
  7.8 3.0 %collective-permute-start.5 = (bf16[128,5120]{1,0:T(8,128)(2,1)}, bf16[128,5120]{1,0:T(8,128)(2,1)S(1)}, u32[]{:S(2)}, u32[]{:S(2)}) collective-permute-start(bf16[128,5120]{1,0:T(8,128)(2,1)} %refs_1_.3), channel_id=1, source_target_pairs={{0,3},{1,0},{2,1},{3,2},{4,7},{5,4},{6,5},{7,6},{8,11},{9,8},{10,9... | collective-permute-start | bytes 3932168 | tf_op jit(solution)/shard_map/ppermute | solution.py:61
  13.0 3.7 %collective-permute-start.12 = (bf16[320,384]{1,0:T(8,128)(2,1)S(1)}, bf16[320,384]{1,0:T(8,128)(2,1)S(1)}, u32[]{:S(2)}, u32[]{:S(2)}) collective-permute-start(bf16[320,384]{1,0:T(8,128)(2,1)S(1)} %collective-permute-done.1.refs_9_), channel_id=1, source_target_pairs={{0,16},{1,17},{2,18},{3,19},{4,20},{5,21},{6,22},{7,23},{8,56},{9,... | collective-permute-start | bytes 737288 | tf_op jit(solution)/shard_map/ppermute | solution.py:61
  17.9 1.8 %collective-permute-start.13 = (bf16[320,384]{1,0:T(8,128)(2,1)S(1)}, bf16[320,384]{1,0:T(8,128)(2,1)S(1)}, u32[]{:S(2)}, u32[]{:S(2)}) collective-permute-start(bf16[320,384]{1,0:T(8,128)(2,1)S(1)} %collective-permute-done.11.refs_0_), channel_id=1, source_target_pairs={{0,16},{1,17},{2,18},{3,19},{4,20},{5,21},{6,22},{7,23},{8,56},{9,... | collective-permute-start | bytes 737288 | tf_op jit(solution)/shard_map/ppermute | solution.py:61
  19.7 4.4 %collective-permute-done.12.refs_1_ = bf16[320,384]{1,0:T(8,128)(2,1)S(1)} collective-permute-done((bf16[320,384]{1,0:T(8,128)(2,1)S(1)}, bf16[320,384]{1,0:T(8,128)(2,1)S(1)}, u32[]{:S(2)}, u32[]{:S(2)}) %collective-permute-start.12) | collective-permute-done | bytes 245792 | tf_op jit(solution)/shard_map/ppermute | solution.py:61
  24.6 4.4 %collective-permute-done.13.refs_2_ = bf16[320,384]{1,0:T(8,128)(2,1)S(1)} collective-permute-done((bf16[320,384]{1,0:T(8,128)(2,1)S(1)}, bf16[320,384]{1,0:T(8,128)(2,1)S(1)}, u32[]{:S(2)}, u32[]{:S(2)}) %collective-permute-start.13) | collective-permute-done | bytes 245792 | tf_op jit(solution)/shard_map/ppermute | solution.py:61
  33.1 9.7 %collective-permute-done.20.refs_18_ = bf16[960,384]{1,0:T(8,128)(2,1)S(1)} collective-permute-done((bf16[960,384]{1,0:T(8,128)(2,1)S(1)}, bf16[960,384]{1,0:T(8,128)(2,1)S(1)}, u32[]{:S(2)}, u32[]{:S(2)}) %collective-permute-start.20) | collective-permute-done | bytes 737312 | tf_op jit(solution)/shard_map/ppermute | solution.py:61
  43.7 6.1 %collective-permute-done.10.refs_6_ = bf16[128,2560]{1,0:T(8,128)(2,1)S(1)} collective-permute-done((bf16[128,2560]{1,0:T(8,128)(2,1)S(1)}, bf16[128,2560]{1,0:T(8,128)(2,1)S(1)}, u32[]{:S(2)}, u32[]{:S(2)}) %collective-permute-start.10) | collective-permute-done | bytes 655392 | tf_op jit(solution)/shard_map/ppermute | solution.py:61
  51.7 12.8 %collective-permute-done.8.refs_2_ = bf16[128,5120]{1,0:T(8,128)(2,1)S(1)} collective-permute-done((bf16[128,5120]{1,0:T(8,128)(2,1)S(1)}, bf16[128,5120]{1,0:T(8,128)(2,1)S(1)}, u32[]{:S(2)}, u32[]{:S(2)}) %collective-permute-start.8) | collective-permute-done | bytes 1310752 | tf_op jit(solution)/shard_map/ppermute | solution.py:61
  67.3 11.2 %collective-permute-done.26.t0 = bf16[128,2560]{1,0:T(8,128)(2,1)S(1)} collective-permute-done((bf16[128,2560]{1,0:T(8,128)(2,1)S(1)}, bf16[128,2560]{1,0:T(8,128)(2,1)S(1)}, u32[]{:S(2)}, u32[]{:S(2)}) %collective-permute-start.26) | collective-permute-done | bytes 655392 | tf_op jit(solution)/shard_map/ppermute | solution.py:61
  80.9 11.1 %collective-permute-done.9.refs_4_ = bf16[128,2560]{1,0:T(8,128)(2,1)S(1)} collective-permute-done((bf16[128,2560]{1,0:T(8,128)(2,1)S(1)}, bf16[128,2560]{1,0:T(8,128)(2,1)S(1)}, u32[]{:S(2)}, u32[]{:S(2)}) %collective-permute-start.9) | collective-permute-done | bytes 655392 | tf_op jit(solution)/shard_map/ppermute | solution.py:61
  92.7 3.5 %collective-permute-done.6.refs_5_ = bf16[128,2560]{1,0:T(8,128)(2,1)S(1)} collective-permute-done((bf16[128,2560]{1,0:T(8,128)(2,1)S(1)}, bf16[128,2560]{1,0:T(8,128)(2,1)S(1)}, u32[]{:S(2)}, u32[]{:S(2)}) %collective-permute-start.6) | collective-permute-done | bytes 655392 | tf_op jit(solution)/shard_map/ppermute | solution.py:61
  96.3 3.0 %collective-permute-start.4 = (bf16[128,2560]{1,0:T(8,128)(2,1)S(1)}, bf16[128,2560]{1,0:T(8,128)(2,1)S(1)}, u32[]{:S(2)}, u32[]{:S(2)}) collective-permute-start(bf16[128,2560]{1,0:T(8,128)(2,1)S(1)} %collective-permute-done.2.refs_7_), channel_id=1, source_target_pairs={{0,3},{1,0},{2,1},{3,2},{4,7},{5,4},{6,5},{7,6},{8,11},{9,8},{10,9... | collective-permute-start | bytes 1966088 | tf_op jit(solution)/shard_map/ppermute | solution.py:61
  100.3 11.4 %shard_map.102 = (bf16[640,768]{1,0:T(8,128)(2,1)S(1)}, bf16[4,1280,768]{2,1,0:T(8,128)(2,1)}) custom-call(s32[7]{0:T(128)S(1)} %stack.27.refs_0_.pos_ref, bf16[128,5120]{1,0:T(8,128)(2,1)S(1)} %copy-done, bf16[128,5120]{1,0:T(8,128)(2,1)S(1)} %collective-permute-done.8.refs_2_, bf16[128,5120]{1,0:T(8,128)(2,1)S(1)} %collective-permute-done.5.refs_3_, ...), custom_call_target="tpu_custom_call" | custom-call | tf_op jit(solution)/shard_map/pallas_call | solution.py:163
  111.8 3.9 %shard_map.103.acc_ref = f32[384,768]{1,0:T(8,128)S(1)} custom-call(bf16[128,2560]{1,0:T(8,128)(2,1)S(1)} %collective-permute-done.26.t0, bf16[128,2560]{1,0:T(8,128)(2,1)S(1)} %collective-permute-done.27.t1, bf16[128,2560]{1,0:T(8,128)(2,1)S(1)} %collective-permute-done.28.t2, bf16[5120,768]{1,0:T(8,128)(2,1)} %bitcast.28), custom_call_target="tpu_custom_call" | custom-call | tf_op jit(solution)/shard_map/pallas_call | solution.py:234
  115.7 6.6 %collective-permute-done.4.t1 = bf16[128,2560]{1,0:T(8,128)(2,1)S(1)} collective-permute-done((bf16[128,2560]{1,0:T(8,128)(2,1)S(1)}, bf16[128,2560]{1,0:T(8,128)(2,1)S(1)}, u32[]{:S(2)}, u32[]{:S(2)}) %collective-permute-start.4) | collective-permute-done | bytes 655392 | tf_op jit(solution)/shard_map/ppermute | solution.py:61
  122.3 4.9 %shard_map.104 = (bf16[1024,384]{1,0:T(8,128)(2,1)S(1)}, bf16[512,384]{1,0:T(8,128)(2,1)S(1)}, bf16[512,384]{1,0:T(8,128)(2,1)S(1)}) custom-call(s32[7]{0:T(128)S(1)} %stack.27.refs_0_.pos_ref, bf16[128,2560]{1,0:T(8,128)(2,1)S(1)} %collective-permute-done.3.t0, bf16[128,2560]{1,0:T(8,128)(2,1)S(1)} %collective-permute-done.4.t1, ...), custom_call_target="tpu_custom_call" | custom-call | tf_op jit(solution)/shard_map/pallas_call | solution.py:309
  127.4 4.1 %collective-permute-start.30 = (bf16[512,384]{1,0:T(8,128)(2,1)S(1)}, bf16[512,384]{1,0:T(8,128)(2,1)S(1)}, u32[]{:S(2)}, u32[]{:S(2)}) collective-permute-start(bf16[512,384]{1,0:T(8,128)(2,1)S(1)} %get-tuple-element.30), channel_id=1, source_target_pairs={{0,248},{1,249},{2,250},{3,251},{4,252},{5,253},{6,254},{7,255},{8... | collective-permute-start | bytes 1179656 | tf_op jit(solution)/shard_map/ppermute | solution.py:61
  131.5 4.9 %shard_map.106 = (bf16[1024,384]{1,0:T(8,128)(2,1)S(1)}, bf16[512,384]{1,0:T(8,128)(2,1)S(1)}, bf16[512,384]{1,0:T(8,128)(2,1)S(1)}) custom-call(s32[7]{0:T(128)S(1)} %stack.27.refs_0_.pos_ref, bf16[128,2560]{1,0:T(8,128)(2,1)S(1)} %collective-permute-done.3.t0, bf16[128,2560]{1,0:T(8,128)(2,1)S(1)} %collective-permute-done.4.t1, ...), custom_call_target="tpu_custom_call" | custom-call | tf_op jit(solution)/shard_map/pallas_call | solution.py:309
  136.6 2.4 %collective-permute-start.32 = (bf16[512,384]{1,0:T(8,128)(2,1)S(1)}, bf16[512,384]{1,0:T(8,128)(2,1)S(1)}, u32[]{:S(2)}, u32[]{:S(2)}) collective-permute-start(bf16[512,384]{1,0:T(8,128)(2,1)S(1)} %get-tuple-element.36), channel_id=1, source_target_pairs={{0,248},{1,249},{2,250},{3,251},{4,252},{5,253},{6,254},{7,255},{8... | collective-permute-start | bytes 1179656 | tf_op jit(solution)/shard_map/ppermute | solution.py:61
  139.0 4.0 %collective-permute-done.30.far_ref = bf16[512,384]{1,0:T(8,128)(2,1)S(1)} collective-permute-done((bf16[512,384]{1,0:T(8,128)(2,1)S(1)}, bf16[512,384]{1,0:T(8,128)(2,1)S(1)}, u32[]{:S(2)}, u32[]{:S(2)}) %collective-permute-start.30) | collective-permute-done | bytes 393248 | tf_op jit(solution)/shard_map/ppermute | solution.py:61
  143.0 6.3 %shard_map.105 = (bf16[4,3,256,768]{3,2,1,0:T(8,128)(2,1)S(1)}, f32[1024,384]{1,0:T(8,128)S(1)}) custom-call(s32[7]{0:T(128)S(1)} %stack.27.refs_0_.pos_ref, bf16[1024,384]{1,0:T(8,128)(2,1)S(1)} %copy-done.1, bf16[1024,384]{1,0:T(8,128)(2,1)S(1)} %get-tuple-element.28.full_ref, bf16[512,384]{1,0:T(8,128)(2,1)S(1)} %collective-permute-done.29.near_ref, ...), custom_call_target="tpu_custom_call" | custom-call | tf_op jit(solution)/shard_map/pallas_call | solution.py:420
  149.3 3.0 %collective-permute-done.32.far_ref = bf16[512,384]{1,0:T(8,128)(2,1)S(1)} collective-permute-done((bf16[512,384]{1,0:T(8,128)(2,1)S(1)}, bf16[512,384]{1,0:T(8,128)(2,1)S(1)}, u32[]{:S(2)}, u32[]{:S(2)}) %collective-permute-start.32) | collective-permute-done | bytes 393248 | tf_op jit(solution)/shard_map/ppermute | solution.py:61
  152.3 4.3 %shard_map.107 = bf16[1024,384]{1,0:T(8,128)(2,1)} custom-call(s32[7]{0:T(128)S(1)} %stack.27.refs_0_.pos_ref, bf16[4,3,256,768]{3,2,1,0:T(8,128)(2,1)S(1)} %get-tuple-element.31.prob_ref, f32[1024,384]{1,0:T(8,128)S(1)} %get-tuple-element.32.total_ref, bf16[1024,384]{1,0:T(8,128)(2,1)S(1)} %get-tuple-element.34.full_ref, ...), custom_call_target="tpu_custom_call" | custom-call | tf_op jit(solution)/shard_map/pallas_call | solution.py:452
  (74 shorter events, 22.6 us)
Async XLA Ops:
  4.5 13.4 %collective-permute-start.11 = (bf16[320,384]{1,0:T(8,128)(2,1)S(1)}, bf16[320,384]{1,0:T(8,128)(2,1)S(1)}, u32[]{:S(2)}, u32[]{:S(2)}) collective-permute-start(bf16[320,384]{1,0:T(8,128)(2,1)S(1)} %shard_map.100.refs_8_), channel_id=1, source_target_pairs={{0,16},{1,17},{2,18},{3,19},{4,20},{5,21},{6,22},{7,23},{8,56},{9,... | collective-permute-start | bytes 737288 | tf_op jit(solution)/shard_map/ppermute | solution.py:61
  7.8 42.3 %collective-permute-start.5 = (bf16[128,5120]{1,0:T(8,128)(2,1)}, bf16[128,5120]{1,0:T(8,128)(2,1)S(1)}, u32[]{:S(2)}, u32[]{:S(2)}) collective-permute-start(bf16[128,5120]{1,0:T(8,128)(2,1)} %refs_1_.3), channel_id=1, source_target_pairs={{0,3},{1,0},{2,1},{3,2},{4,7},{5,4},{6,5},{7,6},{8,11},{9,8},{10,9... | collective-permute-start | bytes 3932168 | tf_op jit(solution)/shard_map/ppermute | solution.py:61
  19.7 11.8 %collective-permute-start.15 = (bf16[320,384]{1,0:T(8,128)(2,1)S(1)}, bf16[320,384]{1,0:T(8,128)(2,1)S(1)}, u32[]{:S(2)}, u32[]{:S(2)}) collective-permute-start(bf16[320,384]{1,0:T(8,128)(2,1)S(1)} %collective-permute-done.refs_12_), channel_id=1, source_target_pairs={{0,8},{1,9},{2,10},{3,11},{4,12},{5,13},{6,14},{7,15},{8,0},{9,1},... | collective-permute-start | bytes 737288 | tf_op jit(solution)/shard_map/ppermute | solution.py:61
  30.0 12.8 %collective-permute-start.20 = (bf16[960,384]{1,0:T(8,128)(2,1)S(1)}, bf16[960,384]{1,0:T(8,128)(2,1)S(1)}, u32[]{:S(2)}, u32[]{:S(2)}) collective-permute-start(bf16[960,384]{1,0:T(8,128)(2,1)S(1)} %shard_map.101.refs_10_), channel_id=1, source_target_pairs={{0,64},{1,65},{2,66},{3,67},{4,68},{5,69},{6,70},{7,71},{8,200},{9... | collective-permute-start | bytes 2211848 | tf_op jit(solution)/shard_map/ppermute | solution.py:61
  31.5 32.9 %collective-permute-start.8 = (bf16[128,5120]{1,0:T(8,128)(2,1)S(1)}, bf16[128,5120]{1,0:T(8,128)(2,1)S(1)}, u32[]{:S(2)}, u32[]{:S(2)}) collective-permute-start(bf16[128,5120]{1,0:T(8,128)(2,1)S(1)} %copy-done), channel_id=1, source_target_pairs={{0,1},{1,2},{2,3},{3,0},{4,5},{5,6},{6,7},{7,4},{8,9},{9,10},{10,1... | collective-permute-start | bytes 3932168 | tf_op jit(solution)/shard_map/ppermute | solution.py:61
  33.1 16.8 %collective-permute-start.10 = (bf16[128,2560]{1,0:T(8,128)(2,1)S(1)}, bf16[128,2560]{1,0:T(8,128)(2,1)S(1)}, u32[]{:S(2)}, u32[]{:S(2)}) collective-permute-start(bf16[128,2560]{1,0:T(8,128)(2,1)S(1)} %get-tuple-element.23), channel_id=1, source_target_pairs={{0,4},{1,5},{2,6},{3,7},{4,0},{5,1},{6,2},{7,3},{8,12},{9,13},{10,... | collective-permute-start | bytes 1966088 | tf_op jit(solution)/shard_map/ppermute | solution.py:61
  42.7 21.7 %collective-permute-start.24 = (bf16[960,384]{1,0:T(8,128)(2,1)S(1)}, bf16[960,384]{1,0:T(8,128)(2,1)S(1)}, u32[]{:S(2)}, u32[]{:S(2)}) collective-permute-start(bf16[960,384]{1,0:T(8,128)(2,1)S(1)} %collective-permute-done.20.refs_18_), channel_id=1, source_target_pairs={{0,64},{1,65},{2,66},{3,67},{4,68},{5,69},{6,70},{7,71},{8,200},{9... | collective-permute-start | bytes 2211848 | tf_op jit(solution)/shard_map/ppermute | solution.py:61
  43.0 22.0 %collective-permute-start.22 = (bf16[960,384]{1,0:T(8,128)(2,1)S(1)}, bf16[960,384]{1,0:T(8,128)(2,1)S(1)}, u32[]{:S(2)}, u32[]{:S(2)}) collective-permute-start(bf16[960,384]{1,0:T(8,128)(2,1)S(1)} %collective-permute-done.14.refs_11_), channel_id=1, source_target_pairs={{0,64},{1,65},{2,66},{3,67},{4,68},{5,69},{6,70},{7,71},{8,200},{9... | collective-permute-start | bytes 2211848 | tf_op jit(solution)/shard_map/ppermute | solution.py:61
  49.8 15.9 %collective-permute-start.2 = (bf16[128,2560]{1,0:T(8,128)(2,1)S(1)}, bf16[128,2560]{1,0:T(8,128)(2,1)S(1)}, u32[]{:S(2)}, u32[]{:S(2)}) collective-permute-start(bf16[128,2560]{1,0:T(8,128)(2,1)S(1)} %get-tuple-element.22), channel_id=1, source_target_pairs={{0,4},{1,5},{2,6},{3,7},{4,0},{5,1},{6,2},{7,3},{8,12},{9,13},{10,... | collective-permute-start | bytes 1966088 | tf_op jit(solution)/shard_map/ppermute | solution.py:61
  50.1 28.4 %collective-permute-start.26 = (bf16[128,2560]{1,0:T(8,128)(2,1)S(1)}, bf16[128,2560]{1,0:T(8,128)(2,1)S(1)}, u32[]{:S(2)}, u32[]{:S(2)}) collective-permute-start(bf16[128,2560]{1,0:T(8,128)(2,1)S(1)} %collective-permute-done.10.refs_6_), channel_id=1, source_target_pairs={{0,1},{1,2},{2,3},{3,0},{4,5},{5,6},{6,7},{7,4},{8,9},{9,10},{10,1... | collective-permute-start | bytes 1966088 | tf_op jit(solution)/shard_map/ppermute | solution.py:61
  64.5 15.7 %collective-permute-start.21 = (bf16[960,384]{1,0:T(8,128)(2,1)S(1)}, bf16[960,384]{1,0:T(8,128)(2,1)S(1)}, u32[]{:S(2)}, u32[]{:S(2)}) collective-permute-start(bf16[960,384]{1,0:T(8,128)(2,1)S(1)} %collective-permute-done.20.refs_18_), channel_id=1, source_target_pairs={{0,8},{1,9},{2,10},{3,11},{4,12},{5,13},{6,14},{7,15},{8,0},{9,1},... | collective-permute-start | bytes 2211848 | tf_op jit(solution)/shard_map/ppermute | solution.py:61
  64.5 31.9 %collective-permute-start.25 = (bf16[960,384]{1,0:T(8,128)(2,1)S(1)}, bf16[960,384]{1,0:T(8,128)(2,1)S(1)}, u32[]{:S(2)}, u32[]{:S(2)}) collective-permute-start(bf16[960,384]{1,0:T(8,128)(2,1)S(1)} %collective-permute-done.24.refs_22_), channel_id=1, source_target_pairs={{0,8},{1,9},{2,10},{3,11},{4,12},{5,13},{6,14},{7,15},{8,0},{9,1},... | collective-permute-start | bytes 2211848 | tf_op jit(solution)/shard_map/ppermute | solution.py:61
  65.0 34.4 %collective-permute-start.23 = (bf16[960,384]{1,0:T(8,128)(2,1)S(1)}, bf16[960,384]{1,0:T(8,128)(2,1)S(1)}, u32[]{:S(2)}, u32[]{:S(2)}) collective-permute-start(bf16[960,384]{1,0:T(8,128)(2,1)S(1)} %collective-permute-done.22.refs_20_), channel_id=1, source_target_pairs={{0,8},{1,9},{2,10},{3,11},{4,12},{5,13},{6,14},{7,15},{8,0},{9,1},... | collective-permute-start | bytes 2211848 | tf_op jit(solution)/shard_map/ppermute | solution.py:61
  65.8 26.3 %collective-permute-start.9 = (bf16[128,2560]{1,0:T(8,128)(2,1)S(1)}, bf16[128,2560]{1,0:T(8,128)(2,1)S(1)}, u32[]{:S(2)}, u32[]{:S(2)}) collective-permute-start(bf16[128,2560]{1,0:T(8,128)(2,1)S(1)} %slice.17), channel_id=1, source_target_pairs={{0,1},{1,2},{2,3},{3,0},{4,5},{5,6},{6,7},{7,4},{8,9},{9,10},{10,1... | collective-permute-start | bytes 1966088 | tf_op jit(solution)/shard_map/ppermute | solution.py:61
  78.5 17.6 %collective-permute-start.6 = (bf16[128,2560]{1,0:T(8,128)(2,1)S(1)}, bf16[128,2560]{1,0:T(8,128)(2,1)S(1)}, u32[]{:S(2)}, u32[]{:S(2)}) collective-permute-start(bf16[128,2560]{1,0:T(8,128)(2,1)S(1)} %slice.16), channel_id=1, source_target_pairs={{0,3},{1,0},{2,1},{3,2},{4,7},{5,4},{6,5},{7,6},{8,11},{9,8},{10,9... | collective-permute-start | bytes 1966088 | tf_op jit(solution)/shard_map/ppermute | solution.py:61
  80.2 31.5 %collective-permute-start.27 = (bf16[128,2560]{1,0:T(8,128)(2,1)S(1)}, bf16[128,2560]{1,0:T(8,128)(2,1)S(1)}, u32[]{:S(2)}, u32[]{:S(2)}) collective-permute-start(bf16[128,2560]{1,0:T(8,128)(2,1)S(1)} %collective-permute-done.10.refs_6_), channel_id=1, source_target_pairs={{0,3},{1,0},{2,1},{3,2},{4,7},{5,4},{6,5},{7,6},{8,11},{9,8},{10,9... | collective-permute-start | bytes 1966088 | tf_op jit(solution)/shard_map/ppermute | solution.py:61
  92.0 19.7 %collective-permute-start.28 = (bf16[128,2560]{1,0:T(8,128)(2,1)S(1)}, bf16[128,2560]{1,0:T(8,128)(2,1)S(1)}, u32[]{:S(2)}, u32[]{:S(2)}) collective-permute-start(bf16[128,2560]{1,0:T(8,128)(2,1)S(1)} %collective-permute-done.9.refs_4_), channel_id=1, source_target_pairs={{0,4},{1,5},{2,6},{3,7},{4,0},{5,1},{6,2},{7,3},{8,12},{9,13},{10,... | collective-permute-start | bytes 1966088 | tf_op jit(solution)/shard_map/ppermute | solution.py:61
  96.1 19.6 %collective-permute-start.3 = (bf16[128,2560]{1,0:T(8,128)(2,1)S(1)}, bf16[128,2560]{1,0:T(8,128)(2,1)S(1)}, u32[]{:S(2)}, u32[]{:S(2)}) collective-permute-start(bf16[128,2560]{1,0:T(8,128)(2,1)S(1)} %collective-permute-done.2.refs_7_), channel_id=1, source_target_pairs={{0,1},{1,2},{2,3},{3,0},{4,5},{5,6},{6,7},{7,4},{8,9},{9,10},{10,1... | collective-permute-start | bytes 1966088 | tf_op jit(solution)/shard_map/ppermute | solution.py:61
  96.3 25.9 %collective-permute-start.4 = (bf16[128,2560]{1,0:T(8,128)(2,1)S(1)}, bf16[128,2560]{1,0:T(8,128)(2,1)S(1)}, u32[]{:S(2)}, u32[]{:S(2)}) collective-permute-start(bf16[128,2560]{1,0:T(8,128)(2,1)S(1)} %collective-permute-done.2.refs_7_), channel_id=1, source_target_pairs={{0,3},{1,0},{2,1},{3,2},{4,7},{5,4},{6,5},{7,6},{8,11},{9,8},{10,9... | collective-permute-start | bytes 1966088 | tf_op jit(solution)/shard_map/ppermute | solution.py:61
  99.4 22.9 %collective-permute-start.7 = (bf16[128,2560]{1,0:T(8,128)(2,1)S(1)}, bf16[128,2560]{1,0:T(8,128)(2,1)S(1)}, u32[]{:S(2)}, u32[]{:S(2)}) collective-permute-start(bf16[128,2560]{1,0:T(8,128)(2,1)S(1)} %collective-permute-done.6.refs_5_), channel_id=1, source_target_pairs={{0,4},{1,5},{2,6},{3,7},{4,0},{5,1},{6,2},{7,3},{8,12},{9,13},{10,... | collective-permute-start | bytes 1966088 | tf_op jit(solution)/shard_map/ppermute | solution.py:61
  127.2 11.7 %collective-permute-start.29 = (bf16[512,384]{1,0:T(8,128)(2,1)S(1)}, bf16[512,384]{1,0:T(8,128)(2,1)S(1)}, u32[]{:S(2)}, u32[]{:S(2)}) collective-permute-start(bf16[512,384]{1,0:T(8,128)(2,1)S(1)} %get-tuple-element.29), channel_id=1, source_target_pairs={{0,8},{1,9},{2,10},{3,11},{4,12},{5,13},{6,14},{7,15},{8,0},{9,1},... | collective-permute-start | bytes 1179656 | tf_op jit(solution)/shard_map/ppermute | solution.py:61
  127.4 15.6 %collective-permute-start.30 = (bf16[512,384]{1,0:T(8,128)(2,1)S(1)}, bf16[512,384]{1,0:T(8,128)(2,1)S(1)}, u32[]{:S(2)}, u32[]{:S(2)}) collective-permute-start(bf16[512,384]{1,0:T(8,128)(2,1)S(1)} %get-tuple-element.30), channel_id=1, source_target_pairs={{0,248},{1,249},{2,250},{3,251},{4,252},{5,253},{6,254},{7,255},{8... | collective-permute-start | bytes 1179656 | tf_op jit(solution)/shard_map/ppermute | solution.py:61
  136.5 12.8 %collective-permute-start.31 = (bf16[512,384]{1,0:T(8,128)(2,1)S(1)}, bf16[512,384]{1,0:T(8,128)(2,1)S(1)}, u32[]{:S(2)}, u32[]{:S(2)}) collective-permute-start(bf16[512,384]{1,0:T(8,128)(2,1)S(1)} %get-tuple-element.35), channel_id=1, source_target_pairs={{0,8},{1,9},{2,10},{3,11},{4,12},{5,13},{6,14},{7,15},{8,0},{9,1},... | collective-permute-start | bytes 1179656 | tf_op jit(solution)/shard_map/ppermute | solution.py:61
  136.6 15.7 %collective-permute-start.32 = (bf16[512,384]{1,0:T(8,128)(2,1)S(1)}, bf16[512,384]{1,0:T(8,128)(2,1)S(1)}, u32[]{:S(2)}, u32[]{:S(2)}) collective-permute-start(bf16[512,384]{1,0:T(8,128)(2,1)S(1)} %get-tuple-element.36), channel_id=1, source_target_pairs={{0,248},{1,249},{2,250},{3,251},{4,252},{5,253},{6,254},{7,255},{8... | collective-permute-start | bytes 1179656 | tf_op jit(solution)/shard_map/ppermute | solution.py:61
  (19 other events, 198.8 us)

commit v6 on v5

--- a/solution.py
+++ b/solution.py
@@ -183,7 +183,7 @@
 CHUNKS = 4
 
 
-def _half_product(toks, w, row0, cols, t_buf, w_buf, t_sem, w_sem):
+def _half_product(toks, w, row0, cols, t_buf, w_buf, t_sem, w_sem, unroll=False):
     n = toks[0].shape[0]
     step = toks[0].shape[1] // CHUNKS
 
@@ -208,7 +208,11 @@
             acc[...] += jnp.dot(t_buf[k], w_buf[k], preferred_element_type=F32)
             return carry
 
-        lax.fori_loop(0, CHUNKS, one, 0)
+        if unroll:
+            for k in range(CHUNKS):
+                one(k, 0)
+        else:
+            lax.fori_loop(0, CHUNKS, one, 0)
 
     return product
 
@@ -262,7 +266,9 @@
         cols = (side * 384, 384)
         begin = pltpu.make_async_copy(acc_ref.at[:, pl.ds(*cols)], acc, a_sem)
         begin.start()
-        product = _half_product((t0, t1, t2), w_ref, half, cols, t_buf, w_buf, t_sem, w_sem)
+        product = _half_product(
+            (t0, t1, t2), w_ref, half, cols, t_buf, w_buf, t_sem, w_sem, unroll=True
+        )
 
         def row_of(place):
             dzl, dy = place

time: 157 us -> 157 us (level)
  transfers between devices with their start and end apart: 33 -> 33, of which waited for: 12 -> 12; matrix products, arithmetic and copies ran while one was open for 1% -> 1% of each run, Pallas kernels for 18% -> 17%
where the time goes in v6:
time: 157 us
  waiting for transfers between devices  77.3 us (49%)
  starting transfers between devices  38.9 us (25%)
  Pallas kernels  37 us (24%)
  local copies, waits for them, and re-layouts  3.39 us (2%)
    ppermute x33, waiting for transfers between devices, send(): lax.ppermute(a, AXES, _far_moves() if 'far' in step else _moves(**step))  77.3 us
    ppermute x33, starting transfers between devices, send(): lax.ppermute(a, AXES, _far_moves() if 'far' in step else _moves(**step))  38.9 us
    pallas_call x1, Pallas kernels, project(): pl.pallas_call(body, out_shape=[jax.ShapeDtypeStruct((rows, 768), BF16),...  11.4 us
    pallas_call x2, Pallas kernels, project_last(): pl.pallas_call(body, out_shape=[jax.ShapeDtypeStruct((TPD * TILE, 384), B...  9.93 us
    pallas_call x1, Pallas kernels, weigh(): pl.pallas_call(body, grid=(TPD,), out_shape=[jax.ShapeDtypeStruct((TPD, 3...  6.26 us
    pallas_call x1, Pallas kernels, mix(): pl.pallas_call(body, grid=(TPD,), out_shape=jax.ShapeDtypeStruct((TPD * T...  4.32 us
    pallas_call x1, Pallas kernels, project_half(): pl.pallas_call(body, out_shape=jax.ShapeDtypeStruct((rows, 768), F32), in...  3.91 us
  transfers between devices with their start and end apart: 33, of which 12 were waited for; matrix products, arithmetic and copies ran while one was open for 1% of the time, Pallas kernels for 17%

profile of v6, /device:TPU:32, one launch (start us, length us, event | category | flops | bytes accessed | tf_op | source)
XLA Modules:
  0.0 156.9 jit_solution(8371727912484780080)
XLA Ops:
  4.5 3.3 %collective-permute-start.11 = (bf16[320,384]{1,0:T(8,128)(2,1)S(1)}, bf16[320,384]{1,0:T(8,128)(2,1)S(1)}, u32[]{:S(2)}, u32[]{:S(2)}) collective-permute-start(bf16[320,384]{1,0:T(8,128)(2,1)S(1)} %shard_map.100.refs_8_), channel_id=1, source_target_pairs={{0,16},{1,17},{2,18},{3,19},{4,20},{5,21},{6,22},{7,23},{8,56},{9,... | collective-permute-start | bytes 737288 | tf_op jit(solution)/shard_map/ppermute | solution.py:61
  7.8 3.0 %collective-permute-start.5 = (bf16[128,5120]{1,0:T(8,128)(2,1)}, bf16[128,5120]{1,0:T(8,128)(2,1)S(1)}, u32[]{:S(2)}, u32[]{:S(2)}) collective-permute-start(bf16[128,5120]{1,0:T(8,128)(2,1)} %refs_1_.3), channel_id=1, source_target_pairs={{0,3},{1,0},{2,1},{3,2},{4,7},{5,4},{6,5},{7,6},{8,11},{9,8},{10,9... | collective-permute-start | bytes 3932168 | tf_op jit(solution)/shard_map/ppermute | solution.py:61
  13.0 3.7 %collective-permute-start.12 = (bf16[320,384]{1,0:T(8,128)(2,1)S(1)}, bf16[320,384]{1,0:T(8,128)(2,1)S(1)}, u32[]{:S(2)}, u32[]{:S(2)}) collective-permute-start(bf16[320,384]{1,0:T(8,128)(2,1)S(1)} %collective-permute-done.1.refs_9_), channel_id=1, source_target_pairs={{0,16},{1,17},{2,18},{3,19},{4,20},{5,21},{6,22},{7,23},{8,56},{9,... | collective-permute-start | bytes 737288 | tf_op jit(solution)/shard_map/ppermute | solution.py:61
  17.9 1.8 %collective-permute-start.13 = (bf16[320,384]{1,0:T(8,128)(2,1)S(1)}, bf16[320,384]{1,0:T(8,128)(2,1)S(1)}, u32[]{:S(2)}, u32[]{:S(2)}) collective-permute-start(bf16[320,384]{1,0:T(8,128)(2,1)S(1)} %collective-permute-done.11.refs_0_), channel_id=1, source_target_pairs={{0,16},{1,17},{2,18},{3,19},{4,20},{5,21},{6,22},{7,23},{8,56},{9,... | collective-permute-start | bytes 737288 | tf_op jit(solution)/shard_map/ppermute | solution.py:61
  19.7 4.4 %collective-permute-done.12.refs_1_ = bf16[320,384]{1,0:T(8,128)(2,1)S(1)} collective-permute-done((bf16[320,384]{1,0:T(8,128)(2,1)S(1)}, bf16[320,384]{1,0:T(8,128)(2,1)S(1)}, u32[]{:S(2)}, u32[]{:S(2)}) %collective-permute-start.12) | collective-permute-done | bytes 245792 | tf_op jit(solution)/shard_map/ppermute | solution.py:61
  24.6 4.4 %collective-permute-done.13.refs_2_ = bf16[320,384]{1,0:T(8,128)(2,1)S(1)} collective-permute-done((bf16[320,384]{1,0:T(8,128)(2,1)S(1)}, bf16[320,384]{1,0:T(8,128)(2,1)S(1)}, u32[]{:S(2)}, u32[]{:S(2)}) %collective-permute-start.13) | collective-permute-done | bytes 245792 | tf_op jit(solution)/shard_map/ppermute | solution.py:61
  33.1 9.7 %collective-permute-done.20.refs_18_ = bf16[960,384]{1,0:T(8,128)(2,1)S(1)} collective-permute-done((bf16[960,384]{1,0:T(8,128)(2,1)S(1)}, bf16[960,384]{1,0:T(8,128)(2,1)S(1)}, u32[]{:S(2)}, u32[]{:S(2)}) %collective-permute-start.20) | collective-permute-done | bytes 737312 | tf_op jit(solution)/shard_map/ppermute | solution.py:61
  43.7 6.1 %collective-permute-done.10.refs_6_ = bf16[128,2560]{1,0:T(8,128)(2,1)S(1)} collective-permute-done((bf16[128,2560]{1,0:T(8,128)(2,1)S(1)}, bf16[128,2560]{1,0:T(8,128)(2,1)S(1)}, u32[]{:S(2)}, u32[]{:S(2)}) %collective-permute-start.10) | collective-permute-done | bytes 655392 | tf_op jit(solution)/shard_map/ppermute | solution.py:61
  51.7 12.8 %collective-permute-done.8.refs_2_ = bf16[128,5120]{1,0:T(8,128)(2,1)S(1)} collective-permute-done((bf16[128,5120]{1,0:T(8,128)(2,1)S(1)}, bf16[128,5120]{1,0:T(8,128)(2,1)S(1)}, u32[]{:S(2)}, u32[]{:S(2)}) %collective-permute-start.8) | collective-permute-done | bytes 1310752 | tf_op jit(solution)/shard_map/ppermute | solution.py:61
  67.3 11.2 %collective-permute-done.26.t0 = bf16[128,2560]{1,0:T(8,128)(2,1)S(1)} collective-permute-done((bf16[128,2560]{1,0:T(8,128)(2,1)S(1)}, bf16[128,2560]{1,0:T(8,128)(2,1)S(1)}, u32[]{:S(2)}, u32[]{:S(2)}) %collective-permute-start.26) | collective-permute-done | bytes 655392 | tf_op jit(solution)/shard_map/ppermute | solution.py:61
  80.9 11.1 %collective-permute-done.9.refs_4_ = bf16[128,2560]{1,0:T(8,128)(2,1)S(1)} collective-permute-done((bf16[128,2560]{1,0:T(8,128)(2,1)S(1)}, bf16[128,2560]{1,0:T(8,128)(2,1)S(1)}, u32[]{:S(2)}, u32[]{:S(2)}) %collective-permute-start.9) | collective-permute-done | bytes 655392 | tf_op jit(solution)/shard_map/ppermute | solution.py:61
  92.7 3.5 %collective-permute-done.6.refs_5_ = bf16[128,2560]{1,0:T(8,128)(2,1)S(1)} collective-permute-done((bf16[128,2560]{1,0:T(8,128)(2,1)S(1)}, bf16[128,2560]{1,0:T(8,128)(2,1)S(1)}, u32[]{:S(2)}, u32[]{:S(2)}) %collective-permute-start.6) | collective-permute-done | bytes 655392 | tf_op jit(solution)/shard_map/ppermute | solution.py:61
  96.3 3.0 %collective-permute-start.4 = (bf16[128,2560]{1,0:T(8,128)(2,1)S(1)}, bf16[128,2560]{1,0:T(8,128)(2,1)S(1)}, u32[]{:S(2)}, u32[]{:S(2)}) collective-permute-start(bf16[128,2560]{1,0:T(8,128)(2,1)S(1)} %collective-permute-done.2.refs_7_), channel_id=1, source_target_pairs={{0,3},{1,0},{2,1},{3,2},{4,7},{5,4},{6,5},{7,6},{8,11},{9,8},{10,9... | collective-permute-start | bytes 1966088 | tf_op jit(solution)/shard_map/ppermute | solution.py:61
  100.3 11.4 %shard_map.102 = (bf16[640,768]{1,0:T(8,128)(2,1)S(1)}, bf16[4,1280,768]{2,1,0:T(8,128)(2,1)}) custom-call(s32[7]{0:T(128)S(1)} %stack.27.refs_0_.pos_ref, bf16[128,5120]{1,0:T(8,128)(2,1)S(1)} %copy-done, bf16[128,5120]{1,0:T(8,128)(2,1)S(1)} %collective-permute-done.8.refs_2_, bf16[128,5120]{1,0:T(8,128)(2,1)S(1)} %collective-permute-done.5.refs_3_, ...), custom_call_target="tpu_custom_call" | custom-call | tf_op jit(solution)/shard_map/pallas_call | solution.py:163
  111.8 3.9 %shard_map.103.acc_ref = f32[384,768]{1,0:T(8,128)S(1)} custom-call(bf16[128,2560]{1,0:T(8,128)(2,1)S(1)} %collective-permute-done.26.t0, bf16[128,2560]{1,0:T(8,128)(2,1)S(1)} %collective-permute-done.27.t1, bf16[128,2560]{1,0:T(8,128)(2,1)S(1)} %collective-permute-done.28.t2, bf16[5120,768]{1,0:T(8,128)(2,1)} %bitcast.28), custom_call_target="tpu_custom_call" | custom-call | tf_op jit(solution)/shard_map/pallas_call | solution.py:238
  115.7 6.6 %collective-permute-done.4.t1 = bf16[128,2560]{1,0:T(8,128)(2,1)S(1)} collective-permute-done((bf16[128,2560]{1,0:T(8,128)(2,1)S(1)}, bf16[128,2560]{1,0:T(8,128)(2,1)S(1)}, u32[]{:S(2)}, u32[]{:S(2)}) %collective-permute-start.4) | collective-permute-done | bytes 655392 | tf_op jit(solution)/shard_map/ppermute | solution.py:61
  122.3 5.0 %shard_map.104 = (bf16[1024,384]{1,0:T(8,128)(2,1)S(1)}, bf16[512,384]{1,0:T(8,128)(2,1)S(1)}, bf16[512,384]{1,0:T(8,128)(2,1)S(1)}) custom-call(s32[7]{0:T(128)S(1)} %stack.27.refs_0_.pos_ref, bf16[128,2560]{1,0:T(8,128)(2,1)S(1)} %collective-permute-done.3.t0, bf16[128,2560]{1,0:T(8,128)(2,1)S(1)} %collective-permute-done.4.t1, ...), custom_call_target="tpu_custom_call" | custom-call | tf_op jit(solution)/shard_map/pallas_call | solution.py:315
  127.4 4.1 %collective-permute-start.30 = (bf16[512,384]{1,0:T(8,128)(2,1)S(1)}, bf16[512,384]{1,0:T(8,128)(2,1)S(1)}, u32[]{:S(2)}, u32[]{:S(2)}) collective-permute-start(bf16[512,384]{1,0:T(8,128)(2,1)S(1)} %get-tuple-element.30), channel_id=1, source_target_pairs={{0,248},{1,249},{2,250},{3,251},{4,252},{5,253},{6,254},{7,255},{8... | collective-permute-start | bytes 1179656 | tf_op jit(solution)/shard_map/ppermute | solution.py:61
  131.5 5.0 %shard_map.106 = (bf16[1024,384]{1,0:T(8,128)(2,1)S(1)}, bf16[512,384]{1,0:T(8,128)(2,1)S(1)}, bf16[512,384]{1,0:T(8,128)(2,1)S(1)}) custom-call(s32[7]{0:T(128)S(1)} %stack.27.refs_0_.pos_ref, bf16[128,2560]{1,0:T(8,128)(2,1)S(1)} %collective-permute-done.3.t0, bf16[128,2560]{1,0:T(8,128)(2,1)S(1)} %collective-permute-done.4.t1, ...), custom_call_target="tpu_custom_call" | custom-call | tf_op jit(solution)/shard_map/pallas_call | solution.py:315
  136.9 2.4 %collective-permute-start.32 = (bf16[512,384]{1,0:T(8,128)(2,1)S(1)}, bf16[512,384]{1,0:T(8,128)(2,1)S(1)}, u32[]{:S(2)}, u32[]{:S(2)}) collective-permute-start(bf16[512,384]{1,0:T(8,128)(2,1)S(1)} %get-tuple-element.36), channel_id=1, source_target_pairs={{0,248},{1,249},{2,250},{3,251},{4,252},{5,253},{6,254},{7,255},{8... | collective-permute-start | bytes 1179656 | tf_op jit(solution)/shard_map/ppermute | solution.py:61
  139.3 3.7 %collective-permute-done.30.far_ref = bf16[512,384]{1,0:T(8,128)(2,1)S(1)} collective-permute-done((bf16[512,384]{1,0:T(8,128)(2,1)S(1)}, bf16[512,384]{1,0:T(8,128)(2,1)S(1)}, u32[]{:S(2)}, u32[]{:S(2)}) %collective-permute-start.30) | collective-permute-done | bytes 393248 | tf_op jit(solution)/shard_map/ppermute | solution.py:61
  143.0 6.3 %shard_map.105 = (bf16[4,3,256,768]{3,2,1,0:T(8,128)(2,1)S(1)}, f32[1024,384]{1,0:T(8,128)S(1)}) custom-call(s32[7]{0:T(128)S(1)} %stack.27.refs_0_.pos_ref, bf16[1024,384]{1,0:T(8,128)(2,1)S(1)} %copy-done.1, bf16[1024,384]{1,0:T(8,128)(2,1)S(1)} %get-tuple-element.28.full_ref, bf16[512,384]{1,0:T(8,128)(2,1)S(1)} %collective-permute-done.29.near_ref, ...), custom_call_target="tpu_custom_call" | custom-call | tf_op jit(solution)/shard_map/pallas_call | solution.py:426
  149.3 3.3 %collective-permute-done.32.far_ref = bf16[512,384]{1,0:T(8,128)(2,1)S(1)} collective-permute-done((bf16[512,384]{1,0:T(8,128)(2,1)S(1)}, bf16[512,384]{1,0:T(8,128)(2,1)S(1)}, u32[]{:S(2)}, u32[]{:S(2)}) %collective-permute-start.32) | collective-permute-done | bytes 393248 | tf_op jit(solution)/shard_map/ppermute | solution.py:61
  152.6 4.3 %shard_map.107 = bf16[1024,384]{1,0:T(8,128)(2,1)} custom-call(s32[7]{0:T(128)S(1)} %stack.27.refs_0_.pos_ref, bf16[4,3,256,768]{3,2,1,0:T(8,128)(2,1)S(1)} %get-tuple-element.31.prob_ref, f32[1024,384]{1,0:T(8,128)S(1)} %get-tuple-element.32.total_ref, bf16[1024,384]{1,0:T(8,128)(2,1)S(1)} %get-tuple-element.34.full_ref, ...), custom_call_target="tpu_custom_call" | custom-call | tf_op jit(solution)/shard_map/pallas_call | solution.py:458
  (74 shorter events, 22.8 us)
Async XLA Ops:
  4.5 13.4 %collective-permute-start.11 = (bf16[320,384]{1,0:T(8,128)(2,1)S(1)}, bf16[320,384]{1,0:T(8,128)(2,1)S(1)}, u32[]{:S(2)}, u32[]{:S(2)}) collective-permute-start(bf16[320,384]{1,0:T(8,128)(2,1)S(1)} %shard_map.100.refs_8_), channel_id=1, source_target_pairs={{0,16},{1,17},{2,18},{3,19},{4,20},{5,21},{6,22},{7,23},{8,56},{9,... | collective-permute-start | bytes 737288 | tf_op jit(solution)/shard_map/ppermute | solution.py:61
  7.8 42.3 %collective-permute-start.5 = (bf16[128,5120]{1,0:T(8,128)(2,1)}, bf16[128,5120]{1,0:T(8,128)(2,1)S(1)}, u32[]{:S(2)}, u32[]{:S(2)}) collective-permute-start(bf16[128,5120]{1,0:T(8,128)(2,1)} %refs_1_.3), channel_id=1, source_target_pairs={{0,3},{1,0},{2,1},{3,2},{4,7},{5,4},{6,5},{7,6},{8,11},{9,8},{10,9... | collective-permute-start | bytes 3932168 | tf_op jit(solution)/shard_map/ppermute | solution.py:61
  19.7 11.8 %collective-permute-start.15 = (bf16[320,384]{1,0:T(8,128)(2,1)S(1)}, bf16[320,384]{1,0:T(8,128)(2,1)S(1)}, u32[]{:S(2)}, u32[]{:S(2)}) collective-permute-start(bf16[320,384]{1,0:T(8,128)(2,1)S(1)} %collective-permute-done.refs_12_), channel_id=1, source_target_pairs={{0,8},{1,9},{2,10},{3,11},{4,12},{5,13},{6,14},{7,15},{8,0},{9,1},... | collective-permute-start | bytes 737288 | tf_op jit(solution)/shard_map/ppermute | solution.py:61
  30.0 12.8 %collective-permute-start.20 = (bf16[960,384]{1,0:T(8,128)(2,1)S(1)}, bf16[960,384]{1,0:T(8,128)(2,1)S(1)}, u32[]{:S(2)}, u32[]{:S(2)}) collective-permute-start(bf16[960,384]{1,0:T(8,128)(2,1)S(1)} %shard_map.101.refs_10_), channel_id=1, source_target_pairs={{0,64},{1,65},{2,66},{3,67},{4,68},{5,69},{6,70},{7,71},{8,200},{9... | collective-permute-start | bytes 2211848 | tf_op jit(solution)/shard_map/ppermute | solution.py:61
  31.5 32.9 %collective-permute-start.8 = (bf16[128,5120]{1,0:T(8,128)(2,1)S(1)}, bf16[128,5120]{1,0:T(8,128)(2,1)S(1)}, u32[]{:S(2)}, u32[]{:S(2)}) collective-permute-start(bf16[128,5120]{1,0:T(8,128)(2,1)S(1)} %copy-done), channel_id=1, source_target_pairs={{0,1},{1,2},{2,3},{3,0},{4,5},{5,6},{6,7},{7,4},{8,9},{9,10},{10,1... | collective-permute-start | bytes 3932168 | tf_op jit(solution)/shard_map/ppermute | solution.py:61
  33.1 16.8 %collective-permute-start.10 = (bf16[128,2560]{1,0:T(8,128)(2,1)S(1)}, bf16[128,2560]{1,0:T(8,128)(2,1)S(1)}, u32[]{:S(2)}, u32[]{:S(2)}) collective-permute-start(bf16[128,2560]{1,0:T(8,128)(2,1)S(1)} %get-tuple-element.23), channel_id=1, source_target_pairs={{0,4},{1,5},{2,6},{3,7},{4,0},{5,1},{6,2},{7,3},{8,12},{9,13},{10,... | collective-permute-start | bytes 1966088 | tf_op jit(solution)/shard_map/ppermute | solution.py:61
  42.7 21.7 %collective-permute-start.24 = (bf16[960,384]{1,0:T(8,128)(2,1)S(1)}, bf16[960,384]{1,0:T(8,128)(2,1)S(1)}, u32[]{:S(2)}, u32[]{:S(2)}) collective-permute-start(bf16[960,384]{1,0:T(8,128)(2,1)S(1)} %collective-permute-done.20.refs_18_), channel_id=1, source_target_pairs={{0,64},{1,65},{2,66},{3,67},{4,68},{5,69},{6,70},{7,71},{8,200},{9... | collective-permute-start | bytes 2211848 | tf_op jit(solution)/shard_map/ppermute | solution.py:61
  43.0 22.0 %collective-permute-start.22 = (bf16[960,384]{1,0:T(8,128)(2,1)S(1)}, bf16[960,384]{1,0:T(8,128)(2,1)S(1)}, u32[]{:S(2)}, u32[]{:S(2)}) collective-permute-start(bf16[960,384]{1,0:T(8,128)(2,1)S(1)} %collective-permute-done.14.refs_11_), channel_id=1, source_target_pairs={{0,64},{1,65},{2,66},{3,67},{4,68},{5,69},{6,70},{7,71},{8,200},{9... | collective-permute-start | bytes 2211848 | tf_op jit(solution)/shard_map/ppermute | solution.py:61
  49.8 15.9 %collective-permute-start.2 = (bf16[128,2560]{1,0:T(8,128)(2,1)S(1)}, bf16[128,2560]{1,0:T(8,128)(2,1)S(1)}, u32[]{:S(2)}, u32[]{:S(2)}) collective-permute-start(bf16[128,2560]{1,0:T(8,128)(2,1)S(1)} %get-tuple-element.22), channel_id=1, source_target_pairs={{0,4},{1,5},{2,6},{3,7},{4,0},{5,1},{6,2},{7,3},{8,12},{9,13},{10,... | collective-permute-start | bytes 1966088 | tf_op jit(solution)/shard_map/ppermute | solution.py:61
  50.1 28.4 %collective-permute-start.26 = (bf16[128,2560]{1,0:T(8,128)(2,1)S(1)}, bf16[128,2560]{1,0:T(8,128)(2,1)S(1)}, u32[]{:S(2)}, u32[]{:S(2)}) collective-permute-start(bf16[128,2560]{1,0:T(8,128)(2,1)S(1)} %collective-permute-done.10.refs_6_), channel_id=1, source_target_pairs={{0,1},{1,2},{2,3},{3,0},{4,5},{5,6},{6,7},{7,4},{8,9},{9,10},{10,1... | collective-permute-start | bytes 1966088 | tf_op jit(solution)/shard_map/ppermute | solution.py:61
  64.5 15.7 %collective-permute-start.21 = (bf16[960,384]{1,0:T(8,128)(2,1)S(1)}, bf16[960,384]{1,0:T(8,128)(2,1)S(1)}, u32[]{:S(2)}, u32[]{:S(2)}) collective-permute-start(bf16[960,384]{1,0:T(8,128)(2,1)S(1)} %collective-permute-done.20.refs_18_), channel_id=1, source_target_pairs={{0,8},{1,9},{2,10},{3,11},{4,12},{5,13},{6,14},{7,15},{8,0},{9,1},... | collective-permute-start | bytes 2211848 | tf_op jit(solution)/shard_map/ppermute | solution.py:61
  64.5 31.9 %collective-permute-start.25 = (bf16[960,384]{1,0:T(8,128)(2,1)S(1)}, bf16[960,384]{1,0:T(8,128)(2,1)S(1)}, u32[]{:S(2)}, u32[]{:S(2)}) collective-permute-start(bf16[960,384]{1,0:T(8,128)(2,1)S(1)} %collective-permute-done.24.refs_22_), channel_id=1, source_target_pairs={{0,8},{1,9},{2,10},{3,11},{4,12},{5,13},{6,14},{7,15},{8,0},{9,1},... | collective-permute-start | bytes 2211848 | tf_op jit(solution)/shard_map/ppermute | solution.py:61
  65.0 34.4 %collective-permute-start.23 = (bf16[960,384]{1,0:T(8,128)(2,1)S(1)}, bf16[960,384]{1,0:T(8,128)(2,1)S(1)}, u32[]{:S(2)}, u32[]{:S(2)}) collective-permute-start(bf16[960,384]{1,0:T(8,128)(2,1)S(1)} %collective-permute-done.22.refs_20_), channel_id=1, source_target_pairs={{0,8},{1,9},{2,10},{3,11},{4,12},{5,13},{6,14},{7,15},{8,0},{9,1},... | collective-permute-start | bytes 2211848 | tf_op jit(solution)/shard_map/ppermute | solution.py:61
  65.8 26.3 %collective-permute-start.9 = (bf16[128,2560]{1,0:T(8,128)(2,1)S(1)}, bf16[128,2560]{1,0:T(8,128)(2,1)S(1)}, u32[]{:S(2)}, u32[]{:S(2)}) collective-permute-start(bf16[128,2560]{1,0:T(8,128)(2,1)S(1)} %slice.17), channel_id=1, source_target_pairs={{0,1},{1,2},{2,3},{3,0},{4,5},{5,6},{6,7},{7,4},{8,9},{9,10},{10,1... | collective-permute-start | bytes 1966088 | tf_op jit(solution)/shard_map/ppermute | solution.py:61
  78.5 17.6 %collective-permute-start.6 = (bf16[128,2560]{1,0:T(8,128)(2,1)S(1)}, bf16[128,2560]{1,0:T(8,128)(2,1)S(1)}, u32[]{:S(2)}, u32[]{:S(2)}) collective-permute-start(bf16[128,2560]{1,0:T(8,128)(2,1)S(1)} %slice.16), channel_id=1, source_target_pairs={{0,3},{1,0},{2,1},{3,2},{4,7},{5,4},{6,5},{7,6},{8,11},{9,8},{10,9... | collective-permute-start | bytes 1966088 | tf_op jit(solution)/shard_map/ppermute | solution.py:61
  80.2 31.5 %collective-permute-start.27 = (bf16[128,2560]{1,0:T(8,128)(2,1)S(1)}, bf16[128,2560]{1,0:T(8,128)(2,1)S(1)}, u32[]{:S(2)}, u32[]{:S(2)}) collective-permute-start(bf16[128,2560]{1,0:T(8,128)(2,1)S(1)} %collective-permute-done.10.refs_6_), channel_id=1, source_target_pairs={{0,3},{1,0},{2,1},{3,2},{4,7},{5,4},{6,5},{7,6},{8,11},{9,8},{10,9... | collective-permute-start | bytes 1966088 | tf_op jit(solution)/shard_map/ppermute | solution.py:61
  92.0 19.7 %collective-permute-start.28 = (bf16[128,2560]{1,0:T(8,128)(2,1)S(1)}, bf16[128,2560]{1,0:T(8,128)(2,1)S(1)}, u32[]{:S(2)}, u32[]{:S(2)}) collective-permute-start(bf16[128,2560]{1,0:T(8,128)(2,1)S(1)} %collective-permute-done.9.refs_4_), channel_id=1, source_target_pairs={{0,4},{1,5},{2,6},{3,7},{4,0},{5,1},{6,2},{7,3},{8,12},{9,13},{10,... | collective-permute-start | bytes 1966088 | tf_op jit(solution)/shard_map/ppermute | solution.py:61
  96.1 19.6 %collective-permute-start.3 = (bf16[128,2560]{1,0:T(8,128)(2,1)S(1)}, bf16[128,2560]{1,0:T(8,128)(2,1)S(1)}, u32[]{:S(2)}, u32[]{:S(2)}) collective-permute-start(bf16[128,2560]{1,0:T(8,128)(2,1)S(1)} %collective-permute-done.2.refs_7_), channel_id=1, source_target_pairs={{0,1},{1,2},{2,3},{3,0},{4,5},{5,6},{6,7},{7,4},{8,9},{9,10},{10,1... | collective-permute-start | bytes 1966088 | tf_op jit(solution)/shard_map/ppermute | solution.py:61
  96.3 25.9 %collective-permute-start.4 = (bf16[128,2560]{1,0:T(8,128)(2,1)S(1)}, bf16[128,2560]{1,0:T(8,128)(2,1)S(1)}, u32[]{:S(2)}, u32[]{:S(2)}) collective-permute-start(bf16[128,2560]{1,0:T(8,128)(2,1)S(1)} %collective-permute-done.2.refs_7_), channel_id=1, source_target_pairs={{0,3},{1,0},{2,1},{3,2},{4,7},{5,4},{6,5},{7,6},{8,11},{9,8},{10,9... | collective-permute-start | bytes 1966088 | tf_op jit(solution)/shard_map/ppermute | solution.py:61
  99.4 22.9 %collective-permute-start.7 = (bf16[128,2560]{1,0:T(8,128)(2,1)S(1)}, bf16[128,2560]{1,0:T(8,128)(2,1)S(1)}, u32[]{:S(2)}, u32[]{:S(2)}) collective-permute-start(bf16[128,2560]{1,0:T(8,128)(2,1)S(1)} %collective-permute-done.6.refs_5_), channel_id=1, source_target_pairs={{0,4},{1,5},{2,6},{3,7},{4,0},{5,1},{6,2},{7,3},{8,12},{9,13},{10,... | collective-permute-start | bytes 1966088 | tf_op jit(solution)/shard_map/ppermute | solution.py:61
  127.3 12.0 %collective-permute-start.29 = (bf16[512,384]{1,0:T(8,128)(2,1)S(1)}, bf16[512,384]{1,0:T(8,128)(2,1)S(1)}, u32[]{:S(2)}, u32[]{:S(2)}) collective-permute-start(bf16[512,384]{1,0:T(8,128)(2,1)S(1)} %get-tuple-element.29), channel_id=1, source_target_pairs={{0,8},{1,9},{2,10},{3,11},{4,12},{5,13},{6,14},{7,15},{8,0},{9,1},... | collective-permute-start | bytes 1179656 | tf_op jit(solution)/shard_map/ppermute | solution.py:61
  127.4 15.6 %collective-permute-start.30 = (bf16[512,384]{1,0:T(8,128)(2,1)S(1)}, bf16[512,384]{1,0:T(8,128)(2,1)S(1)}, u32[]{:S(2)}, u32[]{:S(2)}) collective-permute-start(bf16[512,384]{1,0:T(8,128)(2,1)S(1)} %get-tuple-element.30), channel_id=1, source_target_pairs={{0,248},{1,249},{2,250},{3,251},{4,252},{5,253},{6,254},{7,255},{8... | collective-permute-start | bytes 1179656 | tf_op jit(solution)/shard_map/ppermute | solution.py:61
  136.5 12.8 %collective-permute-start.31 = (bf16[512,384]{1,0:T(8,128)(2,1)S(1)}, bf16[512,384]{1,0:T(8,128)(2,1)S(1)}, u32[]{:S(2)}, u32[]{:S(2)}) collective-permute-start(bf16[512,384]{1,0:T(8,128)(2,1)S(1)} %get-tuple-element.35), channel_id=1, source_target_pairs={{0,8},{1,9},{2,10},{3,11},{4,12},{5,13},{6,14},{7,15},{8,0},{9,1},... | collective-permute-start | bytes 1179656 | tf_op jit(solution)/shard_map/ppermute | solution.py:61
  136.9 15.7 %collective-permute-start.32 = (bf16[512,384]{1,0:T(8,128)(2,1)S(1)}, bf16[512,384]{1,0:T(8,128)(2,1)S(1)}, u32[]{:S(2)}, u32[]{:S(2)}) collective-permute-start(bf16[512,384]{1,0:T(8,128)(2,1)S(1)} %get-tuple-element.36), channel_id=1, source_target_pairs={{0,248},{1,249},{2,250},{3,251},{4,252},{5,253},{6,254},{7,255},{8... | collective-permute-start | bytes 1179656 | tf_op jit(solution)/shard_map/ppermute | solution.py:61
  (19 other events, 198.8 us)

commit v7 on v6

--- a/solution.py
+++ b/solution.py
@@ -180,7 +180,7 @@
     )(pos, *toks, *[p[0] for p in pieces])
 
 
-CHUNKS = 4
+CHUNKS = 2
 
 
 def _half_product(toks, w, row0, cols, t_buf, w_buf, t_sem, w_sem, unroll=False):
@@ -261,7 +261,7 @@
     rows = n * len(toks)
 
     def body(pos_ref, t0, t1, t2, w_ref, acc_ref, done_ref, slot, neighbour, first,
-             full, near, far, t_buf, w_buf, t_sem, w_sem, acc, wide, a_sem):
+             full, near, far, t_buf, w_buf, t_sem, w_sem, acc, wide, a_sem, picks):
         block, zl, y, blocks = pos_ref[3], pos_ref[4], pos_ref[5], pos_ref[6]
         cols = (side * 384, 384)
         begin = pltpu.make_async_copy(acc_ref.at[:, pl.ds(*cols)], acc, a_sem)
@@ -278,17 +278,11 @@
             part = done_ref[i * n : (i + 1) * n, side * 384 : side * 384 + 384]
             full[pl.ds(row_of(place), n), :] = part
             wide[pl.ds(row_of(place), n), :] = part.astype(F32)
-        begin.wait()
-        product(acc)
-        for i, place in enumerate(places):
-            part = acc[i * n : (i + 1) * n, :].astype(BF16)
-            full[pl.ds(row_of(place), n), :] = part
-            wide[pl.ds(row_of(place), n), :] = part.astype(F32)
         up = 1 - 2 * pos_ref[2]
-        for out, step in ((far, -up), (near, up)):
+        for d, step in enumerate((-up, up)):
             target = (block + step + blocks) % blocks
 
-            def pick(p, carry, out=out, target=target):
+            def find(p, carry, d=d, target=target):
                 tile = _tile_at(slot, target, p)
                 seen = jnp.int32(0)
                 starts = [jnp.int32(0), jnp.int32(0)]
@@ -301,16 +295,29 @@
                         starts[o] = jnp.where(take, row, starts[o])
                     seen = seen + hit.astype(jnp.int32)
                 for o in range(2):
-                    al = pl.multiple_of(starts[o] // 8 * 8, 8)
-                    rem = starts[o] - al
-                    window = pltpu.roll(
-                        wide[pl.ds(al, SLAB + 8), :], (SLAB + 8 - rem) % (SLAB + 8), 0
-                    )
-                    at = pl.multiple_of((p * 2 + o) * SLAB, SLAB)
-                    out[pl.ds(at, SLAB), :] = window[:SLAB].astype(BF16)
+                    picks[d * TPD * 2 + p * 2 + o] = starts[o]
                 return carry
 
-            lax.fori_loop(0, TPD, pick, 0)
+            lax.fori_loop(0, TPD, find, 0)
+        begin.wait()
+        product(acc)
+        for i, place in enumerate(places):
+            part = acc[i * n : (i + 1) * n, :].astype(BF16)
+            full[pl.ds(row_of(place), n), :] = part
+            wide[pl.ds(row_of(place), n), :] = part.astype(F32)
+        for d, out in enumerate((far, near)):
+
+            def pick(i, carry, d=d, out=out):
+                start = picks[d * TPD * 2 + i]
+                al = pl.multiple_of(start // 8 * 8, 8)
+                window = pltpu.roll(
+                    wide[pl.ds(al, SLAB + 8), :], (SLAB + 8 - (start - al)) % (SLAB + 8), 0
+                )
+                at = pl.multiple_of(i * SLAB, SLAB)
+                out[pl.ds(at, SLAB), :] = window[:SLAB].astype(BF16)
+                return carry
+
+            lax.fori_loop(0, TPD * 2, pick, 0)
 
     return pl.pallas_call(
         body,
@@ -320,7 +327,7 @@
         out_specs=[VM] * 3,
         scratch_shapes=_half_scratch(rows, half, 384, 3)
         + [pltpu.VMEM((rows, 384), F32), pltpu.VMEM((TPD * TILE + 8, 384), F32)]
-        + [pltpu.SemaphoreType.DMA],
+        + [pltpu.SemaphoreType.DMA, pltpu.SMEM((TPD * 4,), jnp.int32)],
         compiler_params=pltpu.CompilerParams(vmem_limit_bytes=48 * MIB),
     )(pos, *toks, w, acc_in, done, *tables)
 

time: 157 us -> 155 us (0.987); the launches traced: 157 us -> 153 us
  Pallas kernels: 37 us -> 34.9 us
  waiting for transfers between devices: 77.3 us -> 75.4 us
    ppermute x33, waiting for transfers between devices: 77.3 us -> 75.4 us  [send(): lax.ppermute(a, AXES, _far_moves() if 'far' in step else _moves(**step))]
    pallas_call x2, Pallas kernels: 9.93 us -> 8.18 us  [project_last(): pl.pallas_call(body, out_shape=[jax.ShapeDtypeStruct((TPD * TILE, 384), B...]
  transfers between devices with their start and end apart: 33 -> 33, of which waited for: 12 -> 11; matrix products, arithmetic and copies ran while one was open for 1% -> 1% of each run, Pallas kernels for 17% -> 17%
where the time goes in v7:
time: 155 us; the launch traced here: 153 us
  waiting for transfers between devices  75.4 us (49%)
  starting transfers between devices  38.7 us (25%)
  Pallas kernels  34.9 us (23%)
  local copies, waits for them, and re-layouts  3.39 us (2%)
    ppermute x33, waiting for transfers between devices, send(): lax.ppermute(a, AXES, _far_moves() if 'far' in step else _moves(**step))  75.4 us
    ppermute x33, starting transfers between devices, send(): lax.ppermute(a, AXES, _far_moves() if 'far' in step else _moves(**step))  38.7 us
    pallas_call x1, Pallas kernels, project(): pl.pallas_call(body, out_shape=[jax.ShapeDtypeStruct((rows, 768), BF16),...  11.4 us
    pallas_call x2, Pallas kernels, project_last(): pl.pallas_call(body, out_shape=[jax.ShapeDtypeStruct((TPD * TILE, 384), B...  8.18 us
    pallas_call x1, Pallas kernels, weigh(): pl.pallas_call(body, grid=(TPD,), out_shape=[jax.ShapeDtypeStruct((TPD, 3...  6.26 us
    pallas_call x1, Pallas kernels, mix(): pl.pallas_call(body, grid=(TPD,), out_shape=jax.ShapeDtypeStruct((TPD * T...  4.37 us
    pallas_call x1, Pallas kernels, project_half(): pl.pallas_call(body, out_shape=jax.ShapeDtypeStruct((rows, 768), F32), in...  3.52 us
  transfers between devices with their start and end apart: 33, of which 11 were waited for; matrix products, arithmetic and copies ran while one was open for 1% of the time, Pallas kernels for 17%

profile of v7, /device:TPU:32, one launch (start us, length us, event | category | flops | bytes accessed | tf_op | source)
XLA Modules:
  0.0 152.7 jit_solution(11176795592803261651)
XLA Ops:
  4.5 3.3 %collective-permute-start.11 = (bf16[320,384]{1,0:T(8,128)(2,1)S(1)}, bf16[320,384]{1,0:T(8,128)(2,1)S(1)}, u32[]{:S(2)}, u32[]{:S(2)}) collective-permute-start(bf16[320,384]{1,0:T(8,128)(2,1)S(1)} %shard_map.100.refs_8_), channel_id=1, source_target_pairs={{0,16},{1,17},{2,18},{3,19},{4,20},{5,21},{6,22},{7,23},{8,56},{9,... | collective-permute-start | bytes 737288 | tf_op jit(solution)/shard_map/ppermute | solution.py:61
  7.8 3.0 %collective-permute-start.5 = (bf16[128,5120]{1,0:T(8,128)(2,1)}, bf16[128,5120]{1,0:T(8,128)(2,1)S(1)}, u32[]{:S(2)}, u32[]{:S(2)}) collective-permute-start(bf16[128,5120]{1,0:T(8,128)(2,1)} %refs_1_.3), channel_id=1, source_target_pairs={{0,3},{1,0},{2,1},{3,2},{4,7},{5,4},{6,5},{7,6},{8,11},{9,8},{10,9... | collective-permute-start | bytes 3932168 | tf_op jit(solution)/shard_map/ppermute | solution.py:61
  13.0 3.7 %collective-permute-start.12 = (bf16[320,384]{1,0:T(8,128)(2,1)S(1)}, bf16[320,384]{1,0:T(8,128)(2,1)S(1)}, u32[]{:S(2)}, u32[]{:S(2)}) collective-permute-start(bf16[320,384]{1,0:T(8,128)(2,1)S(1)} %collective-permute-done.1.refs_9_), channel_id=1, source_target_pairs={{0,16},{1,17},{2,18},{3,19},{4,20},{5,21},{6,22},{7,23},{8,56},{9,... | collective-permute-start | bytes 737288 | tf_op jit(solution)/shard_map/ppermute | solution.py:61
  17.9 1.8 %collective-permute-start.13 = (bf16[320,384]{1,0:T(8,128)(2,1)S(1)}, bf16[320,384]{1,0:T(8,128)(2,1)S(1)}, u32[]{:S(2)}, u32[]{:S(2)}) collective-permute-start(bf16[320,384]{1,0:T(8,128)(2,1)S(1)} %collective-permute-done.11.refs_0_), channel_id=1, source_target_pairs={{0,16},{1,17},{2,18},{3,19},{4,20},{5,21},{6,22},{7,23},{8,56},{9,... | collective-permute-start | bytes 737288 | tf_op jit(solution)/shard_map/ppermute | solution.py:61
  19.7 4.4 %collective-permute-done.12.refs_1_ = bf16[320,384]{1,0:T(8,128)(2,1)S(1)} collective-permute-done((bf16[320,384]{1,0:T(8,128)(2,1)S(1)}, bf16[320,384]{1,0:T(8,128)(2,1)S(1)}, u32[]{:S(2)}, u32[]{:S(2)}) %collective-permute-start.12) | collective-permute-done | bytes 245792 | tf_op jit(solution)/shard_map/ppermute | solution.py:61
  24.6 4.4 %collective-permute-done.13.refs_2_ = bf16[320,384]{1,0:T(8,128)(2,1)S(1)} collective-permute-done((bf16[320,384]{1,0:T(8,128)(2,1)S(1)}, bf16[320,384]{1,0:T(8,128)(2,1)S(1)}, u32[]{:S(2)}, u32[]{:S(2)}) %collective-permute-start.13) | collective-permute-done | bytes 245792 | tf_op jit(solution)/shard_map/ppermute | solution.py:61
  33.1 9.7 %collective-permute-done.20.refs_18_ = bf16[960,384]{1,0:T(8,128)(2,1)S(1)} collective-permute-done((bf16[960,384]{1,0:T(8,128)(2,1)S(1)}, bf16[960,384]{1,0:T(8,128)(2,1)S(1)}, u32[]{:S(2)}, u32[]{:S(2)}) %collective-permute-start.20) | collective-permute-done | bytes 737312 | tf_op jit(solution)/shard_map/ppermute | solution.py:61
  43.7 6.1 %collective-permute-done.10.refs_6_ = bf16[128,2560]{1,0:T(8,128)(2,1)S(1)} collective-permute-done((bf16[128,2560]{1,0:T(8,128)(2,1)S(1)}, bf16[128,2560]{1,0:T(8,128)(2,1)S(1)}, u32[]{:S(2)}, u32[]{:S(2)}) %collective-permute-start.10) | collective-permute-done | bytes 655392 | tf_op jit(solution)/shard_map/ppermute | solution.py:61
  51.7 12.8 %collective-permute-done.8.refs_2_ = bf16[128,5120]{1,0:T(8,128)(2,1)S(1)} collective-permute-done((bf16[128,5120]{1,0:T(8,128)(2,1)S(1)}, bf16[128,5120]{1,0:T(8,128)(2,1)S(1)}, u32[]{:S(2)}, u32[]{:S(2)}) %collective-permute-start.8) | collective-permute-done | bytes 1310752 | tf_op jit(solution)/shard_map/ppermute | solution.py:61
  67.3 11.2 %collective-permute-done.26.t0 = bf16[128,2560]{1,0:T(8,128)(2,1)S(1)} collective-permute-done((bf16[128,2560]{1,0:T(8,128)(2,1)S(1)}, bf16[128,2560]{1,0:T(8,128)(2,1)S(1)}, u32[]{:S(2)}, u32[]{:S(2)}) %collective-permute-start.26) | collective-permute-done | bytes 655392 | tf_op jit(solution)/shard_map/ppermute | solution.py:61
  78.5 1.7 %collective-permute-start.6 = (bf16[128,2560]{1,0:T(8,128)(2,1)S(1)}, bf16[128,2560]{1,0:T(8,128)(2,1)S(1)}, u32[]{:S(2)}, u32[]{:S(2)}) collective-permute-start(bf16[128,2560]{1,0:T(8,128)(2,1)S(1)} %slice.16), channel_id=1, source_target_pairs={{0,3},{1,0},{2,1},{3,2},{4,7},{5,4},{6,5},{7,6},{8,11},{9,8},{10,9... | collective-permute-start | bytes 1966088 | tf_op jit(solution)/shard_map/ppermute | solution.py:61
  80.9 11.1 %collective-permute-done.9.refs_4_ = bf16[128,2560]{1,0:T(8,128)(2,1)S(1)} collective-permute-done((bf16[128,2560]{1,0:T(8,128)(2,1)S(1)}, bf16[128,2560]{1,0:T(8,128)(2,1)S(1)}, u32[]{:S(2)}, u32[]{:S(2)}) %collective-permute-start.9) | collective-permute-done | bytes 655392 | tf_op jit(solution)/shard_map/ppermute | solution.py:61
  92.7 3.5 %collective-permute-done.6.refs_5_ = bf16[128,2560]{1,0:T(8,128)(2,1)S(1)} collective-permute-done((bf16[128,2560]{1,0:T(8,128)(2,1)S(1)}, bf16[128,2560]{1,0:T(8,128)(2,1)S(1)}, u32[]{:S(2)}, u32[]{:S(2)}) %collective-permute-start.6) | collective-permute-done | bytes 655392 | tf_op jit(solution)/shard_map/ppermute | solution.py:61
  96.3 3.0 %collective-permute-start.4 = (bf16[128,2560]{1,0:T(8,128)(2,1)S(1)}, bf16[128,2560]{1,0:T(8,128)(2,1)S(1)}, u32[]{:S(2)}, u32[]{:S(2)}) collective-permute-start(bf16[128,2560]{1,0:T(8,128)(2,1)S(1)} %collective-permute-done.2.refs_7_), channel_id=1, source_target_pairs={{0,3},{1,0},{2,1},{3,2},{4,7},{5,4},{6,5},{7,6},{8,11},{9,8},{10,9... | collective-permute-start | bytes 1966088 | tf_op jit(solution)/shard_map/ppermute | solution.py:61
  100.3 11.4 %shard_map.102 = (bf16[640,768]{1,0:T(8,128)(2,1)S(1)}, bf16[4,1280,768]{2,1,0:T(8,128)(2,1)}) custom-call(s32[7]{0:T(128)S(1)} %stack.27.refs_0_.pos_ref, bf16[128,5120]{1,0:T(8,128)(2,1)S(1)} %copy-done, bf16[128,5120]{1,0:T(8,128)(2,1)S(1)} %collective-permute-done.8.refs_2_, bf16[128,5120]{1,0:T(8,128)(2,1)S(1)} %collective-permute-done.5.refs_3_, ...), custom_call_target="tpu_custom_call" | custom-call | tf_op jit(solution)/shard_map/pallas_call | solution.py:163
  111.8 3.5 %shard_map.103.acc_ref = f32[384,768]{1,0:T(8,128)S(1)} custom-call(bf16[128,2560]{1,0:T(8,128)(2,1)S(1)} %collective-permute-done.26.t0, bf16[128,2560]{1,0:T(8,128)(2,1)S(1)} %collective-permute-done.27.t1, bf16[128,2560]{1,0:T(8,128)(2,1)S(1)} %collective-permute-done.28.t2, bf16[5120,768]{1,0:T(8,128)(2,1)} %bitcast.28), custom_call_target="tpu_custom_call" | custom-call | tf_op jit(solution)/shard_map/pallas_call | solution.py:238
  115.3 7.0 %collective-permute-done.4.t1 = bf16[128,2560]{1,0:T(8,128)(2,1)S(1)} collective-permute-done((bf16[128,2560]{1,0:T(8,128)(2,1)S(1)}, bf16[128,2560]{1,0:T(8,128)(2,1)S(1)}, u32[]{:S(2)}, u32[]{:S(2)}) %collective-permute-start.4) | collective-permute-done | bytes 655392 | tf_op jit(solution)/shard_map/ppermute | solution.py:61
  122.3 4.1 %shard_map.104 = (bf16[1024,384]{1,0:T(8,128)(2,1)S(1)}, bf16[512,384]{1,0:T(8,128)(2,1)S(1)}, bf16[512,384]{1,0:T(8,128)(2,1)S(1)}) custom-call(s32[7]{0:T(128)S(1)} %stack.27.refs_0_.pos_ref, bf16[128,2560]{1,0:T(8,128)(2,1)S(1)} %collective-permute-done.3.t0, bf16[128,2560]{1,0:T(8,128)(2,1)S(1)} %collective-permute-done.4.t1, ...), custom_call_target="tpu_custom_call" | custom-call | tf_op jit(solution)/shard_map/pallas_call | solution.py:322
  126.5 4.1 %collective-permute-start.30 = (bf16[512,384]{1,0:T(8,128)(2,1)S(1)}, bf16[512,384]{1,0:T(8,128)(2,1)S(1)}, u32[]{:S(2)}, u32[]{:S(2)}) collective-permute-start(bf16[512,384]{1,0:T(8,128)(2,1)S(1)} %get-tuple-element.30), channel_id=1, source_target_pairs={{0,248},{1,249},{2,250},{3,251},{4,252},{5,253},{6,254},{7,255},{8... | collective-permute-start | bytes 1179656 | tf_op jit(solution)/shard_map/ppermute | solution.py:61
  130.7 4.1 %shard_map.106 = (bf16[1024,384]{1,0:T(8,128)(2,1)S(1)}, bf16[512,384]{1,0:T(8,128)(2,1)S(1)}, bf16[512,384]{1,0:T(8,128)(2,1)S(1)}) custom-call(s32[7]{0:T(128)S(1)} %stack.27.refs_0_.pos_ref, bf16[128,2560]{1,0:T(8,128)(2,1)S(1)} %collective-permute-done.3.t0, bf16[128,2560]{1,0:T(8,128)(2,1)S(1)} %collective-permute-done.4.t1, ...), custom_call_target="tpu_custom_call" | custom-call | tf_op jit(solution)/shard_map/pallas_call | solution.py:322
  134.9 2.4 %collective-permute-start.32 = (bf16[512,384]{1,0:T(8,128)(2,1)S(1)}, bf16[512,384]{1,0:T(8,128)(2,1)S(1)}, u32[]{:S(2)}, u32[]{:S(2)}) collective-permute-start(bf16[512,384]{1,0:T(8,128)(2,1)S(1)} %get-tuple-element.36), channel_id=1, source_target_pairs={{0,248},{1,249},{2,250},{3,251},{4,252},{5,253},{6,254},{7,255},{8... | collective-permute-start | bytes 1179656 | tf_op jit(solution)/shard_map/ppermute | solution.py:61
  137.3 4.7 %collective-permute-done.30.far_ref = bf16[512,384]{1,0:T(8,128)(2,1)S(1)} collective-permute-done((bf16[512,384]{1,0:T(8,128)(2,1)S(1)}, bf16[512,384]{1,0:T(8,128)(2,1)S(1)}, u32[]{:S(2)}, u32[]{:S(2)}) %collective-permute-start.30) | collective-permute-done | bytes 393248 | tf_op jit(solution)/shard_map/ppermute | solution.py:61
  142.0 6.3 %shard_map.105 = (bf16[4,3,256,768]{3,2,1,0:T(8,128)(2,1)S(1)}, f32[1024,384]{1,0:T(8,128)S(1)}) custom-call(s32[7]{0:T(128)S(1)} %stack.27.refs_0_.pos_ref, bf16[1024,384]{1,0:T(8,128)(2,1)S(1)} %copy-done.1, bf16[1024,384]{1,0:T(8,128)(2,1)S(1)} %get-tuple-element.28.full_ref, bf16[512,384]{1,0:T(8,128)(2,1)S(1)} %collective-permute-done.29.near_ref, ...), custom_call_target="tpu_custom_call" | custom-call | tf_op jit(solution)/shard_map/pallas_call | solution.py:433
  148.3 4.4 %shard_map.107 = bf16[1024,384]{1,0:T(8,128)(2,1)} custom-call(s32[7]{0:T(128)S(1)} %stack.27.refs_0_.pos_ref, bf16[4,3,256,768]{3,2,1,0:T(8,128)(2,1)S(1)} %get-tuple-element.31.prob_ref, f32[1024,384]{1,0:T(8,128)S(1)} %get-tuple-element.32.total_ref, bf16[1024,384]{1,0:T(8,128)(2,1)S(1)} %get-tuple-element.34.full_ref, ...), custom_call_target="tpu_custom_call" | custom-call | tf_op jit(solution)/shard_map/pallas_call | solution.py:465
  (74 shorter events, 20.9 us)
Async XLA Ops:
  4.5 13.4 %collective-permute-start.11 = (bf16[320,384]{1,0:T(8,128)(2,1)S(1)}, bf16[320,384]{1,0:T(8,128)(2,1)S(1)}, u32[]{:S(2)}, u32[]{:S(2)}) collective-permute-start(bf16[320,384]{1,0:T(8,128)(2,1)S(1)} %shard_map.100.refs_8_), channel_id=1, source_target_pairs={{0,16},{1,17},{2,18},{3,19},{4,20},{5,21},{6,22},{7,23},{8,56},{9,... | collective-permute-start | bytes 737288 | tf_op jit(solution)/shard_map/ppermute | solution.py:61
  7.8 42.3 %collective-permute-start.5 = (bf16[128,5120]{1,0:T(8,128)(2,1)}, bf16[128,5120]{1,0:T(8,128)(2,1)S(1)}, u32[]{:S(2)}, u32[]{:S(2)}) collective-permute-start(bf16[128,5120]{1,0:T(8,128)(2,1)} %refs_1_.3), channel_id=1, source_target_pairs={{0,3},{1,0},{2,1},{3,2},{4,7},{5,4},{6,5},{7,6},{8,11},{9,8},{10,9... | collective-permute-start | bytes 3932168 | tf_op jit(solution)/shard_map/ppermute | solution.py:61
  19.7 11.8 %collective-permute-start.15 = (bf16[320,384]{1,0:T(8,128)(2,1)S(1)}, bf16[320,384]{1,0:T(8,128)(2,1)S(1)}, u32[]{:S(2)}, u32[]{:S(2)}) collective-permute-start(bf16[320,384]{1,0:T(8,128)(2,1)S(1)} %collective-permute-done.refs_12_), channel_id=1, source_target_pairs={{0,8},{1,9},{2,10},{3,11},{4,12},{5,13},{6,14},{7,15},{8,0},{9,1},... | collective-permute-start | bytes 737288 | tf_op jit(solution)/shard_map/ppermute | solution.py:61
  30.0 12.8 %collective-permute-start.20 = (bf16[960,384]{1,0:T(8,128)(2,1)S(1)}, bf16[960,384]{1,0:T(8,128)(2,1)S(1)}, u32[]{:S(2)}, u32[]{:S(2)}) collective-permute-start(bf16[960,384]{1,0:T(8,128)(2,1)S(1)} %shard_map.101.refs_10_), channel_id=1, source_target_pairs={{0,64},{1,65},{2,66},{3,67},{4,68},{5,69},{6,70},{7,71},{8,200},{9... | collective-permute-start | bytes 2211848 | tf_op jit(solution)/shard_map/ppermute | solution.py:61
  31.5 11.5 %collective-permute-start.14 = (bf16[960,384]{1,0:T(8,128)(2,1)S(1)}, bf16[960,384]{1,0:T(8,128)(2,1)S(1)}, u32[]{:S(2)}, u32[]{:S(2)}) collective-permute-start(bf16[960,384]{1,0:T(8,128)(2,1)S(1)} %shard_map.101.refs_10_), channel_id=1, source_target_pairs={{0,8},{1,9},{2,10},{3,11},{4,12},{5,13},{6,14},{7,15},{8,0},{9,1},... | collective-permute-start | bytes 2211848 | tf_op jit(solution)/shard_map/ppermute | solution.py:61
  31.5 32.9 %collective-permute-start.8 = (bf16[128,5120]{1,0:T(8,128)(2,1)S(1)}, bf16[128,5120]{1,0:T(8,128)(2,1)S(1)}, u32[]{:S(2)}, u32[]{:S(2)}) collective-permute-start(bf16[128,5120]{1,0:T(8,128)(2,1)S(1)} %copy-done), channel_id=1, source_target_pairs={{0,1},{1,2},{2,3},{3,0},{4,5},{5,6},{6,7},{7,4},{8,9},{9,10},{10,1... | collective-permute-start | bytes 3932168 | tf_op jit(solution)/shard_map/ppermute | solution.py:61
  33.1 16.8 %collective-permute-start.10 = (bf16[128,2560]{1,0:T(8,128)(2,1)S(1)}, bf16[128,2560]{1,0:T(8,128)(2,1)S(1)}, u32[]{:S(2)}, u32[]{:S(2)}) collective-permute-start(bf16[128,2560]{1,0:T(8,128)(2,1)S(1)} %get-tuple-element.23), channel_id=1, source_target_pairs={{0,4},{1,5},{2,6},{3,7},{4,0},{5,1},{6,2},{7,3},{8,12},{9,13},{10,... | collective-permute-start | bytes 1966088 | tf_op jit(solution)/shard_map/ppermute | solution.py:61
  42.7 21.7 %collective-permute-start.24 = (bf16[960,384]{1,0:T(8,128)(2,1)S(1)}, bf16[960,384]{1,0:T(8,128)(2,1)S(1)}, u32[]{:S(2)}, u32[]{:S(2)}) collective-permute-start(bf16[960,384]{1,0:T(8,128)(2,1)S(1)} %collective-permute-done.20.refs_18_), channel_id=1, source_target_pairs={{0,64},{1,65},{2,66},{3,67},{4,68},{5,69},{6,70},{7,71},{8,200},{9... | collective-permute-start | bytes 2211848 | tf_op jit(solution)/shard_map/ppermute | solution.py:61
  43.0 22.0 %collective-permute-start.22 = (bf16[960,384]{1,0:T(8,128)(2,1)S(1)}, bf16[960,384]{1,0:T(8,128)(2,1)S(1)}, u32[]{:S(2)}, u32[]{:S(2)}) collective-permute-start(bf16[960,384]{1,0:T(8,128)(2,1)S(1)} %collective-permute-done.14.refs_11_), channel_id=1, source_target_pairs={{0,64},{1,65},{2,66},{3,67},{4,68},{5,69},{6,70},{7,71},{8,200},{9... | collective-permute-start | bytes 2211848 | tf_op jit(solution)/shard_map/ppermute | solution.py:61
  49.8 15.9 %collective-permute-start.2 = (bf16[128,2560]{1,0:T(8,128)(2,1)S(1)}, bf16[128,2560]{1,0:T(8,128)(2,1)S(1)}, u32[]{:S(2)}, u32[]{:S(2)}) collective-permute-start(bf16[128,2560]{1,0:T(8,128)(2,1)S(1)} %get-tuple-element.22), channel_id=1, source_target_pairs={{0,4},{1,5},{2,6},{3,7},{4,0},{5,1},{6,2},{7,3},{8,12},{9,13},{10,... | collective-permute-start | bytes 1966088 | tf_op jit(solution)/shard_map/ppermute | solution.py:61
  50.1 28.4 %collective-permute-start.26 = (bf16[128,2560]{1,0:T(8,128)(2,1)S(1)}, bf16[128,2560]{1,0:T(8,128)(2,1)S(1)}, u32[]{:S(2)}, u32[]{:S(2)}) collective-permute-start(bf16[128,2560]{1,0:T(8,128)(2,1)S(1)} %collective-permute-done.10.refs_6_), channel_id=1, source_target_pairs={{0,1},{1,2},{2,3},{3,0},{4,5},{5,6},{6,7},{7,4},{8,9},{9,10},{10,1... | collective-permute-start | bytes 1966088 | tf_op jit(solution)/shard_map/ppermute | solution.py:61
  64.5 15.7 %collective-permute-start.21 = (bf16[960,384]{1,0:T(8,128)(2,1)S(1)}, bf16[960,384]{1,0:T(8,128)(2,1)S(1)}, u32[]{:S(2)}, u32[]{:S(2)}) collective-permute-start(bf16[960,384]{1,0:T(8,128)(2,1)S(1)} %collective-permute-done.20.refs_18_), channel_id=1, source_target_pairs={{0,8},{1,9},{2,10},{3,11},{4,12},{5,13},{6,14},{7,15},{8,0},{9,1},... | collective-permute-start | bytes 2211848 | tf_op jit(solution)/shard_map/ppermute | solution.py:61
  64.5 31.9 %collective-permute-start.25 = (bf16[960,384]{1,0:T(8,128)(2,1)S(1)}, bf16[960,384]{1,0:T(8,128)(2,1)S(1)}, u32[]{:S(2)}, u32[]{:S(2)}) collective-permute-start(bf16[960,384]{1,0:T(8,128)(2,1)S(1)} %collective-permute-done.24.refs_22_), channel_id=1, source_target_pairs={{0,8},{1,9},{2,10},{3,11},{4,12},{5,13},{6,14},{7,15},{8,0},{9,1},... | collective-permute-start | bytes 2211848 | tf_op jit(solution)/shard_map/ppermute | solution.py:61
  65.0 34.4 %collective-permute-start.23 = (bf16[960,384]{1,0:T(8,128)(2,1)S(1)}, bf16[960,384]{1,0:T(8,128)(2,1)S(1)}, u32[]{:S(2)}, u32[]{:S(2)}) collective-permute-start(bf16[960,384]{1,0:T(8,128)(2,1)S(1)} %collective-permute-done.22.refs_20_), channel_id=1, source_target_pairs={{0,8},{1,9},{2,10},{3,11},{4,12},{5,13},{6,14},{7,15},{8,0},{9,1},... | collective-permute-start | bytes 2211848 | tf_op jit(solution)/shard_map/ppermute | solution.py:61
  65.8 26.3 %collective-permute-start.9 = (bf16[128,2560]{1,0:T(8,128)(2,1)S(1)}, bf16[128,2560]{1,0:T(8,128)(2,1)S(1)}, u32[]{:S(2)}, u32[]{:S(2)}) collective-permute-start(bf16[128,2560]{1,0:T(8,128)(2,1)S(1)} %slice.17), channel_id=1, source_target_pairs={{0,1},{1,2},{2,3},{3,0},{4,5},{5,6},{6,7},{7,4},{8,9},{9,10},{10,1... | collective-permute-start | bytes 1966088 | tf_op jit(solution)/shard_map/ppermute | solution.py:61
  78.5 17.6 %collective-permute-start.6 = (bf16[128,2560]{1,0:T(8,128)(2,1)S(1)}, bf16[128,2560]{1,0:T(8,128)(2,1)S(1)}, u32[]{:S(2)}, u32[]{:S(2)}) collective-permute-start(bf16[128,2560]{1,0:T(8,128)(2,1)S(1)} %slice.16), channel_id=1, source_target_pairs={{0,3},{1,0},{2,1},{3,2},{4,7},{5,4},{6,5},{7,6},{8,11},{9,8},{10,9... | collective-permute-start | bytes 1966088 | tf_op jit(solution)/shard_map/ppermute | solution.py:61
  80.2 31.5 %collective-permute-start.27 = (bf16[128,2560]{1,0:T(8,128)(2,1)S(1)}, bf16[128,2560]{1,0:T(8,128)(2,1)S(1)}, u32[]{:S(2)}, u32[]{:S(2)}) collective-permute-start(bf16[128,2560]{1,0:T(8,128)(2,1)S(1)} %collective-permute-done.10.refs_6_), channel_id=1, source_target_pairs={{0,3},{1,0},{2,1},{3,2},{4,7},{5,4},{6,5},{7,6},{8,11},{9,8},{10,9... | collective-permute-start | bytes 1966088 | tf_op jit(solution)/shard_map/ppermute | solution.py:61
  92.0 19.7 %collective-permute-start.28 = (bf16[128,2560]{1,0:T(8,128)(2,1)S(1)}, bf16[128,2560]{1,0:T(8,128)(2,1)S(1)}, u32[]{:S(2)}, u32[]{:S(2)}) collective-permute-start(bf16[128,2560]{1,0:T(8,128)(2,1)S(1)} %collective-permute-done.9.refs_4_), channel_id=1, source_target_pairs={{0,4},{1,5},{2,6},{3,7},{4,0},{5,1},{6,2},{7,3},{8,12},{9,13},{10,... | collective-permute-start | bytes 1966088 | tf_op jit(solution)/shard_map/ppermute | solution.py:61
  96.1 19.2 %collective-permute-start.3 = (bf16[128,2560]{1,0:T(8,128)(2,1)S(1)}, bf16[128,2560]{1,0:T(8,128)(2,1)S(1)}, u32[]{:S(2)}, u32[]{:S(2)}) collective-permute-start(bf16[128,2560]{1,0:T(8,128)(2,1)S(1)} %collective-permute-done.2.refs_7_), channel_id=1, source_target_pairs={{0,1},{1,2},{2,3},{3,0},{4,5},{5,6},{6,7},{7,4},{8,9},{9,10},{10,1... | collective-permute-start | bytes 1966088 | tf_op jit(solution)/shard_map/ppermute | solution.py:61
  96.3 25.9 %collective-permute-start.4 = (bf16[128,2560]{1,0:T(8,128)(2,1)S(1)}, bf16[128,2560]{1,0:T(8,128)(2,1)S(1)}, u32[]{:S(2)}, u32[]{:S(2)}) collective-permute-start(bf16[128,2560]{1,0:T(8,128)(2,1)S(1)} %collective-permute-done.2.refs_7_), channel_id=1, source_target_pairs={{0,3},{1,0},{2,1},{3,2},{4,7},{5,4},{6,5},{7,6},{8,11},{9,8},{10,9... | collective-permute-start | bytes 1966088 | tf_op jit(solution)/shard_map/ppermute | solution.py:61
  99.4 22.9 %collective-permute-start.7 = (bf16[128,2560]{1,0:T(8,128)(2,1)S(1)}, bf16[128,2560]{1,0:T(8,128)(2,1)S(1)}, u32[]{:S(2)}, u32[]{:S(2)}) collective-permute-start(bf16[128,2560]{1,0:T(8,128)(2,1)S(1)} %collective-permute-done.6.refs_5_), channel_id=1, source_target_pairs={{0,4},{1,5},{2,6},{3,7},{4,0},{5,1},{6,2},{7,3},{8,12},{9,13},{10,... | collective-permute-start | bytes 1966088 | tf_op jit(solution)/shard_map/ppermute | solution.py:61
  126.5 15.5 %collective-permute-start.30 = (bf16[512,384]{1,0:T(8,128)(2,1)S(1)}, bf16[512,384]{1,0:T(8,128)(2,1)S(1)}, u32[]{:S(2)}, u32[]{:S(2)}) collective-permute-start(bf16[512,384]{1,0:T(8,128)(2,1)S(1)} %get-tuple-element.30), channel_id=1, source_target_pairs={{0,248},{1,249},{2,250},{3,251},{4,252},{5,253},{6,254},{7,255},{8... | collective-permute-start | bytes 1179656 | tf_op jit(solution)/shard_map/ppermute | solution.py:61
  134.8 13.5 %collective-permute-start.31 = (bf16[512,384]{1,0:T(8,128)(2,1)S(1)}, bf16[512,384]{1,0:T(8,128)(2,1)S(1)}, u32[]{:S(2)}, u32[]{:S(2)}) collective-permute-start(bf16[512,384]{1,0:T(8,128)(2,1)S(1)} %get-tuple-element.35), channel_id=1, source_target_pairs={{0,8},{1,9},{2,10},{3,11},{4,12},{5,13},{6,14},{7,15},{8,0},{9,1},... | collective-permute-start | bytes 1179656 | tf_op jit(solution)/shard_map/ppermute | solution.py:61
  134.9 13.4 %collective-permute-start.32 = (bf16[512,384]{1,0:T(8,128)(2,1)S(1)}, bf16[512,384]{1,0:T(8,128)(2,1)S(1)}, u32[]{:S(2)}, u32[]{:S(2)}) collective-permute-start(bf16[512,384]{1,0:T(8,128)(2,1)S(1)} %get-tuple-element.36), channel_id=1, source_target_pairs={{0,248},{1,249},{2,250},{3,251},{4,252},{5,253},{6,254},{7,255},{8... | collective-permute-start | bytes 1179656 | tf_op jit(solution)/shard_map/ppermute | solution.py:61
  (19 other events, 197.9 us)

commit v8 on v7

--- a/solution.py
+++ b/solution.py
@@ -423,12 +423,12 @@
             )
             own = jnp.exp(own - top)
             slabs = jnp.exp(slabs - top)
-            total[:, cols] = jnp.broadcast_to(
+            total[pl.ds(pl.multiple_of(p * TILE, TILE), TILE), cols] = jnp.broadcast_to(
                 jnp.sum(own, axis=-1, keepdims=True) + jnp.sum(slabs, axis=-1, keepdims=True),
                 (TILE, HD),
             )
-            prob[0, h, :, :TILE] = own.astype(BF16)
-            prob[0, h, :, TILE:] = slabs.astype(BF16)
+            prob[p, h, :, :TILE] = own.astype(BF16)
+            prob[p, h, :, TILE:] = slabs.astype(BF16)
 
     return pl.pallas_call(
         body,
@@ -438,10 +438,7 @@
             jax.ShapeDtypeStruct((TPD * TILE, 384), F32),
         ],
         in_specs=[SM, pl.BlockSpec((TILE, 384), lambda p: (p, 0)), VM, VM, VM] + [SM] * 6,
-        out_specs=[
-            pl.BlockSpec((1, 3, TILE, CAND), lambda p: (p, 0, 0, 0)),
-            pl.BlockSpec((TILE, 384), lambda p: (p, 0)),
-        ],
+        out_specs=[VM, VM],
         scratch_shapes=[pltpu.VMEM((CAND, 384), BF16)],
         compiler_params=pltpu.CompilerParams(vmem_limit_bytes=24 * MIB),
     )(pos, queries, full, near_k, far_k, *tables)
@@ -459,8 +456,9 @@
         _collect(p, pos_ref, slot, neighbour, first, full_ref, near_ref, far_ref, cand)
         for h in range(3):
             cols = slice(h * HD, h * HD + HD)
-            mixed = jnp.dot(prob_ref[0, h], cand[:, cols], preferred_element_type=F32)
-            out[:, cols] = (mixed / total_ref[:, cols]).astype(BF16)
+            mixed = jnp.dot(prob_ref[p, h], cand[:, cols], preferred_element_type=F32)
+            rows = pl.ds(pl.multiple_of(p * TILE, TILE), TILE)
+            out[:, cols] = (mixed / total_ref[rows, cols]).astype(BF16)
 
     return pl.pallas_call(
         body,
@@ -468,8 +466,8 @@
         out_shape=jax.ShapeDtypeStruct((TPD * TILE, 384), BF16),
         in_specs=[
             SM,
-            pl.BlockSpec((1, 3, TILE, CAND), lambda p: (p, 0, 0, 0)),
-            pl.BlockSpec((TILE, 384), lambda p: (p, 0)),
+            VM,
+            VM,
             VM,
             VM,
             VM,

time: 155 us -> 155 us (level)
  no operation moved by 1% of the time
where the time goes in v8:
time: 155 us; the launch traced here: 153 us
  waiting for transfers between devices  75.4 us (49%)
  starting transfers between devices  38.7 us (25%)
  Pallas kernels  34.9 us (23%)
  local copies, waits for them, and re-layouts  3.39 us (2%)
    ppermute x33, waiting for transfers between devices, send(): lax.ppermute(a, AXES, _far_moves() if 'far' in step else _moves(**step))  75.4 us
    ppermute x33, starting transfers between devices, send(): lax.ppermute(a, AXES, _far_moves() if 'far' in step else _moves(**step))  38.7 us
    pallas_call x1, Pallas kernels, project(): pl.pallas_call(body, out_shape=[jax.ShapeDtypeStruct((rows, 768), BF16),...  11.4 us
    pallas_call x2, Pallas kernels, project_last(): pl.pallas_call(body, out_shape=[jax.ShapeDtypeStruct((TPD * TILE, 384), B...  8.18 us
    pallas_call x1, Pallas kernels, weigh(): pl.pallas_call(body, grid=(TPD,), out_shape=[jax.ShapeDtypeStruct((TPD, 3...  6.28 us
    pallas_call x1, Pallas kernels, mix(): pl.pallas_call(body, grid=(TPD,), out_shape=jax.ShapeDtypeStruct((TPD * T...  4.34 us
    pallas_call x1, Pallas kernels, project_half(): pl.pallas_call(body, out_shape=jax.ShapeDtypeStruct((rows, 768), F32), in...  3.52 us
  transfers between devices with their start and end apart: 33, of which 11 were waited for; matrix products, arithmetic and copies ran while one was open for 1% of the time, Pallas kernels for 17%

profile of v8, /device:TPU:32, one launch (start us, length us, event | category | flops | bytes accessed | tf_op | source)
XLA Modules:
  0.0 152.7 jit_solution(17408808594662365562)
XLA Ops:
  4.5 3.3 %collective-permute-start.11 = (bf16[320,384]{1,0:T(8,128)(2,1)S(1)}, bf16[320,384]{1,0:T(8,128)(2,1)S(1)}, u32[]{:S(2)}, u32[]{:S(2)}) collective-permute-start(bf16[320,384]{1,0:T(8,128)(2,1)S(1)} %shard_map.100.refs_8_), channel_id=1, source_target_pairs={{0,16},{1,17},{2,18},{3,19},{4,20},{5,21},{6,22},{7,23},{8,56},{9,... | collective-permute-start | bytes 737288 | tf_op jit(solution)/shard_map/ppermute | solution.py:61
  7.8 3.0 %collective-permute-start.5 = (bf16[128,5120]{1,0:T(8,128)(2,1)}, bf16[128,5120]{1,0:T(8,128)(2,1)S(1)}, u32[]{:S(2)}, u32[]{:S(2)}) collective-permute-start(bf16[128,5120]{1,0:T(8,128)(2,1)} %refs_1_.3), channel_id=1, source_target_pairs={{0,3},{1,0},{2,1},{3,2},{4,7},{5,4},{6,5},{7,6},{8,11},{9,8},{10,9... | collective-permute-start | bytes 3932168 | tf_op jit(solution)/shard_map/ppermute | solution.py:61
  13.0 3.7 %collective-permute-start.12 = (bf16[320,384]{1,0:T(8,128)(2,1)S(1)}, bf16[320,384]{1,0:T(8,128)(2,1)S(1)}, u32[]{:S(2)}, u32[]{:S(2)}) collective-permute-start(bf16[320,384]{1,0:T(8,128)(2,1)S(1)} %collective-permute-done.1.refs_9_), channel_id=1, source_target_pairs={{0,16},{1,17},{2,18},{3,19},{4,20},{5,21},{6,22},{7,23},{8,56},{9,... | collective-permute-start | bytes 737288 | tf_op jit(solution)/shard_map/ppermute | solution.py:61
  17.9 1.8 %collective-permute-start.13 = (bf16[320,384]{1,0:T(8,128)(2,1)S(1)}, bf16[320,384]{1,0:T(8,128)(2,1)S(1)}, u32[]{:S(2)}, u32[]{:S(2)}) collective-permute-start(bf16[320,384]{1,0:T(8,128)(2,1)S(1)} %collective-permute-done.11.refs_0_), channel_id=1, source_target_pairs={{0,16},{1,17},{2,18},{3,19},{4,20},{5,21},{6,22},{7,23},{8,56},{9,... | collective-permute-start | bytes 737288 | tf_op jit(solution)/shard_map/ppermute | solution.py:61
  19.7 4.4 %collective-permute-done.12.refs_1_ = bf16[320,384]{1,0:T(8,128)(2,1)S(1)} collective-permute-done((bf16[320,384]{1,0:T(8,128)(2,1)S(1)}, bf16[320,384]{1,0:T(8,128)(2,1)S(1)}, u32[]{:S(2)}, u32[]{:S(2)}) %collective-permute-start.12) | collective-permute-done | bytes 245792 | tf_op jit(solution)/shard_map/ppermute | solution.py:61
  24.6 4.4 %collective-permute-done.13.refs_2_ = bf16[320,384]{1,0:T(8,128)(2,1)S(1)} collective-permute-done((bf16[320,384]{1,0:T(8,128)(2,1)S(1)}, bf16[320,384]{1,0:T(8,128)(2,1)S(1)}, u32[]{:S(2)}, u32[]{:S(2)}) %collective-permute-start.13) | collective-permute-done | bytes 245792 | tf_op jit(solution)/shard_map/ppermute | solution.py:61
  33.1 9.7 %collective-permute-done.20.refs_18_ = bf16[960,384]{1,0:T(8,128)(2,1)S(1)} collective-permute-done((bf16[960,384]{1,0:T(8,128)(2,1)S(1)}, bf16[960,384]{1,0:T(8,128)(2,1)S(1)}, u32[]{:S(2)}, u32[]{:S(2)}) %collective-permute-start.20) | collective-permute-done | bytes 737312 | tf_op jit(solution)/shard_map/ppermute | solution.py:61
  43.7 6.1 %collective-permute-done.10.refs_6_ = bf16[128,2560]{1,0:T(8,128)(2,1)S(1)} collective-permute-done((bf16[128,2560]{1,0:T(8,128)(2,1)S(1)}, bf16[128,2560]{1,0:T(8,128)(2,1)S(1)}, u32[]{:S(2)}, u32[]{:S(2)}) %collective-permute-start.10) | collective-permute-done | bytes 655392 | tf_op jit(solution)/shard_map/ppermute | solution.py:61
  51.7 12.8 %collective-permute-done.8.refs_2_ = bf16[128,5120]{1,0:T(8,128)(2,1)S(1)} collective-permute-done((bf16[128,5120]{1,0:T(8,128)(2,1)S(1)}, bf16[128,5120]{1,0:T(8,128)(2,1)S(1)}, u32[]{:S(2)}, u32[]{:S(2)}) %collective-permute-start.8) | collective-permute-done | bytes 1310752 | tf_op jit(solution)/shard_map/ppermute | solution.py:61
  67.3 11.2 %collective-permute-done.26.t0 = bf16[128,2560]{1,0:T(8,128)(2,1)S(1)} collective-permute-done((bf16[128,2560]{1,0:T(8,128)(2,1)S(1)}, bf16[128,2560]{1,0:T(8,128)(2,1)S(1)}, u32[]{:S(2)}, u32[]{:S(2)}) %collective-permute-start.26) | collective-permute-done | bytes 655392 | tf_op jit(solution)/shard_map/ppermute | solution.py:61
  78.5 1.7 %collective-permute-start.6 = (bf16[128,2560]{1,0:T(8,128)(2,1)S(1)}, bf16[128,2560]{1,0:T(8,128)(2,1)S(1)}, u32[]{:S(2)}, u32[]{:S(2)}) collective-permute-start(bf16[128,2560]{1,0:T(8,128)(2,1)S(1)} %slice.16), channel_id=1, source_target_pairs={{0,3},{1,0},{2,1},{3,2},{4,7},{5,4},{6,5},{7,6},{8,11},{9,8},{10,9... | collective-permute-start | bytes 1966088 | tf_op jit(solution)/shard_map/ppermute | solution.py:61
  80.9 11.1 %collective-permute-done.9.refs_4_ = bf16[128,2560]{1,0:T(8,128)(2,1)S(1)} collective-permute-done((bf16[128,2560]{1,0:T(8,128)(2,1)S(1)}, bf16[128,2560]{1,0:T(8,128)(2,1)S(1)}, u32[]{:S(2)}, u32[]{:S(2)}) %collective-permute-start.9) | collective-permute-done | bytes 655392 | tf_op jit(solution)/shard_map/ppermute | solution.py:61
  92.7 3.5 %collective-permute-done.6.refs_5_ = bf16[128,2560]{1,0:T(8,128)(2,1)S(1)} collective-permute-done((bf16[128,2560]{1,0:T(8,128)(2,1)S(1)}, bf16[128,2560]{1,0:T(8,128)(2,1)S(1)}, u32[]{:S(2)}, u32[]{:S(2)}) %collective-permute-start.6) | collective-permute-done | bytes 655392 | tf_op jit(solution)/shard_map/ppermute | solution.py:61
  96.3 3.0 %collective-permute-start.4 = (bf16[128,2560]{1,0:T(8,128)(2,1)S(1)}, bf16[128,2560]{1,0:T(8,128)(2,1)S(1)}, u32[]{:S(2)}, u32[]{:S(2)}) collective-permute-start(bf16[128,2560]{1,0:T(8,128)(2,1)S(1)} %collective-permute-done.2.refs_7_), channel_id=1, source_target_pairs={{0,3},{1,0},{2,1},{3,2},{4,7},{5,4},{6,5},{7,6},{8,11},{9,8},{10,9... | collective-permute-start | bytes 1966088 | tf_op jit(solution)/shard_map/ppermute | solution.py:61
  100.3 11.4 %shard_map.102 = (bf16[640,768]{1,0:T(8,128)(2,1)S(1)}, bf16[4,1280,768]{2,1,0:T(8,128)(2,1)}) custom-call(s32[7]{0:T(128)S(1)} %stack.27.refs_0_.pos_ref, bf16[128,5120]{1,0:T(8,128)(2,1)S(1)} %copy-done, bf16[128,5120]{1,0:T(8,128)(2,1)S(1)} %collective-permute-done.8.refs_2_, bf16[128,5120]{1,0:T(8,128)(2,1)S(1)} %collective-permute-done.5.refs_3_, ...), custom_call_target="tpu_custom_call" | custom-call | tf_op jit(solution)/shard_map/pallas_call | solution.py:163
  111.8 3.5 %shard_map.103.acc_ref = f32[384,768]{1,0:T(8,128)S(1)} custom-call(bf16[128,2560]{1,0:T(8,128)(2,1)S(1)} %collective-permute-done.26.t0, bf16[128,2560]{1,0:T(8,128)(2,1)S(1)} %collective-permute-done.27.t1, bf16[128,2560]{1,0:T(8,128)(2,1)S(1)} %collective-permute-done.28.t2, bf16[5120,768]{1,0:T(8,128)(2,1)} %bitcast.28), custom_call_target="tpu_custom_call" | custom-call | tf_op jit(solution)/shard_map/pallas_call | solution.py:238
  115.3 7.0 %collective-permute-done.4.t1 = bf16[128,2560]{1,0:T(8,128)(2,1)S(1)} collective-permute-done((bf16[128,2560]{1,0:T(8,128)(2,1)S(1)}, bf16[128,2560]{1,0:T(8,128)(2,1)S(1)}, u32[]{:S(2)}, u32[]{:S(2)}) %collective-permute-start.4) | collective-permute-done | bytes 655392 | tf_op jit(solution)/shard_map/ppermute | solution.py:61
  122.3 4.1 %shard_map.104 = (bf16[1024,384]{1,0:T(8,128)(2,1)S(1)}, bf16[512,384]{1,0:T(8,128)(2,1)S(1)}, bf16[512,384]{1,0:T(8,128)(2,1)S(1)}) custom-call(s32[7]{0:T(128)S(1)} %stack.27.refs_0_.pos_ref, bf16[128,2560]{1,0:T(8,128)(2,1)S(1)} %collective-permute-done.3.t0, bf16[128,2560]{1,0:T(8,128)(2,1)S(1)} %collective-permute-done.4.t1, ...), custom_call_target="tpu_custom_call" | custom-call | tf_op jit(solution)/shard_map/pallas_call | solution.py:322
  126.5 4.1 %collective-permute-start.30 = (bf16[512,384]{1,0:T(8,128)(2,1)S(1)}, bf16[512,384]{1,0:T(8,128)(2,1)S(1)}, u32[]{:S(2)}, u32[]{:S(2)}) collective-permute-start(bf16[512,384]{1,0:T(8,128)(2,1)S(1)} %get-tuple-element.30), channel_id=1, source_target_pairs={{0,248},{1,249},{2,250},{3,251},{4,252},{5,253},{6,254},{7,255},{8... | collective-permute-start | bytes 1179656 | tf_op jit(solution)/shard_map/ppermute | solution.py:61
  130.7 4.1 %shard_map.106 = (bf16[1024,384]{1,0:T(8,128)(2,1)S(1)}, bf16[512,384]{1,0:T(8,128)(2,1)S(1)}, bf16[512,384]{1,0:T(8,128)(2,1)S(1)}) custom-call(s32[7]{0:T(128)S(1)} %stack.27.refs_0_.pos_ref, bf16[128,2560]{1,0:T(8,128)(2,1)S(1)} %collective-permute-done.3.t0, bf16[128,2560]{1,0:T(8,128)(2,1)S(1)} %collective-permute-done.4.t1, ...), custom_call_target="tpu_custom_call" | custom-call | tf_op jit(solution)/shard_map/pallas_call | solution.py:322
  134.9 2.4 %collective-permute-start.32 = (bf16[512,384]{1,0:T(8,128)(2,1)S(1)}, bf16[512,384]{1,0:T(8,128)(2,1)S(1)}, u32[]{:S(2)}, u32[]{:S(2)}) collective-permute-start(bf16[512,384]{1,0:T(8,128)(2,1)S(1)} %get-tuple-element.36), channel_id=1, source_target_pairs={{0,248},{1,249},{2,250},{3,251},{4,252},{5,253},{6,254},{7,255},{8... | collective-permute-start | bytes 1179656 | tf_op jit(solution)/shard_map/ppermute | solution.py:61
  137.3 4.7 %collective-permute-done.30.far_ref = bf16[512,384]{1,0:T(8,128)(2,1)S(1)} collective-permute-done((bf16[512,384]{1,0:T(8,128)(2,1)S(1)}, bf16[512,384]{1,0:T(8,128)(2,1)S(1)}, u32[]{:S(2)}, u32[]{:S(2)}) %collective-permute-start.30) | collective-permute-done | bytes 393248 | tf_op jit(solution)/shard_map/ppermute | solution.py:61
  142.0 6.3 %shard_map.105 = (bf16[4,3,256,768]{3,2,1,0:T(8,128)(2,1)S(1)}, f32[1024,384]{1,0:T(8,128)S(1)}) custom-call(s32[7]{0:T(128)S(1)} %stack.27.refs_0_.pos_ref, bf16[1024,384]{1,0:T(8,128)(2,1)S(1)} %copy-done.1, bf16[1024,384]{1,0:T(8,128)(2,1)S(1)} %get-tuple-element.28.full_ref, bf16[512,384]{1,0:T(8,128)(2,1)S(1)} %collective-permute-done.29.near_ref, ...), custom_call_target="tpu_custom_call" | custom-call | tf_op jit(solution)/shard_map/pallas_call | solution.py:433
  148.3 4.3 %shard_map.107 = bf16[1024,384]{1,0:T(8,128)(2,1)} custom-call(s32[7]{0:T(128)S(1)} %stack.27.refs_0_.pos_ref, bf16[4,3,256,768]{3,2,1,0:T(8,128)(2,1)S(1)} %get-tuple-element.31.prob_ref, f32[1024,384]{1,0:T(8,128)S(1)} %get-tuple-element.32.total_ref, bf16[1024,384]{1,0:T(8,128)(2,1)S(1)} %get-tuple-element.34.full_ref, ...), custom_call_target="tpu_custom_call" | custom-call | tf_op jit(solution)/shard_map/pallas_call | solution.py:463
  (74 shorter events, 20.9 us)
Async XLA Ops:
  4.5 13.4 %collective-permute-start.11 = (bf16[320,384]{1,0:T(8,128)(2,1)S(1)}, bf16[320,384]{1,0:T(8,128)(2,1)S(1)}, u32[]{:S(2)}, u32[]{:S(2)}) collective-permute-start(bf16[320,384]{1,0:T(8,128)(2,1)S(1)} %shard_map.100.refs_8_), channel_id=1, source_target_pairs={{0,16},{1,17},{2,18},{3,19},{4,20},{5,21},{6,22},{7,23},{8,56},{9,... | collective-permute-start | bytes 737288 | tf_op jit(solution)/shard_map/ppermute | solution.py:61
  7.8 42.3 %collective-permute-start.5 = (bf16[128,5120]{1,0:T(8,128)(2,1)}, bf16[128,5120]{1,0:T(8,128)(2,1)S(1)}, u32[]{:S(2)}, u32[]{:S(2)}) collective-permute-start(bf16[128,5120]{1,0:T(8,128)(2,1)} %refs_1_.3), channel_id=1, source_target_pairs={{0,3},{1,0},{2,1},{3,2},{4,7},{5,4},{6,5},{7,6},{8,11},{9,8},{10,9... | collective-permute-start | bytes 3932168 | tf_op jit(solution)/shard_map/ppermute | solution.py:61
  19.7 11.8 %collective-permute-start.15 = (bf16[320,384]{1,0:T(8,128)(2,1)S(1)}, bf16[320,384]{1,0:T(8,128)(2,1)S(1)}, u32[]{:S(2)}, u32[]{:S(2)}) collective-permute-start(bf16[320,384]{1,0:T(8,128)(2,1)S(1)} %collective-permute-done.refs_12_), channel_id=1, source_target_pairs={{0,8},{1,9},{2,10},{3,11},{4,12},{5,13},{6,14},{7,15},{8,0},{9,1},... | collective-permute-start | bytes 737288 | tf_op jit(solution)/shard_map/ppermute | solution.py:61
  30.0 12.8 %collective-permute-start.20 = (bf16[960,384]{1,0:T(8,128)(2,1)S(1)}, bf16[960,384]{1,0:T(8,128)(2,1)S(1)}, u32[]{:S(2)}, u32[]{:S(2)}) collective-permute-start(bf16[960,384]{1,0:T(8,128)(2,1)S(1)} %shard_map.101.refs_10_), channel_id=1, source_target_pairs={{0,64},{1,65},{2,66},{3,67},{4,68},{5,69},{6,70},{7,71},{8,200},{9... | collective-permute-start | bytes 2211848 | tf_op jit(solution)/shard_map/ppermute | solution.py:61
  31.5 11.5 %collective-permute-start.14 = (bf16[960,384]{1,0:T(8,128)(2,1)S(1)}, bf16[960,384]{1,0:T(8,128)(2,1)S(1)}, u32[]{:S(2)}, u32[]{:S(2)}) collective-permute-start(bf16[960,384]{1,0:T(8,128)(2,1)S(1)} %shard_map.101.refs_10_), channel_id=1, source_target_pairs={{0,8},{1,9},{2,10},{3,11},{4,12},{5,13},{6,14},{7,15},{8,0},{9,1},... | collective-permute-start | bytes 2211848 | tf_op jit(solution)/shard_map/ppermute | solution.py:61
  31.5 32.9 %collective-permute-start.8 = (bf16[128,5120]{1,0:T(8,128)(2,1)S(1)}, bf16[128,5120]{1,0:T(8,128)(2,1)S(1)}, u32[]{:S(2)}, u32[]{:S(2)}) collective-permute-start(bf16[128,5120]{1,0:T(8,128)(2,1)S(1)} %copy-done), channel_id=1, source_target_pairs={{0,1},{1,2},{2,3},{3,0},{4,5},{5,6},{6,7},{7,4},{8,9},{9,10},{10,1... | collective-permute-start | bytes 3932168 | tf_op jit(solution)/shard_map/ppermute | solution.py:61
  33.1 16.8 %collective-permute-start.10 = (bf16[128,2560]{1,0:T(8,128)(2,1)S(1)}, bf16[128,2560]{1,0:T(8,128)(2,1)S(1)}, u32[]{:S(2)}, u32[]{:S(2)}) collective-permute-start(bf16[128,2560]{1,0:T(8,128)(2,1)S(1)} %get-tuple-element.23), channel_id=1, source_target_pairs={{0,4},{1,5},{2,6},{3,7},{4,0},{5,1},{6,2},{7,3},{8,12},{9,13},{10,... | collective-permute-start | bytes 1966088 | tf_op jit(solution)/shard_map/ppermute | solution.py:61
  42.7 21.7 %collective-permute-start.24 = (bf16[960,384]{1,0:T(8,128)(2,1)S(1)}, bf16[960,384]{1,0:T(8,128)(2,1)S(1)}, u32[]{:S(2)}, u32[]{:S(2)}) collective-permute-start(bf16[960,384]{1,0:T(8,128)(2,1)S(1)} %collective-permute-done.20.refs_18_), channel_id=1, source_target_pairs={{0,64},{1,65},{2,66},{3,67},{4,68},{5,69},{6,70},{7,71},{8,200},{9... | collective-permute-start | bytes 2211848 | tf_op jit(solution)/shard_map/ppermute | solution.py:61
  43.0 22.0 %collective-permute-start.22 = (bf16[960,384]{1,0:T(8,128)(2,1)S(1)}, bf16[960,384]{1,0:T(8,128)(2,1)S(1)}, u32[]{:S(2)}, u32[]{:S(2)}) collective-permute-start(bf16[960,384]{1,0:T(8,128)(2,1)S(1)} %collective-permute-done.14.refs_11_), channel_id=1, source_target_pairs={{0,64},{1,65},{2,66},{3,67},{4,68},{5,69},{6,70},{7,71},{8,200},{9... | collective-permute-start | bytes 2211848 | tf_op jit(solution)/shard_map/ppermute | solution.py:61
  49.8 15.9 %collective-permute-start.2 = (bf16[128,2560]{1,0:T(8,128)(2,1)S(1)}, bf16[128,2560]{1,0:T(8,128)(2,1)S(1)}, u32[]{:S(2)}, u32[]{:S(2)}) collective-permute-start(bf16[128,2560]{1,0:T(8,128)(2,1)S(1)} %get-tuple-element.22), channel_id=1, source_target_pairs={{0,4},{1,5},{2,6},{3,7},{4,0},{5,1},{6,2},{7,3},{8,12},{9,13},{10,... | collective-permute-start | bytes 1966088 | tf_op jit(solution)/shard_map/ppermute | solution.py:61
  50.1 28.4 %collective-permute-start.26 = (bf16[128,2560]{1,0:T(8,128)(2,1)S(1)}, bf16[128,2560]{1,0:T(8,128)(2,1)S(1)}, u32[]{:S(2)}, u32[]{:S(2)}) collective-permute-start(bf16[128,2560]{1,0:T(8,128)(2,1)S(1)} %collective-permute-done.10.refs_6_), channel_id=1, source_target_pairs={{0,1},{1,2},{2,3},{3,0},{4,5},{5,6},{6,7},{7,4},{8,9},{9,10},{10,1... | collective-permute-start | bytes 1966088 | tf_op jit(solution)/shard_map/ppermute | solution.py:61
  64.5 15.7 %collective-permute-start.21 = (bf16[960,384]{1,0:T(8,128)(2,1)S(1)}, bf16[960,384]{1,0:T(8,128)(2,1)S(1)}, u32[]{:S(2)}, u32[]{:S(2)}) collective-permute-start(bf16[960,384]{1,0:T(8,128)(2,1)S(1)} %collective-permute-done.20.refs_18_), channel_id=1, source_target_pairs={{0,8},{1,9},{2,10},{3,11},{4,12},{5,13},{6,14},{7,15},{8,0},{9,1},... | collective-permute-start | bytes 2211848 | tf_op jit(solution)/shard_map/ppermute | solution.py:61
  64.5 31.9 %collective-permute-start.25 = (bf16[960,384]{1,0:T(8,128)(2,1)S(1)}, bf16[960,384]{1,0:T(8,128)(2,1)S(1)}, u32[]{:S(2)}, u32[]{:S(2)}) collective-permute-start(bf16[960,384]{1,0:T(8,128)(2,1)S(1)} %collective-permute-done.24.refs_22_), channel_id=1, source_target_pairs={{0,8},{1,9},{2,10},{3,11},{4,12},{5,13},{6,14},{7,15},{8,0},{9,1},... | collective-permute-start | bytes 2211848 | tf_op jit(solution)/shard_map/ppermute | solution.py:61
  65.0 34.4 %collective-permute-start.23 = (bf16[960,384]{1,0:T(8,128)(2,1)S(1)}, bf16[960,384]{1,0:T(8,128)(2,1)S(1)}, u32[]{:S(2)}, u32[]{:S(2)}) collective-permute-start(bf16[960,384]{1,0:T(8,128)(2,1)S(1)} %collective-permute-done.22.refs_20_), channel_id=1, source_target_pairs={{0,8},{1,9},{2,10},{3,11},{4,12},{5,13},{6,14},{7,15},{8,0},{9,1},... | collective-permute-start | bytes 2211848 | tf_op jit(solution)/shard_map/ppermute | solution.py:61
  65.8 26.3 %collective-permute-start.9 = (bf16[128,2560]{1,0:T(8,128)(2,1)S(1)}, bf16[128,2560]{1,0:T(8,128)(2,1)S(1)}, u32[]{:S(2)}, u32[]{:S(2)}) collective-permute-start(bf16[128,2560]{1,0:T(8,128)(2,1)S(1)} %slice.17), channel_id=1, source_target_pairs={{0,1},{1,2},{2,3},{3,0},{4,5},{5,6},{6,7},{7,4},{8,9},{9,10},{10,1... | collective-permute-start | bytes 1966088 | tf_op jit(solution)/shard_map/ppermute | solution.py:61
  78.5 17.6 %collective-permute-start.6 = (bf16[128,2560]{1,0:T(8,128)(2,1)S(1)}, bf16[128,2560]{1,0:T(8,128)(2,1)S(1)}, u32[]{:S(2)}, u32[]{:S(2)}) collective-permute-start(bf16[128,2560]{1,0:T(8,128)(2,1)S(1)} %slice.16), channel_id=1, source_target_pairs={{0,3},{1,0},{2,1},{3,2},{4,7},{5,4},{6,5},{7,6},{8,11},{9,8},{10,9... | collective-permute-start | bytes 1966088 | tf_op jit(solution)/shard_map/ppermute | solution.py:61
  80.2 31.5 %collective-permute-start.27 = (bf16[128,2560]{1,0:T(8,128)(2,1)S(1)}, bf16[128,2560]{1,0:T(8,128)(2,1)S(1)}, u32[]{:S(2)}, u32[]{:S(2)}) collective-permute-start(bf16[128,2560]{1,0:T(8,128)(2,1)S(1)} %collective-permute-done.10.refs_6_), channel_id=1, source_target_pairs={{0,3},{1,0},{2,1},{3,2},{4,7},{5,4},{6,5},{7,6},{8,11},{9,8},{10,9... | collective-permute-start | bytes 1966088 | tf_op jit(solution)/shard_map/ppermute | solution.py:61
  92.0 19.7 %collective-permute-start.28 = (bf16[128,2560]{1,0:T(8,128)(2,1)S(1)}, bf16[128,2560]{1,0:T(8,128)(2,1)S(1)}, u32[]{:S(2)}, u32[]{:S(2)}) collective-permute-start(bf16[128,2560]{1,0:T(8,128)(2,1)S(1)} %collective-permute-done.9.refs_4_), channel_id=1, source_target_pairs={{0,4},{1,5},{2,6},{3,7},{4,0},{5,1},{6,2},{7,3},{8,12},{9,13},{10,... | collective-permute-start | bytes 1966088 | tf_op jit(solution)/shard_map/ppermute | solution.py:61
  96.1 19.2 %collective-permute-start.3 = (bf16[128,2560]{1,0:T(8,128)(2,1)S(1)}, bf16[128,2560]{1,0:T(8,128)(2,1)S(1)}, u32[]{:S(2)}, u32[]{:S(2)}) collective-permute-start(bf16[128,2560]{1,0:T(8,128)(2,1)S(1)} %collective-permute-done.2.refs_7_), channel_id=1, source_target_pairs={{0,1},{1,2},{2,3},{3,0},{4,5},{5,6},{6,7},{7,4},{8,9},{9,10},{10,1... | collective-permute-start | bytes 1966088 | tf_op jit(solution)/shard_map/ppermute | solution.py:61
  96.3 25.9 %collective-permute-start.4 = (bf16[128,2560]{1,0:T(8,128)(2,1)S(1)}, bf16[128,2560]{1,0:T(8,128)(2,1)S(1)}, u32[]{:S(2)}, u32[]{:S(2)}) collective-permute-start(bf16[128,2560]{1,0:T(8,128)(2,1)S(1)} %collective-permute-done.2.refs_7_), channel_id=1, source_target_pairs={{0,3},{1,0},{2,1},{3,2},{4,7},{5,4},{6,5},{7,6},{8,11},{9,8},{10,9... | collective-permute-start | bytes 1966088 | tf_op jit(solution)/shard_map/ppermute | solution.py:61
  99.4 22.9 %collective-permute-start.7 = (bf16[128,2560]{1,0:T(8,128)(2,1)S(1)}, bf16[128,2560]{1,0:T(8,128)(2,1)S(1)}, u32[]{:S(2)}, u32[]{:S(2)}) collective-permute-start(bf16[128,2560]{1,0:T(8,128)(2,1)S(1)} %collective-permute-done.6.refs_5_), channel_id=1, source_target_pairs={{0,4},{1,5},{2,6},{3,7},{4,0},{5,1},{6,2},{7,3},{8,12},{9,13},{10,... | collective-permute-start | bytes 1966088 | tf_op jit(solution)/shard_map/ppermute | solution.py:61
  126.5 15.5 %collective-permute-start.30 = (bf16[512,384]{1,0:T(8,128)(2,1)S(1)}, bf16[512,384]{1,0:T(8,128)(2,1)S(1)}, u32[]{:S(2)}, u32[]{:S(2)}) collective-permute-start(bf16[512,384]{1,0:T(8,128)(2,1)S(1)} %get-tuple-element.30), channel_id=1, source_target_pairs={{0,248},{1,249},{2,250},{3,251},{4,252},{5,253},{6,254},{7,255},{8... | collective-permute-start | bytes 1179656 | tf_op jit(solution)/shard_map/ppermute | solution.py:61
  134.8 13.6 %collective-permute-start.31 = (bf16[512,384]{1,0:T(8,128)(2,1)S(1)}, bf16[512,384]{1,0:T(8,128)(2,1)S(1)}, u32[]{:S(2)}, u32[]{:S(2)}) collective-permute-start(bf16[512,384]{1,0:T(8,128)(2,1)S(1)} %get-tuple-element.35), channel_id=1, source_target_pairs={{0,8},{1,9},{2,10},{3,11},{4,12},{5,13},{6,14},{7,15},{8,0},{9,1},... | collective-permute-start | bytes 1179656 | tf_op jit(solution)/shard_map/ppermute | solution.py:61
  134.9 13.5 %collective-permute-start.32 = (bf16[512,384]{1,0:T(8,128)(2,1)S(1)}, bf16[512,384]{1,0:T(8,128)(2,1)S(1)}, u32[]{:S(2)}, u32[]{:S(2)}) collective-permute-start(bf16[512,384]{1,0:T(8,128)(2,1)S(1)} %get-tuple-element.36), channel_id=1, source_target_pairs={{0,248},{1,249},{2,250},{3,251},{4,252},{5,253},{6,254},{7,255},{8... | collective-permute-start | bytes 1179656 | tf_op jit(solution)/shard_map/ppermute | solution.py:61
  (19 other events, 197.9 us)

commit v9 on v8

--- a/solution.py
+++ b/solution.py
@@ -408,14 +408,18 @@
             highs = jnp.where(valid, high[j, tile], highs)
         row = lax.broadcasted_iota(jnp.int32, (TILE, CAND - TILE), 0)
         allowed = jnp.logical_and(row >= lows[0:1, TILE:], row < highs[0:1, TILE:])
+        raw = [
+            lax.dot_general(
+                q_ref[:, h * HD : h * HD + HD],
+                cand[:, h * HD : h * HD + HD],
+                (((1,), (1,)), ((), ())),
+                preferred_element_type=F32,
+            )
+            for h in range(3)
+        ]
         for h in range(3):
             cols = slice(h * HD, h * HD + HD)
-            scores = lax.dot_general(
-                q_ref[:, cols],
-                cand[:, cols],
-                (((1,), (1,)), ((), ())),
-                preferred_element_type=F32,
-            ) * scale
+            scores = raw[h] * scale
             own = scores[:, :TILE]
             slabs = jnp.where(allowed, scores[:, TILE:], -jnp.inf)
             top = jnp.maximum(

time: 155 us -> 155 us (level)
  no operation moved by 1% of the time
where the time goes in v9:
time: 155 us; the launch traced here: 153 us
  waiting for transfers between devices  75.4 us (49%)
  starting transfers between devices  38.7 us (25%)
  Pallas kernels  34.9 us (23%)
  local copies, waits for them, and re-layouts  3.39 us (2%)
    ppermute x33, waiting for transfers between devices, send(): lax.ppermute(a, AXES, _far_moves() if 'far' in step else _moves(**step))  75.4 us
    ppermute x33, starting transfers between devices, send(): lax.ppermute(a, AXES, _far_moves() if 'far' in step else _moves(**step))  38.7 us
    pallas_call x1, Pallas kernels, project(): pl.pallas_call(body, out_shape=[jax.ShapeDtypeStruct((rows, 768), BF16),...  11.4 us
    pallas_call x2, Pallas kernels, project_last(): pl.pallas_call(body, out_shape=[jax.ShapeDtypeStruct((TPD * TILE, 384), B...  8.18 us
    pallas_call x1, Pallas kernels, weigh(): pl.pallas_call(body, grid=(TPD,), out_shape=[jax.ShapeDtypeStruct((TPD, 3...  6.28 us
    pallas_call x1, Pallas kernels, mix(): pl.pallas_call(body, grid=(TPD,), out_shape=jax.ShapeDtypeStruct((TPD * T...  4.34 us
    pallas_call x1, Pallas kernels, project_half(): pl.pallas_call(body, out_shape=jax.ShapeDtypeStruct((rows, 768), F32), in...  3.52 us
  transfers between devices with their start and end apart: 33, of which 11 were waited for; matrix products, arithmetic and copies ran while one was open for 1% of the time, Pallas kernels for 17%

profile of v9, /device:TPU:32, one launch (start us, length us, event | category | flops | bytes accessed | tf_op | source)
XLA Modules:
  0.0 152.7 jit_solution(17408808594662365562)
XLA Ops:
  4.5 3.3 %collective-permute-start.11 = (bf16[320,384]{1,0:T(8,128)(2,1)S(1)}, bf16[320,384]{1,0:T(8,128)(2,1)S(1)}, u32[]{:S(2)}, u32[]{:S(2)}) collective-permute-start(bf16[320,384]{1,0:T(8,128)(2,1)S(1)} %shard_map.100.refs_8_), channel_id=1, source_target_pairs={{0,16},{1,17},{2,18},{3,19},{4,20},{5,21},{6,22},{7,23},{8,56},{9,... | collective-permute-start | bytes 737288 | tf_op jit(solution)/shard_map/ppermute | solution.py:61
  7.8 3.0 %collective-permute-start.5 = (bf16[128,5120]{1,0:T(8,128)(2,1)}, bf16[128,5120]{1,0:T(8,128)(2,1)S(1)}, u32[]{:S(2)}, u32[]{:S(2)}) collective-permute-start(bf16[128,5120]{1,0:T(8,128)(2,1)} %refs_1_.3), channel_id=1, source_target_pairs={{0,3},{1,0},{2,1},{3,2},{4,7},{5,4},{6,5},{7,6},{8,11},{9,8},{10,9... | collective-permute-start | bytes 3932168 | tf_op jit(solution)/shard_map/ppermute | solution.py:61
  13.0 3.7 %collective-permute-start.12 = (bf16[320,384]{1,0:T(8,128)(2,1)S(1)}, bf16[320,384]{1,0:T(8,128)(2,1)S(1)}, u32[]{:S(2)}, u32[]{:S(2)}) collective-permute-start(bf16[320,384]{1,0:T(8,128)(2,1)S(1)} %collective-permute-done.1.refs_9_), channel_id=1, source_target_pairs={{0,16},{1,17},{2,18},{3,19},{4,20},{5,21},{6,22},{7,23},{8,56},{9,... | collective-permute-start | bytes 737288 | tf_op jit(solution)/shard_map/ppermute | solution.py:61
  17.9 1.8 %collective-permute-start.13 = (bf16[320,384]{1,0:T(8,128)(2,1)S(1)}, bf16[320,384]{1,0:T(8,128)(2,1)S(1)}, u32[]{:S(2)}, u32[]{:S(2)}) collective-permute-start(bf16[320,384]{1,0:T(8,128)(2,1)S(1)} %collective-permute-done.11.refs_0_), channel_id=1, source_target_pairs={{0,16},{1,17},{2,18},{3,19},{4,20},{5,21},{6,22},{7,23},{8,56},{9,... | collective-permute-start | bytes 737288 | tf_op jit(solution)/shard_map/ppermute | solution.py:61
  19.7 4.4 %collective-permute-done.12.refs_1_ = bf16[320,384]{1,0:T(8,128)(2,1)S(1)} collective-permute-done((bf16[320,384]{1,0:T(8,128)(2,1)S(1)}, bf16[320,384]{1,0:T(8,128)(2,1)S(1)}, u32[]{:S(2)}, u32[]{:S(2)}) %collective-permute-start.12) | collective-permute-done | bytes 245792 | tf_op jit(solution)/shard_map/ppermute | solution.py:61
  24.6 4.4 %collective-permute-done.13.refs_2_ = bf16[320,384]{1,0:T(8,128)(2,1)S(1)} collective-permute-done((bf16[320,384]{1,0:T(8,128)(2,1)S(1)}, bf16[320,384]{1,0:T(8,128)(2,1)S(1)}, u32[]{:S(2)}, u32[]{:S(2)}) %collective-permute-start.13) | collective-permute-done | bytes 245792 | tf_op jit(solution)/shard_map/ppermute | solution.py:61
  33.1 9.7 %collective-permute-done.20.refs_18_ = bf16[960,384]{1,0:T(8,128)(2,1)S(1)} collective-permute-done((bf16[960,384]{1,0:T(8,128)(2,1)S(1)}, bf16[960,384]{1,0:T(8,128)(2,1)S(1)}, u32[]{:S(2)}, u32[]{:S(2)}) %collective-permute-start.20) | collective-permute-done | bytes 737312 | tf_op jit(solution)/shard_map/ppermute | solution.py:61
  43.7 6.1 %collective-permute-done.10.refs_6_ = bf16[128,2560]{1,0:T(8,128)(2,1)S(1)} collective-permute-done((bf16[128,2560]{1,0:T(8,128)(2,1)S(1)}, bf16[128,2560]{1,0:T(8,128)(2,1)S(1)}, u32[]{:S(2)}, u32[]{:S(2)}) %collective-permute-start.10) | collective-permute-done | bytes 655392 | tf_op jit(solution)/shard_map/ppermute | solution.py:61
  51.7 12.8 %collective-permute-done.8.refs_2_ = bf16[128,5120]{1,0:T(8,128)(2,1)S(1)} collective-permute-done((bf16[128,5120]{1,0:T(8,128)(2,1)S(1)}, bf16[128,5120]{1,0:T(8,128)(2,1)S(1)}, u32[]{:S(2)}, u32[]{:S(2)}) %collective-permute-start.8) | collective-permute-done | bytes 1310752 | tf_op jit(solution)/shard_map/ppermute | solution.py:61
  67.3 11.2 %collective-permute-done.26.t0 = bf16[128,2560]{1,0:T(8,128)(2,1)S(1)} collective-permute-done((bf16[128,2560]{1,0:T(8,128)(2,1)S(1)}, bf16[128,2560]{1,0:T(8,128)(2,1)S(1)}, u32[]{:S(2)}, u32[]{:S(2)}) %collective-permute-start.26) | collective-permute-done | bytes 655392 | tf_op jit(solution)/shard_map/ppermute | solution.py:61
  78.5 1.7 %collective-permute-start.6 = (bf16[128,2560]{1,0:T(8,128)(2,1)S(1)}, bf16[128,2560]{1,0:T(8,128)(2,1)S(1)}, u32[]{:S(2)}, u32[]{:S(2)}) collective-permute-start(bf16[128,2560]{1,0:T(8,128)(2,1)S(1)} %slice.16), channel_id=1, source_target_pairs={{0,3},{1,0},{2,1},{3,2},{4,7},{5,4},{6,5},{7,6},{8,11},{9,8},{10,9... | collective-permute-start | bytes 1966088 | tf_op jit(solution)/shard_map/ppermute | solution.py:61
  80.9 11.1 %collective-permute-done.9.refs_4_ = bf16[128,2560]{1,0:T(8,128)(2,1)S(1)} collective-permute-done((bf16[128,2560]{1,0:T(8,128)(2,1)S(1)}, bf16[128,2560]{1,0:T(8,128)(2,1)S(1)}, u32[]{:S(2)}, u32[]{:S(2)}) %collective-permute-start.9) | collective-permute-done | bytes 655392 | tf_op jit(solution)/shard_map/ppermute | solution.py:61
  92.7 3.5 %collective-permute-done.6.refs_5_ = bf16[128,2560]{1,0:T(8,128)(2,1)S(1)} collective-permute-done((bf16[128,2560]{1,0:T(8,128)(2,1)S(1)}, bf16[128,2560]{1,0:T(8,128)(2,1)S(1)}, u32[]{:S(2)}, u32[]{:S(2)}) %collective-permute-start.6) | collective-permute-done | bytes 655392 | tf_op jit(solution)/shard_map/ppermute | solution.py:61
  96.3 3.0 %collective-permute-start.4 = (bf16[128,2560]{1,0:T(8,128)(2,1)S(1)}, bf16[128,2560]{1,0:T(8,128)(2,1)S(1)}, u32[]{:S(2)}, u32[]{:S(2)}) collective-permute-start(bf16[128,2560]{1,0:T(8,128)(2,1)S(1)} %collective-permute-done.2.refs_7_), channel_id=1, source_target_pairs={{0,3},{1,0},{2,1},{3,2},{4,7},{5,4},{6,5},{7,6},{8,11},{9,8},{10,9... | collective-permute-start | bytes 1966088 | tf_op jit(solution)/shard_map/ppermute | solution.py:61
  100.3 11.4 %shard_map.102 = (bf16[640,768]{1,0:T(8,128)(2,1)S(1)}, bf16[4,1280,768]{2,1,0:T(8,128)(2,1)}) custom-call(s32[7]{0:T(128)S(1)} %stack.27.refs_0_.pos_ref, bf16[128,5120]{1,0:T(8,128)(2,1)S(1)} %copy-done, bf16[128,5120]{1,0:T(8,128)(2,1)S(1)} %collective-permute-done.8.refs_2_, bf16[128,5120]{1,0:T(8,128)(2,1)S(1)} %collective-permute-done.5.refs_3_, ...), custom_call_target="tpu_custom_call" | custom-call | tf_op jit(solution)/shard_map/pallas_call | solution.py:163
  111.8 3.5 %shard_map.103.acc_ref = f32[384,768]{1,0:T(8,128)S(1)} custom-call(bf16[128,2560]{1,0:T(8,128)(2,1)S(1)} %collective-permute-done.26.t0, bf16[128,2560]{1,0:T(8,128)(2,1)S(1)} %collective-permute-done.27.t1, bf16[128,2560]{1,0:T(8,128)(2,1)S(1)} %collective-permute-done.28.t2, bf16[5120,768]{1,0:T(8,128)(2,1)} %bitcast.28), custom_call_target="tpu_custom_call" | custom-call | tf_op jit(solution)/shard_map/pallas_call | solution.py:238
  115.3 7.0 %collective-permute-done.4.t1 = bf16[128,2560]{1,0:T(8,128)(2,1)S(1)} collective-permute-done((bf16[128,2560]{1,0:T(8,128)(2,1)S(1)}, bf16[128,2560]{1,0:T(8,128)(2,1)S(1)}, u32[]{:S(2)}, u32[]{:S(2)}) %collective-permute-start.4) | collective-permute-done | bytes 655392 | tf_op jit(solution)/shard_map/ppermute | solution.py:61
  122.3 4.1 %shard_map.104 = (bf16[1024,384]{1,0:T(8,128)(2,1)S(1)}, bf16[512,384]{1,0:T(8,128)(2,1)S(1)}, bf16[512,384]{1,0:T(8,128)(2,1)S(1)}) custom-call(s32[7]{0:T(128)S(1)} %stack.27.refs_0_.pos_ref, bf16[128,2560]{1,0:T(8,128)(2,1)S(1)} %collective-permute-done.3.t0, bf16[128,2560]{1,0:T(8,128)(2,1)S(1)} %collective-permute-done.4.t1, ...), custom_call_target="tpu_custom_call" | custom-call | tf_op jit(solution)/shard_map/pallas_call | solution.py:322
  126.5 4.1 %collective-permute-start.30 = (bf16[512,384]{1,0:T(8,128)(2,1)S(1)}, bf16[512,384]{1,0:T(8,128)(2,1)S(1)}, u32[]{:S(2)}, u32[]{:S(2)}) collective-permute-start(bf16[512,384]{1,0:T(8,128)(2,1)S(1)} %get-tuple-element.30), channel_id=1, source_target_pairs={{0,248},{1,249},{2,250},{3,251},{4,252},{5,253},{6,254},{7,255},{8... | collective-permute-start | bytes 1179656 | tf_op jit(solution)/shard_map/ppermute | solution.py:61
  130.7 4.1 %shard_map.106 = (bf16[1024,384]{1,0:T(8,128)(2,1)S(1)}, bf16[512,384]{1,0:T(8,128)(2,1)S(1)}, bf16[512,384]{1,0:T(8,128)(2,1)S(1)}) custom-call(s32[7]{0:T(128)S(1)} %stack.27.refs_0_.pos_ref, bf16[128,2560]{1,0:T(8,128)(2,1)S(1)} %collective-permute-done.3.t0, bf16[128,2560]{1,0:T(8,128)(2,1)S(1)} %collective-permute-done.4.t1, ...), custom_call_target="tpu_custom_call" | custom-call | tf_op jit(solution)/shard_map/pallas_call | solution.py:322
  134.9 2.4 %collective-permute-start.32 = (bf16[512,384]{1,0:T(8,128)(2,1)S(1)}, bf16[512,384]{1,0:T(8,128)(2,1)S(1)}, u32[]{:S(2)}, u32[]{:S(2)}) collective-permute-start(bf16[512,384]{1,0:T(8,128)(2,1)S(1)} %get-tuple-element.36), channel_id=1, source_target_pairs={{0,248},{1,249},{2,250},{3,251},{4,252},{5,253},{6,254},{7,255},{8... | collective-permute-start | bytes 1179656 | tf_op jit(solution)/shard_map/ppermute | solution.py:61
  137.3 4.7 %collective-permute-done.30.far_ref = bf16[512,384]{1,0:T(8,128)(2,1)S(1)} collective-permute-done((bf16[512,384]{1,0:T(8,128)(2,1)S(1)}, bf16[512,384]{1,0:T(8,128)(2,1)S(1)}, u32[]{:S(2)}, u32[]{:S(2)}) %collective-permute-start.30) | collective-permute-done | bytes 393248 | tf_op jit(solution)/shard_map/ppermute | solution.py:61
  142.0 6.3 %shard_map.105 = (bf16[4,3,256,768]{3,2,1,0:T(8,128)(2,1)S(1)}, f32[1024,384]{1,0:T(8,128)S(1)}) custom-call(s32[7]{0:T(128)S(1)} %stack.27.refs_0_.pos_ref, bf16[1024,384]{1,0:T(8,128)(2,1)S(1)} %copy-done.1, bf16[1024,384]{1,0:T(8,128)(2,1)S(1)} %get-tuple-element.28.full_ref, bf16[512,384]{1,0:T(8,128)(2,1)S(1)} %collective-permute-done.29.near_ref, ...), custom_call_target="tpu_custom_call" | custom-call | tf_op jit(solution)/shard_map/pallas_call | solution.py:437
  148.3 4.3 %shard_map.107 = bf16[1024,384]{1,0:T(8,128)(2,1)} custom-call(s32[7]{0:T(128)S(1)} %stack.27.refs_0_.pos_ref, bf16[4,3,256,768]{3,2,1,0:T(8,128)(2,1)S(1)} %get-tuple-element.31.prob_ref, f32[1024,384]{1,0:T(8,128)S(1)} %get-tuple-element.32.total_ref, bf16[1024,384]{1,0:T(8,128)(2,1)S(1)} %get-tuple-element.34.full_ref, ...), custom_call_target="tpu_custom_call" | custom-call | tf_op jit(solution)/shard_map/pallas_call | solution.py:467
  (74 shorter events, 20.9 us)
Async XLA Ops:
  4.5 13.4 %collective-permute-start.11 = (bf16[320,384]{1,0:T(8,128)(2,1)S(1)}, bf16[320,384]{1,0:T(8,128)(2,1)S(1)}, u32[]{:S(2)}, u32[]{:S(2)}) collective-permute-start(bf16[320,384]{1,0:T(8,128)(2,1)S(1)} %shard_map.100.refs_8_), channel_id=1, source_target_pairs={{0,16},{1,17},{2,18},{3,19},{4,20},{5,21},{6,22},{7,23},{8,56},{9,... | collective-permute-start | bytes 737288 | tf_op jit(solution)/shard_map/ppermute | solution.py:61
  7.8 42.3 %collective-permute-start.5 = (bf16[128,5120]{1,0:T(8,128)(2,1)}, bf16[128,5120]{1,0:T(8,128)(2,1)S(1)}, u32[]{:S(2)}, u32[]{:S(2)}) collective-permute-start(bf16[128,5120]{1,0:T(8,128)(2,1)} %refs_1_.3), channel_id=1, source_target_pairs={{0,3},{1,0},{2,1},{3,2},{4,7},{5,4},{6,5},{7,6},{8,11},{9,8},{10,9... | collective-permute-start | bytes 3932168 | tf_op jit(solution)/shard_map/ppermute | solution.py:61
  19.7 11.8 %collective-permute-start.15 = (bf16[320,384]{1,0:T(8,128)(2,1)S(1)}, bf16[320,384]{1,0:T(8,128)(2,1)S(1)}, u32[]{:S(2)}, u32[]{:S(2)}) collective-permute-start(bf16[320,384]{1,0:T(8,128)(2,1)S(1)} %collective-permute-done.refs_12_), channel_id=1, source_target_pairs={{0,8},{1,9},{2,10},{3,11},{4,12},{5,13},{6,14},{7,15},{8,0},{9,1},... | collective-permute-start | bytes 737288 | tf_op jit(solution)/shard_map/ppermute | solution.py:61
  30.0 12.8 %collective-permute-start.20 = (bf16[960,384]{1,0:T(8,128)(2,1)S(1)}, bf16[960,384]{1,0:T(8,128)(2,1)S(1)}, u32[]{:S(2)}, u32[]{:S(2)}) collective-permute-start(bf16[960,384]{1,0:T(8,128)(2,1)S(1)} %shard_map.101.refs_10_), channel_id=1, source_target_pairs={{0,64},{1,65},{2,66},{3,67},{4,68},{5,69},{6,70},{7,71},{8,200},{9... | collective-permute-start | bytes 2211848 | tf_op jit(solution)/shard_map/ppermute | solution.py:61
  31.5 11.5 %collective-permute-start.14 = (bf16[960,384]{1,0:T(8,128)(2,1)S(1)}, bf16[960,384]{1,0:T(8,128)(2,1)S(1)}, u32[]{:S(2)}, u32[]{:S(2)}) collective-permute-start(bf16[960,384]{1,0:T(8,128)(2,1)S(1)} %shard_map.101.refs_10_), channel_id=1, source_target_pairs={{0,8},{1,9},{2,10},{3,11},{4,12},{5,13},{6,14},{7,15},{8,0},{9,1},... | collective-permute-start | bytes 2211848 | tf_op jit(solution)/shard_map/ppermute | solution.py:61
  31.5 32.9 %collective-permute-start.8 = (bf16[128,5120]{1,0:T(8,128)(2,1)S(1)}, bf16[128,5120]{1,0:T(8,128)(2,1)S(1)}, u32[]{:S(2)}, u32[]{:S(2)}) collective-permute-start(bf16[128,5120]{1,0:T(8,128)(2,1)S(1)} %copy-done), channel_id=1, source_target_pairs={{0,1},{1,2},{2,3},{3,0},{4,5},{5,6},{6,7},{7,4},{8,9},{9,10},{10,1... | collective-permute-start | bytes 3932168 | tf_op jit(solution)/shard_map/ppermute | solution.py:61
  33.1 16.8 %collective-permute-start.10 = (bf16[128,2560]{1,0:T(8,128)(2,1)S(1)}, bf16[128,2560]{1,0:T(8,128)(2,1)S(1)}, u32[]{:S(2)}, u32[]{:S(2)}) collective-permute-start(bf16[128,2560]{1,0:T(8,128)(2,1)S(1)} %get-tuple-element.23), channel_id=1, source_target_pairs={{0,4},{1,5},{2,6},{3,7},{4,0},{5,1},{6,2},{7,3},{8,12},{9,13},{10,... | collective-permute-start | bytes 1966088 | tf_op jit(solution)/shard_map/ppermute | solution.py:61
  42.7 21.7 %collective-permute-start.24 = (bf16[960,384]{1,0:T(8,128)(2,1)S(1)}, bf16[960,384]{1,0:T(8,128)(2,1)S(1)}, u32[]{:S(2)}, u32[]{:S(2)}) collective-permute-start(bf16[960,384]{1,0:T(8,128)(2,1)S(1)} %collective-permute-done.20.refs_18_), channel_id=1, source_target_pairs={{0,64},{1,65},{2,66},{3,67},{4,68},{5,69},{6,70},{7,71},{8,200},{9... | collective-permute-start | bytes 2211848 | tf_op jit(solution)/shard_map/ppermute | solution.py:61
  43.0 22.0 %collective-permute-start.22 = (bf16[960,384]{1,0:T(8,128)(2,1)S(1)}, bf16[960,384]{1,0:T(8,128)(2,1)S(1)}, u32[]{:S(2)}, u32[]{:S(2)}) collective-permute-start(bf16[960,384]{1,0:T(8,128)(2,1)S(1)} %collective-permute-done.14.refs_11_), channel_id=1, source_target_pairs={{0,64},{1,65},{2,66},{3,67},{4,68},{5,69},{6,70},{7,71},{8,200},{9... | collective-permute-start | bytes 2211848 | tf_op jit(solution)/shard_map/ppermute | solution.py:61
  49.8 15.9 %collective-permute-start.2 = (bf16[128,2560]{1,0:T(8,128)(2,1)S(1)}, bf16[128,2560]{1,0:T(8,128)(2,1)S(1)}, u32[]{:S(2)}, u32[]{:S(2)}) collective-permute-start(bf16[128,2560]{1,0:T(8,128)(2,1)S(1)} %get-tuple-element.22), channel_id=1, source_target_pairs={{0,4},{1,5},{2,6},{3,7},{4,0},{5,1},{6,2},{7,3},{8,12},{9,13},{10,... | collective-permute-start | bytes 1966088 | tf_op jit(solution)/shard_map/ppermute | solution.py:61
  50.1 28.4 %collective-permute-start.26 = (bf16[128,2560]{1,0:T(8,128)(2,1)S(1)}, bf16[128,2560]{1,0:T(8,128)(2,1)S(1)}, u32[]{:S(2)}, u32[]{:S(2)}) collective-permute-start(bf16[128,2560]{1,0:T(8,128)(2,1)S(1)} %collective-permute-done.10.refs_6_), channel_id=1, source_target_pairs={{0,1},{1,2},{2,3},{3,0},{4,5},{5,6},{6,7},{7,4},{8,9},{9,10},{10,1... | collective-permute-start | bytes 1966088 | tf_op jit(solution)/shard_map/ppermute | solution.py:61
  64.5 15.7 %collective-permute-start.21 = (bf16[960,384]{1,0:T(8,128)(2,1)S(1)}, bf16[960,384]{1,0:T(8,128)(2,1)S(1)}, u32[]{:S(2)}, u32[]{:S(2)}) collective-permute-start(bf16[960,384]{1,0:T(8,128)(2,1)S(1)} %collective-permute-done.20.refs_18_), channel_id=1, source_target_pairs={{0,8},{1,9},{2,10},{3,11},{4,12},{5,13},{6,14},{7,15},{8,0},{9,1},... | collective-permute-start | bytes 2211848 | tf_op jit(solution)/shard_map/ppermute | solution.py:61
  64.5 31.9 %collective-permute-start.25 = (bf16[960,384]{1,0:T(8,128)(2,1)S(1)}, bf16[960,384]{1,0:T(8,128)(2,1)S(1)}, u32[]{:S(2)}, u32[]{:S(2)}) collective-permute-start(bf16[960,384]{1,0:T(8,128)(2,1)S(1)} %collective-permute-done.24.refs_22_), channel_id=1, source_target_pairs={{0,8},{1,9},{2,10},{3,11},{4,12},{5,13},{6,14},{7,15},{8,0},{9,1},... | collective-permute-start | bytes 2211848 | tf_op jit(solution)/shard_map/ppermute | solution.py:61
  65.0 34.4 %collective-permute-start.23 = (bf16[960,384]{1,0:T(8,128)(2,1)S(1)}, bf16[960,384]{1,0:T(8,128)(2,1)S(1)}, u32[]{:S(2)}, u32[]{:S(2)}) collective-permute-start(bf16[960,384]{1,0:T(8,128)(2,1)S(1)} %collective-permute-done.22.refs_20_), channel_id=1, source_target_pairs={{0,8},{1,9},{2,10},{3,11},{4,12},{5,13},{6,14},{7,15},{8,0},{9,1},... | collective-permute-start | bytes 2211848 | tf_op jit(solution)/shard_map/ppermute | solution.py:61
  65.8 26.3 %collective-permute-start.9 = (bf16[128,2560]{1,0:T(8,128)(2,1)S(1)}, bf16[128,2560]{1,0:T(8,128)(2,1)S(1)}, u32[]{:S(2)}, u32[]{:S(2)}) collective-permute-start(bf16[128,2560]{1,0:T(8,128)(2,1)S(1)} %slice.17), channel_id=1, source_target_pairs={{0,1},{1,2},{2,3},{3,0},{4,5},{5,6},{6,7},{7,4},{8,9},{9,10},{10,1... | collective-permute-start | bytes 1966088 | tf_op jit(solution)/shard_map/ppermute | solution.py:61
  78.5 17.6 %collective-permute-start.6 = (bf16[128,2560]{1,0:T(8,128)(2,1)S(1)}, bf16[128,2560]{1,0:T(8,128)(2,1)S(1)}, u32[]{:S(2)}, u32[]{:S(2)}) collective-permute-start(bf16[128,2560]{1,0:T(8,128)(2,1)S(1)} %slice.16), channel_id=1, source_target_pairs={{0,3},{1,0},{2,1},{3,2},{4,7},{5,4},{6,5},{7,6},{8,11},{9,8},{10,9... | collective-permute-start | bytes 1966088 | tf_op jit(solution)/shard_map/ppermute | solution.py:61
  80.2 31.5 %collective-permute-start.27 = (bf16[128,2560]{1,0:T(8,128)(2,1)S(1)}, bf16[128,2560]{1,0:T(8,128)(2,1)S(1)}, u32[]{:S(2)}, u32[]{:S(2)}) collective-permute-start(bf16[128,2560]{1,0:T(8,128)(2,1)S(1)} %collective-permute-done.10.refs_6_), channel_id=1, source_target_pairs={{0,3},{1,0},{2,1},{3,2},{4,7},{5,4},{6,5},{7,6},{8,11},{9,8},{10,9... | collective-permute-start | bytes 1966088 | tf_op jit(solution)/shard_map/ppermute | solution.py:61
  92.0 19.7 %collective-permute-start.28 = (bf16[128,2560]{1,0:T(8,128)(2,1)S(1)}, bf16[128,2560]{1,0:T(8,128)(2,1)S(1)}, u32[]{:S(2)}, u32[]{:S(2)}) collective-permute-start(bf16[128,2560]{1,0:T(8,128)(2,1)S(1)} %collective-permute-done.9.refs_4_), channel_id=1, source_target_pairs={{0,4},{1,5},{2,6},{3,7},{4,0},{5,1},{6,2},{7,3},{8,12},{9,13},{10,... | collective-permute-start | bytes 1966088 | tf_op jit(solution)/shard_map/ppermute | solution.py:61
  96.1 19.2 %collective-permute-start.3 = (bf16[128,2560]{1,0:T(8,128)(2,1)S(1)}, bf16[128,2560]{1,0:T(8,128)(2,1)S(1)}, u32[]{:S(2)}, u32[]{:S(2)}) collective-permute-start(bf16[128,2560]{1,0:T(8,128)(2,1)S(1)} %collective-permute-done.2.refs_7_), channel_id=1, source_target_pairs={{0,1},{1,2},{2,3},{3,0},{4,5},{5,6},{6,7},{7,4},{8,9},{9,10},{10,1... | collective-permute-start | bytes 1966088 | tf_op jit(solution)/shard_map/ppermute | solution.py:61
  96.3 25.9 %collective-permute-start.4 = (bf16[128,2560]{1,0:T(8,128)(2,1)S(1)}, bf16[128,2560]{1,0:T(8,128)(2,1)S(1)}, u32[]{:S(2)}, u32[]{:S(2)}) collective-permute-start(bf16[128,2560]{1,0:T(8,128)(2,1)S(1)} %collective-permute-done.2.refs_7_), channel_id=1, source_target_pairs={{0,3},{1,0},{2,1},{3,2},{4,7},{5,4},{6,5},{7,6},{8,11},{9,8},{10,9... | collective-permute-start | bytes 1966088 | tf_op jit(solution)/shard_map/ppermute | solution.py:61
  99.4 22.9 %collective-permute-start.7 = (bf16[128,2560]{1,0:T(8,128)(2,1)S(1)}, bf16[128,2560]{1,0:T(8,128)(2,1)S(1)}, u32[]{:S(2)}, u32[]{:S(2)}) collective-permute-start(bf16[128,2560]{1,0:T(8,128)(2,1)S(1)} %collective-permute-done.6.refs_5_), channel_id=1, source_target_pairs={{0,4},{1,5},{2,6},{3,7},{4,0},{5,1},{6,2},{7,3},{8,12},{9,13},{10,... | collective-permute-start | bytes 1966088 | tf_op jit(solution)/shard_map/ppermute | solution.py:61
  126.5 15.5 %collective-permute-start.30 = (bf16[512,384]{1,0:T(8,128)(2,1)S(1)}, bf16[512,384]{1,0:T(8,128)(2,1)S(1)}, u32[]{:S(2)}, u32[]{:S(2)}) collective-permute-start(bf16[512,384]{1,0:T(8,128)(2,1)S(1)} %get-tuple-element.30), channel_id=1, source_target_pairs={{0,248},{1,249},{2,250},{3,251},{4,252},{5,253},{6,254},{7,255},{8... | collective-permute-start | bytes 1179656 | tf_op jit(solution)/shard_map/ppermute | solution.py:61
  134.8 13.6 %collective-permute-start.31 = (bf16[512,384]{1,0:T(8,128)(2,1)S(1)}, bf16[512,384]{1,0:T(8,128)(2,1)S(1)}, u32[]{:S(2)}, u32[]{:S(2)}) collective-permute-start(bf16[512,384]{1,0:T(8,128)(2,1)S(1)} %get-tuple-element.35), channel_id=1, source_target_pairs={{0,8},{1,9},{2,10},{3,11},{4,12},{5,13},{6,14},{7,15},{8,0},{9,1},... | collective-permute-start | bytes 1179656 | tf_op jit(solution)/shard_map/ppermute | solution.py:61
  134.9 13.5 %collective-permute-start.32 = (bf16[512,384]{1,0:T(8,128)(2,1)S(1)}, bf16[512,384]{1,0:T(8,128)(2,1)S(1)}, u32[]{:S(2)}, u32[]{:S(2)}) collective-permute-start(bf16[512,384]{1,0:T(8,128)(2,1)S(1)} %get-tuple-element.36), channel_id=1, source_target_pairs={{0,248},{1,249},{2,250},{3,251},{4,252},{5,253},{6,254},{7,255},{8... | collective-permute-start | bytes 1179656 | tf_op jit(solution)/shard_map/ppermute | solution.py:61
  (19 other events, 197.9 us)
